TPU v7x, 128 devices: a whole 4x4x4 slice. The times are simulated.
128 devices in a mesh: wide: 32 (over x, z, core), narrow: 4 (over y).
Axes of the slice: x: 4, y: 4, z: 4, core: 2. Of those that a mesh axis runs over, the one named last changes fastest.
Arguments:
- front: bfloat16 [4, 32, 128, 32, 4, 128], P(None, 'wide', None, None, 'narrow'), may hold values from -6 to 6
- pivot_inverse: bfloat16 [4, 128, 128], replicated, may hold values from -0.0105112052 to 0.17838107
- rhs: bfloat16 [4, 32, 128, 256], P(None, 'wide'), may hold values from -6 to 6
- trail_sol: bfloat16 [4, 32, 128, 256], P(None, 'wide'), may hold values from -1.1953125 to 1.1953125
- block_mask: int32 [4, 32, 32, 4], P(None, 'wide', None, 'narrow'), may hold values 0 or 1
- panel_order: int32 [4], replicated, may hold values from 0 to 3, each once
Outputs:
- front_out: bfloat16 [4, 32, 128, 32, 4, 128], P(None, 'wide', None, None, 'narrow')
- forward_rhs: bfloat16 [4, 32, 128, 256], P(None, 'wide')
- window_solution: bfloat16 [4, 128, 256], replicated
Inputs may be any that keep to these rules, and one draw needn't show every extreme that they name: `panel_order`: each value 0 to 3 appears once.
All inputs are finite; a program needn't handle non-finite values. No bound on the sum of `block_mask` on one device may be relied on, other than what follows from the above.
Results may differ from a plain program's by a relative error of at most 0.0076.
Values may be sent and summed in bfloat16 or wider, within the bound.
No kernel may reach another device: no remote copies, remote signals or barrier semaphores. Data moves between devices by JAX's collectives and lax.ppermute only.
A program may use at most 64 MiB of HBM per device.

v0:
```python
import jax
import jax.numpy as jnp
from jax import lax
from jax.experimental import pallas as pl
from jax.experimental.pallas import tpu as pltpu
from jax.sharding import PartitionSpec as P


BF = jnp.bfloat16
F32 = jnp.float32
BS = 128
NP = 4
NR = 4
NC = 32
NRHS = 256
NW = 32
PIECES = 8
CPP = NC // PIECES
SUB = 16
EXTRA = SUB + 8 + 8


def holder(p, i):
    z = i >> 1 if p % 2 == 0 else 3 - (i >> 1)
    return (p >> 1) * 8 + z * 2 + (i & 1)


def dot(a, b, ca=1, cb=0):
    return lax.dot_general(a, b, (((ca,), (cb,)), ((), ())), preferred_element_type=F32)


def ranks_of(order, w):
    rank = [sum(jnp.where(order[s] == i, s, 0) for s in range(NP)) for i in range(NP)]
    own = jnp.int32(NP)
    for i in range(NP):
        own = jnp.where(w == i, rank[i], own)
    return rank, own


def one_hot(rows, fn):
    r = lax.broadcasted_iota(jnp.int32, (rows, BS), 0)
    c = lax.broadcasted_iota(jnp.int32, (rows, BS), 1)
    return jnp.where(fn(r) == c, 1.0, 0.0).astype(BF)


def prep_kernel(row_ref, col_ref, b_ref, mask_ref, *outs):
    q = lax.axis_index("narrow")
    sent, mine = outs[:PIECES], outs[PIECES]
    gather = one_hot(BS, lambda r: (r % SUB) * 8 + r // SUB)
    for ct in range(NC // 8):
        for ag in range(BS // SUB):
            native = row_ref[0, ag * SUB : (ag + 1) * SUB, ct * 8 : (ct + 1) * 8, :]
            native = native.astype(F32).reshape(BS, BS).astype(BF)
            blocks = dot(gather, native).astype(BF)
            for e in range(8):
                p, cc = divmod(ct * 8 + e, CPP)
                sent[p][cc * BS + ag * SUB : cc * BS + (ag + 1) * SUB] = blocks[e * SUB : (e + 1) * SUB]
            if ct == 0:
                sent[ag][CPP * BS : CPP * BS + SUB] = blocks[:SUB]
    pick = one_hot(SUB, lambda r: r * 8)
    for r in range(NR):
        for ag in range(BS // SUB):
            native = col_ref[r, ag * SUB : (ag + 1) * SUB].astype(F32).reshape(BS, BS).astype(BF)
            mine[r * BS + ag * SUB : r * BS + (ag + 1) * SUB] = dot(pick, native).astype(BF)
    mask = mask_ref[...].astype(F32)
    widen = one_hot(NC, lambda r: r)
    line = jnp.broadcast_to(dot(mask.astype(BF), widen)[0:1], (8, BS)).astype(BF)
    for p in range(PIECES):
        rows = b_ref[0, p * SUB : (p + 1) * SUB, :].astype(F32)
        rows = jnp.where((q & 2) != 0, rows[8:], rows[:8])
        rows = jnp.where((q & 1) != 0, rows[:, BS:], rows[:, :BS])
        sent[p][CPP * BS + SUB : CPP * BS + SUB + 8] = rows.astype(BF)
        sent[p][CPP * BS + SUB + 8 :] = line
    first = jnp.broadcast_to(mask[:, 0:1], (NR, BS))
    mine[NR * BS :] = jnp.concatenate([first, jnp.zeros((8 - NR, BS), F32)], axis=0).astype(BF)


def panel_kernel(order, own, d1, d2, d3, got, w_ref, b_ref, y_ref,
                 lown, lpiv, zt, frhs, tpart, delta, mpiv, pan, bs, ztall, tall, mk):
    w, q = lax.axis_index("wide"), lax.axis_index("narrow")
    rank, own_rank = ranks_of(order, w)
    for i in range(NP):
        mpiv[i : i + 1] = got[holder(0, i), q, SUB + 8 : SUB + 16].astype(F32)[0:1].astype(jnp.int32)
    for d, ref in enumerate((own, d1, d2, d3)):
        k = lax.rem(q - d + 4, 4)
        pan[k, 0 : NR * BS] = ref[0 : NR * BS]
        mk[k] = ref[NR * BS : NR * BS + 8].astype(F32)
    for k in range(NP):
        for i in range(NP):
            for p in range(PIECES):
                pan[k, NR * BS + i * BS + p * SUB : NR * BS + i * BS + (p + 1) * SUB] = got[holder(p, i), k, 0:SUB]
    for r in range(NR):
        bs[r] = b_ref[r].astype(F32)
    for i in range(NP):
        for p in range(PIECES):
            for n in range(4):
                r0 = p * SUB + 8 * (n >> 1)
                c0 = 128 * (n & 1)
                bs[NR + i, r0 : r0 + 8, c0 : c0 + 128] = got[holder(p, i), n, SUB : SUB + 8].astype(F32)
    row_rank = [own_rank, None, None, None] + rank
    for s in range(NP):
        k = order[s]
        weight = w_ref[k]
        left = dot(pan[k], weight)
        parts = []
        for i in range(NR + NP):
            part = left[i * BS : (i + 1) * BS]
            if row_rank[i] is not None:
                part = jnp.where(row_rank[i] > s, part, 0.0)
            parts.append(part.astype(BF))
        lb = jnp.concatenate(parts, axis=0)
        lown[:, s * BS : (s + 1) * BS] = lb[: NR * BS]
        lpiv[s] = lb[NR * BS :]
        for t in range(s + 1, NP):
            j = order[t]
            akj = pan[j, pl.ds(pl.multiple_of(NR * BS + k * BS, BS), BS), :]
            prod = dot(lb, dot(weight, akj, 0, 0).astype(BF))
            for i in range(NR + NP):
                sl = slice(i * BS, (i + 1) * BS)
                if i < NR:
                    m = mk[j, i : i + 1, :]
                else:
                    m = got[holder(0, i - NR), j, SUB + 8 : SUB + 16].astype(F32)[0:1, 0:1]
                pan[j, sl] = (pan[j, sl].astype(F32) - m * prod[sl]).astype(BF)
        bk = bs[NR + k].astype(BF)
        z = dot(weight, bk, 0, 0).astype(BF)
        ztall[...] = dot(bk, weight, 0, 0).astype(BF).astype(F32)
        for j in range(2):
            zt[s * 2 + j : s * 2 + j + 1] = ztall[pl.ds(j * BS + q * NW + w, 1), :]
        elim = dot(lb, z)
        for i in range(NR + NP):
            bs[i] = (bs[i] - elim[i * BS : (i + 1) * BS]).astype(BF).astype(F32)
    for r in range(NR):
        frhs[r] = bs[r].astype(BF)
    delta[...] = (own[0 : NR * BS].astype(F32) - pan[q, 0 : NR * BS].astype(F32)).astype(BF)
    y0 = jnp.where(w < NP, jnp.zeros_like(y_ref[0]), y_ref[0])
    y = jnp.concatenate([y0] + [y_ref[r] for r in range(1, NR)], axis=0)
    tall[...] = dot(y, lown[...], 0, 0)
    for j in range(2):
        mine_cols = tall[pl.ds(pl.multiple_of(j * BS + q * NW, NW), NW), :]
        for s in range(NP):
            tpart[:, s * 2 + j, :] = mine_cols[:, s * BS : (s + 1) * BS]


def solve_kernel(order, parts, zt, lpiv, w_ref, h, out, xs):
    total = jnp.sum(parts[...], axis=0)
    for s in reversed(range(NP)):
        k = order[s]
        acc = total[s * 2 : s * 2 + 2]
        for t in range(s + 1, NP):
            i = order[t]
            acc = acc + dot(xs[i].astype(BF), lpiv[s, pl.ds(pl.multiple_of(i * BS, BS), BS), :])
        c = (zt[s * 2 : s * 2 + 2] - acc).astype(BF)
        xs[k] = dot(c, w_ref[k], 1, 1).astype(BF).astype(F32)
    x = jnp.concatenate([xs[i] for i in range(NP)], axis=0).astype(BF)
    for d in range(NW * 4):
        out[d] = x


def combine_kernel(order, lown, lpiv, w_ref, h):
    def low(t, s):
        return lpiv[s, pl.ds(pl.multiple_of(order[t] * BS, BS), BS), :]

    def right(coeff, s):
        return dot(coeff.astype(BF), w_ref[order[s]], 1, 1).astype(BF)

    base = [lown[:, s * BS : (s + 1) * BS].astype(F32) for s in range(NP)]
    r3 = right(base[3], 3)
    r3_low = [dot(r3, low(3, s)) for s in range(3)]
    for m3 in range(2):
        c3 = [base[s] - r3_low[s] if m3 else base[s] for s in range(3)]
        r2 = right(c3[2], 2)
        r2_low = [dot(r2, low(2, s)) for s in range(2)]
        for m2 in range(2):
            c2 = [c3[s] - r2_low[s] if m2 else c3[s] for s in range(2)]
            r1 = right(c2[1], 1)
            r1_low = dot(r1, low(1, 0))
            for m1 in range(2):
                r0 = right(c2[0] - r1_low if m1 else c2[0], 0)
                pat = m1 + 2 * m2 + 4 * m3
                for s, block in enumerate((r0, r1, r2, r3)):
                    h[pat, :, pl.ds(pl.multiple_of(order[s] * BS, BS), BS)] = block


GC = 8


def update_kernel(order, mown, mpiv, a_ref, u_ref, h, delta, out):
    g = pl.program_id(0)
    rows = lax.broadcasted_iota(jnp.int32, (BS, BS), 0)
    cols = lax.broadcasted_iota(jnp.int32, (BS, BS), 1)
    perm = jnp.where((rows % GC) * SUB + rows // GC == cols, 1.0, 0.0).astype(BF)
    cols_out = []
    for col in range(GC):
        c = g * GC + col
        pat = mpiv[order[1], c] + 2 * mpiv[order[2], c] + 4 * mpiv[order[3], c]
        p, cc = divmod(col, CPP)
        raw = [u_ref[holder(p, k), cc * BS : (cc + 1) * BS] for k in range(NP)]
        raw = jnp.concatenate(raw, axis=0)
        lu = dot(h[pat], raw)
        parts = []
        for r in range(NR):
            parts.append(jnp.where(mown[r, c] != 0, lu[r * BS : (r + 1) * BS], 0.0).astype(BF))
        if col == 0:
            parts = [jnp.where(g == 0, delta[r * BS : (r + 1) * BS], parts[r]) for r in range(NR)]
        cols_out.append(parts)
    for r in range(NR):
        for ag in range(0, BS // SUB, 2):
            sls = [slice((ag + e) * SUB, (ag + e + 1) * SUB) for e in range(2)]
            stack = jnp.concatenate(
                [jnp.concatenate([cols_out[col][r][sl] for col in range(GC)], axis=0) for sl in sls], axis=1
            )
            change = dot(perm, stack)
            for e, sl in enumerate(sls):
                part = change[:, e * BS : (e + 1) * BS].reshape(SUB, GC, BS)
                out[r, sl] = (a_ref[r, sl].astype(F32) - part).astype(BF)


def vmem(n):
    return [pl.BlockSpec(memory_space=pltpu.VMEM)] * n


def smem(n):
    return [pl.BlockSpec(memory_space=pltpu.SMEM)] * n


def body(front, pivot_inverse, rhs, trail_sol, block_mask, panel_order):
    w = lax.axis_index("wide")
    blocks = front.reshape(NR, BS, NC, BS)
    mask = block_mask.reshape(NR, NC)
    b = rhs.reshape(NR, BS, NRHS)
    y = trail_sol.reshape(NR, BS, NRHS)

    fixed = lambda shape: pl.BlockSpec(shape, lambda g: (0,) * len(shape))
    shapes = [(CPP * BS + EXTRA, BS)] * PIECES + [(NR * BS + 8, BS)]
    *sent, mine = pl.pallas_call(
        prep_kernel,
        out_shape=tuple(jax.ShapeDtypeStruct(shape, BF) for shape in shapes),
        grid=(1,),
        in_specs=[fixed((1, BS, NC, BS)), fixed((NR, BS, 8, BS)), fixed((1, BS, NRHS)), fixed((NR, NC))],
        out_specs=tuple(fixed(shape) for shape in shapes),
        name="prep",
    )(blocks, blocks, b, mask)

    others = [lax.ppermute(mine, "narrow", [(i, (i + d) % 4) for i in range(4)]) for d in (1, 2, 3)]

    pieces = [
        lax.ppermute(sent[p], "wide", [(i, holder(p, i)) for i in range(NP)]) for p in range(1, PIECES)
    ]
    got = sum(pieces, jnp.where(w < NP, sent[0], jnp.zeros_like(sent[0])))

    ugath = lax.all_gather(got[: CPP * BS], "wide")

    small = jnp.broadcast_to(got[None, CPP * BS :], (NW * 4, EXTRA, BS))
    small = lax.all_to_all(small, ("wide", "narrow"), 0, 0).reshape(NW, 4, EXTRA, BS)

    lown, lpiv, zt, frhs, tpart, delta, mpiv = pl.pallas_call(
        panel_kernel,
        out_shape=(
            jax.ShapeDtypeStruct((NR * BS, NP * BS), BF),
            jax.ShapeDtypeStruct((NP, NP * BS, BS), BF),
            jax.ShapeDtypeStruct((8, BS), F32),
            jax.ShapeDtypeStruct((NR, BS, NRHS), BF),
            jax.ShapeDtypeStruct((NW, 8, BS), F32),
            jax.ShapeDtypeStruct((NR * BS, BS), BF),
            jax.ShapeDtypeStruct((NP, BS), jnp.int32),
        ),
        in_specs=smem(1) + vmem(8),
        out_specs=tuple(vmem(7)),
        scratch_shapes=[
            pltpu.VMEM((NP, (NR + NP) * BS, BS), BF),
            pltpu.VMEM((NR + NP, BS, NRHS), F32),
            pltpu.VMEM((NRHS, BS), F32),
            pltpu.VMEM((NRHS, NP * BS), F32),
            pltpu.VMEM((NP, 8, BS), F32),
        ],
        name="panel",
    )(panel_order, mine, *others, small, pivot_inverse, b, y)

    h = pl.pallas_call(
        combine_kernel,
        out_shape=jax.ShapeDtypeStruct((8, NR * BS, NP * BS), BF),
        in_specs=smem(1) + vmem(3),
        out_specs=vmem(1)[0],
        name="combine",
    )(panel_order, lown, lpiv, pivot_inverse)

    tparts = lax.all_to_all(tpart, "wide", 0, 0)
    xg = pl.pallas_call(
        solve_kernel,
        out_shape=jax.ShapeDtypeStruct((NW * 4, 8, BS), BF),
        in_specs=smem(1) + vmem(4) + [pl.BlockSpec(memory_space=pl.ANY)],
        out_specs=vmem(1)[0],
        scratch_shapes=[pltpu.VMEM((NP, 2, BS), F32)],
        name="solve",
    )(panel_order, tparts, zt, lpiv, pivot_inverse, h)
    xall = lax.all_to_all(xg, ("narrow", "wide"), 0, 0)

    front_out = pl.pallas_call(
        update_kernel,
        out_shape=jax.ShapeDtypeStruct((NR, BS, NC, BS), BF),
        grid=(NC // GC,),
        in_specs=smem(3)
        + [
            pl.BlockSpec((NR, BS, GC, BS), lambda g: (0, 0, g, 0)),
            pl.BlockSpec((8, CPP * BS, BS), lambda g: (g, 0, 0)),
            fixed((8, NR * BS, NP * BS)),
            fixed((NR * BS, BS)),
        ],
        out_specs=pl.BlockSpec((NR, BS, GC, BS), lambda g: (0, 0, g, 0)),
        name="update",
    )(panel_order, mask, mpiv, blocks, ugath.reshape(NW, CPP * BS, BS), h, delta)
    front_out, xall = lax.optimization_barrier((front_out, xall))
    window = xall.reshape(NW * 4, NP, 2, BS).transpose(1, 3, 2, 0).reshape(NP, BS, NRHS)
    return front_out.reshape(front.shape), frhs.reshape(rhs.shape), window


def solution(mesh):
    in_specs = (
        P(None, "wide", None, None, "narrow", None),
        P(),
        P(None, "wide", None, None),
        P(None, "wide", None, None),
        P(None, "wide", None, "narrow"),
        P(),
    )
    out_specs = (P(None, "wide", None, None, "narrow", None), P(None, "wide", None, None), P())

    def step(*args):
        return body(*args)

    step = jax.shard_map(step, mesh=mesh, in_specs=in_specs, out_specs=out_specs, check_vma=False)
    return step
```

profile of v0, /device:TPU:1, one launch (start us, length us, event | category | flops | bytes accessed | tf_op | source)
XLA Modules:
  0.0 113.5 jit_solution(9763336629094022638)
XLA Ops:
  7.2 0.0 all-gather.3.cloned.1.call-start
  7.2 3.3 %prep.1 = (bf16[544,128]{1,0:T(8,128)(2,1)}, bf16[544,128]{1,0:T(8,128)(2,1)}, bf16[544,128]{1,0:T(8,128)(2,1)}, bf16[544,128]{1,0:T(8,128)(2,1)}, bf16[544,128]...) custom-call(bf16[4,128,32,128]{3,2,1,0:T(8,128)(2,1)} %bitcast.15, ...), custom_call_target="tpu_custom_call" | custom-call | tf_op jit(solution)/shard_map/prep/pallas_call | solution.py:236
  10.5 0.0 copy-start.2
  10.5 6.6 %collective-permute-start.3 = (bf16[544,128]{1,0:T(8,128)(2,1)}, bf16[544,128]{1,0:T(8,128)(2,1)S(1)}, u32[]{:S(2)}, u32[]{:S(2)}) collective-permute-start(bf16[544,128]{1,0:T(8,128)(2,1)} %get-tuple-element.23), channel_id=1, source_target_pairs={{0,24},{4,28},{8,16},{12,20},{1,25},{5,29},{9,17},{13,21},{2,26},{... | collective-permute-start | bytes 417800 | tf_op jit(solution)/shard_map/ppermute | solution.py:248
  17.1 1.3 %collective-permute-start.4 = (bf16[544,128]{1,0:T(8,128)(2,1)}, bf16[544,128]{1,0:T(8,128)(2,1)S(1)}, u32[]{:S(2)}, u32[]{:S(2)}) collective-permute-start(bf16[544,128]{1,0:T(8,128)(2,1)} %get-tuple-element.24), channel_id=1, source_target_pairs={{0,32},{4,36},{8,40},{12,44},{1,33},{5,37},{9,41},{13,45},{2,34},{... | collective-permute-start | bytes 417800 | tf_op jit(solution)/shard_map/ppermute | solution.py:248
  18.4 1.3 %collective-permute-start.5 = (bf16[544,128]{1,0:T(8,128)(2,1)}, bf16[544,128]{1,0:T(8,128)(2,1)S(1)}, u32[]{:S(2)}, u32[]{:S(2)}) collective-permute-start(bf16[544,128]{1,0:T(8,128)(2,1)} %get-tuple-element.25), channel_id=1, source_target_pairs={{0,56},{4,60},{8,48},{12,52},{1,57},{5,61},{9,49},{13,53},{2,58},{... | collective-permute-start | bytes 417800 | tf_op jit(solution)/shard_map/ppermute | solution.py:248
  19.7 1.3 %collective-permute-start.6 = (bf16[544,128]{1,0:T(8,128)(2,1)}, bf16[544,128]{1,0:T(8,128)(2,1)S(1)}, u32[]{:S(2)}, u32[]{:S(2)}) collective-permute-start(bf16[544,128]{1,0:T(8,128)(2,1)} %get-tuple-element.26), channel_id=1, source_target_pairs={{0,64},{4,68},{8,72},{12,76},{1,65},{5,69},{9,73},{13,77},{2,66},{... | collective-permute-start | bytes 417800 | tf_op jit(solution)/shard_map/ppermute | solution.py:248
  21.0 1.3 %collective-permute-start.7 = (bf16[544,128]{1,0:T(8,128)(2,1)}, bf16[544,128]{1,0:T(8,128)(2,1)S(1)}, u32[]{:S(2)}, u32[]{:S(2)}) collective-permute-start(bf16[544,128]{1,0:T(8,128)(2,1)} %get-tuple-element.27), channel_id=1, source_target_pairs={{0,88},{4,92},{8,80},{12,84},{1,89},{5,93},{9,81},{13,85},{2,90},{... | collective-permute-start | bytes 417800 | tf_op jit(solution)/shard_map/ppermute | solution.py:248
  22.3 0.0 collective-permute-done.3
  22.4 1.3 %collective-permute-start.8 = (bf16[544,128]{1,0:T(8,128)(2,1)}, bf16[544,128]{1,0:T(8,128)(2,1)S(1)}, u32[]{:S(2)}, u32[]{:S(2)}) collective-permute-start(bf16[544,128]{1,0:T(8,128)(2,1)} %get-tuple-element.28), channel_id=1, source_target_pairs={{0,96},{4,100},{8,104},{12,108},{1,97},{5,101},{9,105},{13,109},{2... | collective-permute-start | bytes 417800 | tf_op jit(solution)/shard_map/ppermute | solution.py:248
  23.7 0.0 collective-permute-done.4
  23.7 1.3 %collective-permute-start.9 = (bf16[544,128]{1,0:T(8,128)(2,1)}, bf16[544,128]{1,0:T(8,128)(2,1)S(1)}, u32[]{:S(2)}, u32[]{:S(2)}) collective-permute-start(bf16[544,128]{1,0:T(8,128)(2,1)} %get-tuple-element.29), channel_id=1, source_target_pairs={{0,120},{4,124},{8,112},{12,116},{1,121},{5,125},{9,113},{13,117},... | collective-permute-start | bytes 417800 | tf_op jit(solution)/shard_map/ppermute | solution.py:248
  25.0 0.0 collective-permute-done.5
  25.0 2.1 %collective-permute-done.6 = bf16[544,128]{1,0:T(8,128)(2,1)S(1)} collective-permute-done((bf16[544,128]{1,0:T(8,128)(2,1)}, bf16[544,128]{1,0:T(8,128)(2,1)S(1)}, u32[]{:S(2)}, u32[]{:S(2)}) %collective-permute-start.6) | collective-permute-done | bytes 139296 | tf_op jit(solution)/shard_map/ppermute | solution.py:248
  27.0 3.0 %collective-permute-done.7 = bf16[544,128]{1,0:T(8,128)(2,1)S(1)} collective-permute-done((bf16[544,128]{1,0:T(8,128)(2,1)}, bf16[544,128]{1,0:T(8,128)(2,1)S(1)}, u32[]{:S(2)}, u32[]{:S(2)}) %collective-permute-start.7) | collective-permute-done | bytes 139296 | tf_op jit(solution)/shard_map/ppermute | solution.py:248
  30.0 0.0 collective-permute-done.8
  30.0 0.0 collective-permute-done.9
  30.0 1.0 add_add_fusion
  31.0 0.6 slice.9
  31.7 0.0 all-gather.3.cloned.1.call-update
  31.7 1.1 broadcast_in_dim.10
  32.8 10.1 %all-to-all-start = ((bf16[128,32,128]{2,1,0:T(8,128)(2,1)}), bf16[128,32,128]{2,1,0:T(8,128)(2,1)S(1)}, u32[]{:S(2)}, u32[]{:S(2)}) async-start(bf16[128,32,128]{2,1,0:T(8,128)(2,1)} %broadcast_in_dim.10), calls=%async_computation | async-start | bytes 2097152 | tf_op jit(solution)/shard_map/all_to_all | solution.py:255
  42.9 0.0 copy-done.2
  42.9 2.7 %collective-permute-start.2 = (bf16[520,128]{1,0:T(8,128)(2,1)S(1)}, bf16[520,128]{1,0:T(8,128)(2,1)S(1)}, u32[]{:S(2)}, u32[]{:S(2)}) collective-permute-start(bf16[520,128]{1,0:T(8,128)(2,1)S(1)} %copy-done.2), channel_id=1, source_target_pairs={{0,3},{1,0},{2,1},{3,2},{4,7},{5,4},{6,5},{7,6},{8,11},{9,8},{10,9... | collective-permute-start | bytes 399368 | tf_op jit(solution)/shard_map/ppermute | solution.py:245
  45.6 0.5 collective-permute-start.1
  46.2 0.6 collective-permute-start
  46.7 9.7 %collective-permute-done.2.d3 = bf16[520,128]{1,0:T(8,128)(2,1)S(1)} collective-permute-done((bf16[520,128]{1,0:T(8,128)(2,1)S(1)}, bf16[520,128]{1,0:T(8,128)(2,1)S(1)}, u32[]{:S(2)}, u32[]{:S(2)}) %collective-permute-start.2) | collective-permute-done | bytes 133152 | tf_op jit(solution)/shard_map/ppermute | solution.py:245
  56.5 0.0 copy-start.3
  56.5 1.2 %collective-permute-done.1.d2 = bf16[520,128]{1,0:T(8,128)(2,1)S(1)} collective-permute-done((bf16[520,128]{1,0:T(8,128)(2,1)S(1)}, bf16[520,128]{1,0:T(8,128)(2,1)S(1)}, u32[]{:S(2)}, u32[]{:S(2)}) %collective-permute-start.1) | collective-permute-done | bytes 133152 | tf_op jit(solution)/shard_map/ppermute | solution.py:245
  57.7 0.0 copy-start.4
  57.7 5.2 %collective-permute-done.d1 = bf16[520,128]{1,0:T(8,128)(2,1)S(1)} collective-permute-done((bf16[520,128]{1,0:T(8,128)(2,1)S(1)}, bf16[520,128]{1,0:T(8,128)(2,1)S(1)}, u32[]{:S(2)}, u32[]{:S(2)}) %collective-permute-start) | collective-permute-done | bytes 133152 | tf_op jit(solution)/shard_map/ppermute | solution.py:245
  62.9 1.8 %all-to-all-done = bf16[128,32,128]{2,1,0:T(8,128)(2,1)S(1)} async-done(((bf16[128,32,128]{2,1,0:T(8,128)(2,1)}), bf16[128,32,128]{2,1,0:T(8,128)(2,1)S(1)}, u32[]{:S(2)}, u32[]{:S(2)}) %all-to-all-start) | async-done | bytes 1048608 | tf_op jit(solution)/shard_map/all_to_all | solution.py:255
  64.7 0.0 copy-done.3
  64.7 0.0 copy-done.4
  64.7 0.0 copy-done.5
  64.7 1.0 copy-done
  65.7 6.1 %panel.1 = (bf16[512,512]{1,0:T(8,128)(2,1)}, bf16[4,512,128]{2,1,0:T(8,128)(2,1)}, f32[8,128]{1,0:T(8,128)}, bf16[4,128,256]{2,1,0:T(8,128)(2,1)}, f32[32,8,128...) custom-call(s32[4]{0:T(128)} %order.7, bf16[520,128]{1,0:T(8,128)(2,1)} %get-tuple-element.21.own, ...), custom_call_target="tpu_custom_call" | custom-call | tf_op jit(solution)/shard_map/panel/pallas_call | solution.py:257
  71.7 6.2 %all-to-all-start.1 = ((f32[32,8,128]{2,1,0:T(8,128)}), f32[32,8,128]{2,1,0:T(8,128)S(1)}, u32[]{:S(2)}, u32[]{:S(2)}) async-start(f32[32,8,128]{2,1,0:T(8,128)} %get-tuple-element.34), calls=%async_computation.1 | async-start | bytes 262144 | tf_op jit(solution)/shard_map/all_to_all | solution.py:288
  78.0 5.5 %combine.1.h = bf16[8,512,512]{2,1,0:T(8,128)(2,1)} custom-call(s32[4]{0:T(128)} %order.7, bf16[512,512]{1,0:T(8,128)(2,1)} %get-tuple-element.31.lown, bf16[4,512,128]{2,1,0:T(8,128)(2,1)} %get-tuple-element.32.lpiv, bf16[4,128,128]{2,1,0:T(8,128)(2,1)} %w_ref.5), custom_call_target="tpu_custom_call" | custom-call | tf_op jit(solution)/shard_map/combine/pallas_call | solution.py:280
  83.5 3.1 %all-to-all-done.1.parts = f32[32,8,128]{2,1,0:T(8,128)S(1)} async-done(((f32[32,8,128]{2,1,0:T(8,128)}), f32[32,8,128]{2,1,0:T(8,128)S(1)}, u32[]{:S(2)}, u32[]{:S(2)}) %all-to-all-start.1) | async-done | bytes 131104 | tf_op jit(solution)/shard_map/all_to_all | solution.py:288
  86.6 0.7 copy-done.1
  87.2 2.8 %solve.1 = bf16[128,8,128]{2,1,0:T(8,128)(2,1)} custom-call(s32[4]{0:T(128)} %order.7, f32[32,8,128]{2,1,0:T(8,128)} %copy-done.1, f32[8,128]{1,0:T(8,128)} %get-tuple-element.35.zt, bf16[4,512,128]{2,1,0:T(8,128)(2,1)} %get-tuple-element.32.lpiv, bf16[4,128,128]{2,1,0:T(8,128)(2,1)} %w_ref.5, bf16[8,512,512]{2,1,0:T(8,128)(2,1)} %combine.1.h), custom_call_target="tpu_custom_call" | custom-call | tf_op jit(solution)/shard_map/solve/pallas_call | solution.py:289
  90.0 4.5 %all-to-all-start.2 = ((bf16[128,8,128]{2,1,0:T(8,128)(2,1)}), bf16[128,8,128]{2,1,0:T(8,128)(2,1)S(1)}, u32[]{:S(2)}, u32[]{:S(2)}) async-start(bf16[128,8,128]{2,1,0:T(8,128)(2,1)} %solve.1), calls=%async_computation.2 | async-start | bytes 524288 | tf_op jit(solution)/shard_map/all_to_all | solution.py:297
  94.5 0.0 all-gather.3.cloned.1.call-done
  94.6 10.6 %update.1 = bf16[4,128,32,128]{3,2,1,0:T(8,128)(2,1)} custom-call(s32[4]{0:T(128)} %order.7, s32[4,32]{1,0:T(4,128)} %bitcast.26, s32[4,128]{1,0:T(4,128)} %get-tuple-element.30.mpiv, bf16[4,128,32,128]{3,2,1,0:T(8,128)(2,1)} %bitcast.17, bf16[32,512,128]{2,1,0:T(8,128)(2,1)} %bitcast.19, bf16[8,512,512]{2,1,0:T(8,128)(2,1)} %combine.1.h, ...), custom_call_target="tpu_custom_call" | custom-call | tf_op jit(solution)/shard_map/update/pallas_call | solution.py:299
  105.2 0.2 all-to-all-done.2
  105.4 0.4 copy.9
  105.8 0.9 reshape.42
  (4 shorter events, 0.0 us)
Async XLA Ops:
  7.2 87.4 %all-gather.3.cloned.1.call-start = ((), (), s32[]{:S(2)}) async-start(), calls=%async_computation.3 | async-start | bytes 4325376 | tf_op jit(solution)/shard_map/all_gather | solution.py:252
  10.5 32.4 %copy-start.2 = (bf16[520,128]{1,0:T(8,128)(2,1)S(1)}, bf16[520,128]{1,0:T(8,128)(2,1)}, u32[]{:S(2)}) copy-start(bf16[520,128]{1,0:T(8,128)(2,1)} %get-tuple-element.21.own) | copy-start | bytes 399364
  10.5 11.8 %collective-permute-start.3 = (bf16[544,128]{1,0:T(8,128)(2,1)}, bf16[544,128]{1,0:T(8,128)(2,1)S(1)}, u32[]{:S(2)}, u32[]{:S(2)}) collective-permute-start(bf16[544,128]{1,0:T(8,128)(2,1)} %get-tuple-element.23), channel_id=1, source_target_pairs={{0,24},{4,28},{8,16},{12,20},{1,25},{5,29},{9,17},{13,21},{2,26},{... | collective-permute-start | bytes 417800 | tf_op jit(solution)/shard_map/ppermute | solution.py:248
  17.1 6.5 %collective-permute-start.4 = (bf16[544,128]{1,0:T(8,128)(2,1)}, bf16[544,128]{1,0:T(8,128)(2,1)S(1)}, u32[]{:S(2)}, u32[]{:S(2)}) collective-permute-start(bf16[544,128]{1,0:T(8,128)(2,1)} %get-tuple-element.24), channel_id=1, source_target_pairs={{0,32},{4,36},{8,40},{12,44},{1,33},{5,37},{9,41},{13,45},{2,34},{... | collective-permute-start | bytes 417800 | tf_op jit(solution)/shard_map/ppermute | solution.py:248
  18.4 6.6 %collective-permute-start.5 = (bf16[544,128]{1,0:T(8,128)(2,1)}, bf16[544,128]{1,0:T(8,128)(2,1)S(1)}, u32[]{:S(2)}, u32[]{:S(2)}) collective-permute-start(bf16[544,128]{1,0:T(8,128)(2,1)} %get-tuple-element.25), channel_id=1, source_target_pairs={{0,56},{4,60},{8,48},{12,52},{1,57},{5,61},{9,49},{13,53},{2,58},{... | collective-permute-start | bytes 417800 | tf_op jit(solution)/shard_map/ppermute | solution.py:248
  19.7 7.3 %collective-permute-start.6 = (bf16[544,128]{1,0:T(8,128)(2,1)}, bf16[544,128]{1,0:T(8,128)(2,1)S(1)}, u32[]{:S(2)}, u32[]{:S(2)}) collective-permute-start(bf16[544,128]{1,0:T(8,128)(2,1)} %get-tuple-element.26), channel_id=1, source_target_pairs={{0,64},{4,68},{8,72},{12,76},{1,65},{5,69},{9,73},{13,77},{2,66},{... | collective-permute-start | bytes 417800 | tf_op jit(solution)/shard_map/ppermute | solution.py:248
  21.0 9.0 %collective-permute-start.7 = (bf16[544,128]{1,0:T(8,128)(2,1)}, bf16[544,128]{1,0:T(8,128)(2,1)S(1)}, u32[]{:S(2)}, u32[]{:S(2)}) collective-permute-start(bf16[544,128]{1,0:T(8,128)(2,1)} %get-tuple-element.27), channel_id=1, source_target_pairs={{0,88},{4,92},{8,80},{12,84},{1,89},{5,93},{9,81},{13,85},{2,90},{... | collective-permute-start | bytes 417800 | tf_op jit(solution)/shard_map/ppermute | solution.py:248
  22.4 7.7 %collective-permute-start.8 = (bf16[544,128]{1,0:T(8,128)(2,1)}, bf16[544,128]{1,0:T(8,128)(2,1)S(1)}, u32[]{:S(2)}, u32[]{:S(2)}) collective-permute-start(bf16[544,128]{1,0:T(8,128)(2,1)} %get-tuple-element.28), channel_id=1, source_target_pairs={{0,96},{4,100},{8,104},{12,108},{1,97},{5,101},{9,105},{13,109},{2... | collective-permute-start | bytes 417800 | tf_op jit(solution)/shard_map/ppermute | solution.py:248
  23.7 6.4 %collective-permute-start.9 = (bf16[544,128]{1,0:T(8,128)(2,1)}, bf16[544,128]{1,0:T(8,128)(2,1)S(1)}, u32[]{:S(2)}, u32[]{:S(2)}) collective-permute-start(bf16[544,128]{1,0:T(8,128)(2,1)} %get-tuple-element.29), channel_id=1, source_target_pairs={{0,120},{4,124},{8,112},{12,116},{1,121},{5,125},{9,113},{13,117},... | collective-permute-start | bytes 417800 | tf_op jit(solution)/shard_map/ppermute | solution.py:248
  32.8 31.9 %all-to-all-start = ((bf16[128,32,128]{2,1,0:T(8,128)(2,1)}), bf16[128,32,128]{2,1,0:T(8,128)(2,1)S(1)}, u32[]{:S(2)}, u32[]{:S(2)}) async-start(bf16[128,32,128]{2,1,0:T(8,128)(2,1)} %broadcast_in_dim.10), calls=%async_computation | async-start | bytes 2097152 | tf_op jit(solution)/shard_map/all_to_all | solution.py:255
  42.9 13.5 %collective-permute-start.2 = (bf16[520,128]{1,0:T(8,128)(2,1)S(1)}, bf16[520,128]{1,0:T(8,128)(2,1)S(1)}, u32[]{:S(2)}, u32[]{:S(2)}) collective-permute-start(bf16[520,128]{1,0:T(8,128)(2,1)S(1)} %copy-done.2), channel_id=1, source_target_pairs={{0,3},{1,0},{2,1},{3,2},{4,7},{5,4},{6,5},{7,6},{8,11},{9,8},{10,9... | collective-permute-start | bytes 399368 | tf_op jit(solution)/shard_map/ppermute | solution.py:245
  45.6 12.1 %collective-permute-start.1 = (bf16[520,128]{1,0:T(8,128)(2,1)S(1)}, bf16[520,128]{1,0:T(8,128)(2,1)S(1)}, u32[]{:S(2)}, u32[]{:S(2)}) collective-permute-start(bf16[520,128]{1,0:T(8,128)(2,1)S(1)} %copy-done.2), channel_id=1, source_target_pairs={{0,2},{1,3},{2,0},{3,1},{4,6},{5,7},{6,4},{7,5},{8,10},{9,11},{10,... | collective-permute-start | bytes 399368 | tf_op jit(solution)/shard_map/ppermute | solution.py:245
  46.2 16.8 %collective-permute-start = (bf16[520,128]{1,0:T(8,128)(2,1)S(1)}, bf16[520,128]{1,0:T(8,128)(2,1)S(1)}, u32[]{:S(2)}, u32[]{:S(2)}) collective-permute-start(bf16[520,128]{1,0:T(8,128)(2,1)S(1)} %copy-done.2), channel_id=1, source_target_pairs={{0,1},{1,2},{2,3},{3,0},{4,5},{5,6},{6,7},{7,4},{8,9},{9,10},{10,1... | collective-permute-start | bytes 399368 | tf_op jit(solution)/shard_map/ppermute | solution.py:245
  56.5 8.2 %copy-start.3 = (bf16[520,128]{1,0:T(8,128)(2,1)}, bf16[520,128]{1,0:T(8,128)(2,1)S(1)}, u32[]{:S(2)}) copy-start(bf16[520,128]{1,0:T(8,128)(2,1)S(1)} %collective-permute-done.2.d3) | copy-start | bytes 399364
  57.7 7.0 %copy-start.4 = (bf16[520,128]{1,0:T(8,128)(2,1)}, bf16[520,128]{1,0:T(8,128)(2,1)S(1)}, u32[]{:S(2)}) copy-start(bf16[520,128]{1,0:T(8,128)(2,1)S(1)} %collective-permute-done.1.d2) | copy-start | bytes 399364
  62.9 1.8 %copy-start.5 = (bf16[520,128]{1,0:T(8,128)(2,1)}, bf16[520,128]{1,0:T(8,128)(2,1)S(1)}, u32[]{:S(2)}) copy-start(bf16[520,128]{1,0:T(8,128)(2,1)S(1)} %collective-permute-done.d1) | copy-start | bytes 399364
  64.7 1.0 copy-start
  71.7 14.8 %all-to-all-start.1 = ((f32[32,8,128]{2,1,0:T(8,128)}), f32[32,8,128]{2,1,0:T(8,128)S(1)}, u32[]{:S(2)}, u32[]{:S(2)}) async-start(f32[32,8,128]{2,1,0:T(8,128)} %get-tuple-element.34), calls=%async_computation.1 | async-start | bytes 262144 | tf_op jit(solution)/shard_map/all_to_all | solution.py:288
  86.6 0.7 copy-start.1
  90.0 15.4 %all-to-all-start.2 = ((bf16[128,8,128]{2,1,0:T(8,128)(2,1)}), bf16[128,8,128]{2,1,0:T(8,128)(2,1)S(1)}, u32[]{:S(2)}, u32[]{:S(2)}) async-start(bf16[128,8,128]{2,1,0:T(8,128)(2,1)} %solve.1), calls=%async_computation.2 | async-start | bytes 524288 | tf_op jit(solution)/shard_map/all_to_all | solution.py:297
Sparse Core Ops, SparseCore 0:
  31.8 56.2 all-gather.2
where the time goes:
time: 114 us
  starting transfers between devices  39.1 us (34%)
  Pallas kernels  28.3 us (25%)
  waiting for transfers between devices  26.3 us (23%)
  between operations  14.2 us (12%)
  local copies, waits for them, and re-layouts  4.65 us (4%)
    ppermute x3, waiting for transfers between devices, body(): lax.ppermute(mine, 'narrow', [(i, (i + d) % 4) for i in range(4)])  16.2 us
    ppermute x7, starting transfers between devices, body(): lax.ppermute(sent[p], 'wide', [(i, holder(p, i)) for i in range(NP)])  14.4 us
    pallas_call x1, Pallas kernels, body(): pl.pallas_call(update_kernel, out_shape=jax.ShapeDtypeStruct((NR, BS, NC,...  10.6 us
    all_to_all x1, starting transfers between devices, body(): lax.all_to_all(small, ('wide', 'narrow'), 0, 0).reshape(NW, 4, EXTRA, BS)  10.1 us
    all_to_all x1, starting transfers between devices, body(): tparts = lax.all_to_all(tpart, 'wide', 0, 0)  6.24 us
    pallas_call x1, Pallas kernels, body(): pl.pallas_call(panel_kernel, out_shape=(jax.ShapeDtypeStruct((NR * BS, NP...  6.09 us
    pallas_call x1, Pallas kernels, body(): pl.pallas_call(combine_kernel, out_shape=jax.ShapeDtypeStruct((8, NR * BS...  5.53 us
    ppermute x7, waiting for transfers between devices, body(): lax.ppermute(sent[p], 'wide', [(i, holder(p, i)) for i in range(NP)])  5.05 us
  transfers between devices with their start and end apart: 14, of which 8 were waited for; matrix products, arithmetic and copies ran while one was open for 1% of the time, Pallas kernels for 22%

commit v1 on v0

--- a/solution.py
+++ b/solution.py
@@ -3,6 +3,7 @@
 from jax import lax
 from jax.experimental import pallas as pl
 from jax.experimental.pallas import tpu as pltpu
+from jax.sharding import Mesh
 from jax.sharding import PartitionSpec as P
 
 
@@ -14,6 +15,7 @@
 NC = 32
 NRHS = 256
 NW = 32
+WIDE = ("chip", "core")
 PIECES = 8
 CPP = NC // PIECES
 SUB = 16
@@ -75,28 +77,47 @@
     mine[NR * BS :] = jnp.concatenate([first, jnp.zeros((8 - NR, BS), F32)], axis=0).astype(BF)
 
 
-def panel_kernel(order, own, d1, d2, d3, got, w_ref, b_ref, y_ref,
-                 lown, lpiv, zt, frhs, tpart, delta, mpiv, pan, bs, ztall, tall, mk):
-    w, q = lax.axis_index("wide"), lax.axis_index("narrow")
+def merge_kernel(*refs):
+    parts, (piece, copies) = refs[:PIECES], refs[PIECES:]
+    first = parts[0][...]
+    is_source = lax.axis_index("chip") < 2
+    total = jnp.where(is_source, first, jnp.zeros_like(first))
+    for part in parts[1:]:
+        total = total + part[...]
+    piece[...] = total[: CPP * BS]
+    for d in range(NW * 2):
+        copies[d] = total[CPP * BS :]
+
+
+def wide_index():
+    return lax.axis_index("chip") * 2 + lax.axis_index("core")
+
+
+def arrivals(near, far):
+    core = lax.axis_index("core")
+    for ref, c in ((near, core), (far, 1 - core)):
+        for zg in range(2):
+            for p in range(PIECES):
+                z = zg if p % 2 == 0 else 3 - zg
+                yield 2 * zg + c, p, ref.at[(p >> 1) * 4 + z]
+
+
+def panel_kernel(order, own, d1, d2, d3, near, far, w_ref, y_ref,
+                 lown, lpiv, tpart, delta, mpiv, pan, tall, mk, mkp):
+    w, q = wide_index(), lax.axis_index("narrow")
     rank, own_rank = ranks_of(order, w)
-    for i in range(NP):
-        mpiv[i : i + 1] = got[holder(0, i), q, SUB + 8 : SUB + 16].astype(F32)[0:1].astype(jnp.int32)
     for d, ref in enumerate((own, d1, d2, d3)):
         k = lax.rem(q - d + 4, 4)
         pan[k, 0 : NR * BS] = ref[0 : NR * BS]
         mk[k] = ref[NR * BS : NR * BS + 8].astype(F32)
-    for k in range(NP):
-        for i in range(NP):
-            for p in range(PIECES):
-                pan[k, NR * BS + i * BS + p * SUB : NR * BS + i * BS + (p + 1) * SUB] = got[holder(p, i), k, 0:SUB]
-    for r in range(NR):
-        bs[r] = b_ref[r].astype(F32)
+    for i, p, tile in arrivals(near, far):
+        row = pl.multiple_of(NR * BS + i * BS + p * SUB, SUB)
+        for k in range(NP):
+            pan[k, pl.ds(row, SUB), :] = tile[k, 0:SUB]
+            if p == 0:
+                mkp[i, k] = tile[k, SUB + 8 : SUB + 16].astype(F32)
     for i in range(NP):
-        for p in range(PIECES):
-            for n in range(4):
-                r0 = p * SUB + 8 * (n >> 1)
-                c0 = 128 * (n & 1)
-                bs[NR + i, r0 : r0 + 8, c0 : c0 + 128] = got[holder(p, i), n, SUB : SUB + 8].astype(F32)
+        mpiv[i : i + 1] = mkp[i, q, 0:1].astype(jnp.int32)
     row_rank = [own_rank, None, None, None] + rank
     for s in range(NP):
         k = order[s]
@@ -117,21 +138,8 @@
             prod = dot(lb, dot(weight, akj, 0, 0).astype(BF))
             for i in range(NR + NP):
                 sl = slice(i * BS, (i + 1) * BS)
-                if i < NR:
-                    m = mk[j, i : i + 1, :]
-                else:
-                    m = got[holder(0, i - NR), j, SUB + 8 : SUB + 16].astype(F32)[0:1, 0:1]
+                m = mk[j, i : i + 1, :] if i < NR else mkp[i - NR, j, 0:1, 0:1]
                 pan[j, sl] = (pan[j, sl].astype(F32) - m * prod[sl]).astype(BF)
-        bk = bs[NR + k].astype(BF)
-        z = dot(weight, bk, 0, 0).astype(BF)
-        ztall[...] = dot(bk, weight, 0, 0).astype(BF).astype(F32)
-        for j in range(2):
-            zt[s * 2 + j : s * 2 + j + 1] = ztall[pl.ds(j * BS + q * NW + w, 1), :]
-        elim = dot(lb, z)
-        for i in range(NR + NP):
-            bs[i] = (bs[i] - elim[i * BS : (i + 1) * BS]).astype(BF).astype(F32)
-    for r in range(NR):
-        frhs[r] = bs[r].astype(BF)
     delta[...] = (own[0 : NR * BS].astype(F32) - pan[q, 0 : NR * BS].astype(F32)).astype(BF)
     y0 = jnp.where(w < NP, jnp.zeros_like(y_ref[0]), y_ref[0])
     y = jnp.concatenate([y0] + [y_ref[r] for r in range(1, NR)], axis=0)
@@ -140,6 +148,31 @@
         mine_cols = tall[pl.ds(pl.multiple_of(j * BS + q * NW, NW), NW), :]
         for s in range(NP):
             tpart[:, s * 2 + j, :] = mine_cols[:, s * BS : (s + 1) * BS]
+
+
+def forward_kernel(order, near, far, w_ref, b_ref, lown, lpiv, zt, frhs, bs, ztall):
+    w, q = wide_index(), lax.axis_index("narrow")
+    for r in range(NR):
+        bs[r] = b_ref[r].astype(F32)
+    for i, p, tile in arrivals(near, far):
+        for n in range(4):
+            r0 = p * SUB + 8 * (n >> 1)
+            c0 = 128 * (n & 1)
+            bs[NR + i, r0 : r0 + 8, c0 : c0 + 128] = tile[n, SUB : SUB + 8].astype(F32)
+    for s in range(NP):
+        k = order[s]
+        weight = w_ref[k]
+        bk = bs[NR + k].astype(BF)
+        z = dot(weight, bk, 0, 0).astype(BF)
+        ztall[...] = dot(bk, weight, 0, 0).astype(BF).astype(F32)
+        for j in range(2):
+            zt[s * 2 + j : s * 2 + j + 1] = ztall[pl.ds(j * BS + q * NW + w, 1), :]
+        for ref, base, part in ((lown[:, s * BS : (s + 1) * BS], 0, NR), (lpiv[s], NR, NP)):
+            elim = dot(ref, z)
+            for i in range(part):
+                bs[base + i] = (bs[base + i] - elim[i * BS : (i + 1) * BS]).astype(BF).astype(F32)
+    for r in range(NR):
+        frhs[r] = bs[r].astype(BF)
 
 
 def solve_kernel(order, parts, zt, lpiv, w_ref, h, out, xs):
@@ -225,7 +258,6 @@
 
 
 def body(front, pivot_inverse, rhs, trail_sol, block_mask, panel_order):
-    w = lax.axis_index("wide")
     blocks = front.reshape(NR, BS, NC, BS)
     mask = block_mask.reshape(NR, NC)
     b = rhs.reshape(NR, BS, NRHS)
@@ -245,37 +277,58 @@
     others = [lax.ppermute(mine, "narrow", [(i, (i + d) % 4) for i in range(4)]) for d in (1, 2, 3)]
 
     pieces = [
-        lax.ppermute(sent[p], "wide", [(i, holder(p, i)) for i in range(NP)]) for p in range(1, PIECES)
+        lax.ppermute(sent[p], WIDE, [(i, holder(p, i)) for i in range(NP)]) for p in range(1, PIECES)
     ]
-    got = sum(pieces, jnp.where(w < NP, sent[0], jnp.zeros_like(sent[0])))
-
-    ugath = lax.all_gather(got[: CPP * BS], "wide")
-
-    small = jnp.broadcast_to(got[None, CPP * BS :], (NW * 4, EXTRA, BS))
-    small = lax.all_to_all(small, ("wide", "narrow"), 0, 0).reshape(NW, 4, EXTRA, BS)
-
-    lown, lpiv, zt, frhs, tpart, delta, mpiv = pl.pallas_call(
+    piece, copies = pl.pallas_call(
+        merge_kernel,
+        out_shape=(
+            jax.ShapeDtypeStruct((CPP * BS, BS), BF),
+            jax.ShapeDtypeStruct((NW * 2, EXTRA, BS), BF),
+        ),
+        in_specs=vmem(PIECES),
+        out_specs=tuple(vmem(2)),
+        name="merge",
+    )(sent[0], *pieces)
+
+    ugath = lax.all_gather(piece, WIDE)
+
+    near = lax.all_to_all(copies, ("chip", "narrow"), 0, 0).reshape(NW // 2, 4, EXTRA, BS)
+    far = lax.ppermute(near, "core", [(0, 1), (1, 0)])
+
+    lown, lpiv, tpart, delta, mpiv = pl.pallas_call(
         panel_kernel,
         out_shape=(
             jax.ShapeDtypeStruct((NR * BS, NP * BS), BF),
             jax.ShapeDtypeStruct((NP, NP * BS, BS), BF),
-            jax.ShapeDtypeStruct((8, BS), F32),
-            jax.ShapeDtypeStruct((NR, BS, NRHS), BF),
             jax.ShapeDtypeStruct((NW, 8, BS), F32),
             jax.ShapeDtypeStruct((NR * BS, BS), BF),
             jax.ShapeDtypeStruct((NP, BS), jnp.int32),
         ),
         in_specs=smem(1) + vmem(8),
-        out_specs=tuple(vmem(7)),
+        out_specs=tuple(vmem(5)),
         scratch_shapes=[
             pltpu.VMEM((NP, (NR + NP) * BS, BS), BF),
+            pltpu.VMEM((NRHS, NP * BS), F32),
+            pltpu.VMEM((NP, 8, BS), F32),
+            pltpu.VMEM((NP, NP, 8, BS), F32),
+        ],
+        name="panel",
+    )(panel_order, mine, *others, near, far, pivot_inverse, y)
+
+    zt, frhs = pl.pallas_call(
+        forward_kernel,
+        out_shape=(
+            jax.ShapeDtypeStruct((8, BS), F32),
+            jax.ShapeDtypeStruct((NR, BS, NRHS), BF),
+        ),
+        in_specs=smem(1) + vmem(6),
+        out_specs=tuple(vmem(2)),
+        scratch_shapes=[
             pltpu.VMEM((NR + NP, BS, NRHS), F32),
             pltpu.VMEM((NRHS, BS), F32),
-            pltpu.VMEM((NRHS, NP * BS), F32),
-            pltpu.VMEM((NP, 8, BS), F32),
         ],
-        name="panel",
-    )(panel_order, mine, *others, small, pivot_inverse, b, y)
+        name="forward",
+    )(panel_order, near, far, pivot_inverse, b, lown, lpiv)
 
     h = pl.pallas_call(
         combine_kernel,
@@ -285,7 +338,7 @@
         name="combine",
     )(panel_order, lown, lpiv, pivot_inverse)
 
-    tparts = lax.all_to_all(tpart, "wide", 0, 0)
+    tparts = lax.all_to_all(tpart, WIDE, 0, 0)
     xg = pl.pallas_call(
         solve_kernel,
         out_shape=jax.ShapeDtypeStruct((NW * 4, 8, BS), BF),
@@ -294,7 +347,7 @@
         scratch_shapes=[pltpu.VMEM((NP, 2, BS), F32)],
         name="solve",
     )(panel_order, tparts, zt, lpiv, pivot_inverse, h)
-    xall = lax.all_to_all(xg, ("narrow", "wide"), 0, 0)
+    xall = lax.all_to_all(xg, ("narrow", *WIDE), 0, 0)
 
     front_out = pl.pallas_call(
         update_kernel,
@@ -317,14 +370,16 @@
 
 def solution(mesh):
     in_specs = (
-        P(None, "wide", None, None, "narrow", None),
+        P(None, WIDE, None, None, "narrow", None),
         P(),
-        P(None, "wide", None, None),
-        P(None, "wide", None, None),
-        P(None, "wide", None, "narrow"),
+        P(None, WIDE, None, None),
+        P(None, WIDE, None, None),
+        P(None, WIDE, None, "narrow"),
         P(),
     )
-    out_specs = (P(None, "wide", None, None, "narrow", None), P(None, "wide", None, None), P())
+    out_specs = (P(None, WIDE, None, None, "narrow", None), P(None, WIDE, None, None), P())
+    axes = {"chip": NW // 2, "core": 2, "narrow": 4}
+    mesh = Mesh(mesh.devices.reshape(tuple(axes.values())), tuple(axes))
 
     def step(*args):
         return body(*args)

time: 114 us -> 120 us (1.053)
  blocking collectives: 0 us -> 21.4 us
  waiting for transfers between devices: 26.3 us -> 13.9 us
  starting transfers between devices: 39.1 us -> 32.7 us
  Pallas kernels: 28.3 us -> 34 us
    all_to_all x0 -> x1, blocking collectives: none -> 21.4 us  [body(): lax.all_to_all(copies, ('chip', 'narrow'), 0, 0)]
    all_to_all x3 -> x2, starting transfers between devices: 20.8 us -> 12.1 us  [the longest x1 8.1 us: body(): xall = lax.all_to_all(xg, ('narrow', *WIDE), 0, 0)]
    ppermute x3, waiting for transfers between devices: 16.2 us -> 8.53 us  [body(): lax.ppermute(mine, 'narrow', [(i, (i + d) % 4) for i in range(4)])]
    pallas_call x0 -> x2, Pallas kernels: none -> 6.48 us  [the longest x1 4.22 us: body(): pl.pallas_call(forward_kernel, out_shape=(jax.ShapeDtypeStruct((8, BS), F...]
    all_to_all x3 -> x2, waiting for transfers between devices: 5.07 us -> 0.3 us  [the longest x1 0.3 us: body(): xall = lax.all_to_all(xg, ('narrow', *WIDE), 0, 0)]
    ppermute x7 -> x8, starting transfers between devices: 14.4 us -> 18.4 us  [the longest x7 14.3 us: body(): lax.ppermute(sent[p], WIDE, [(i, holder(p, i)) for i in range(NP)])]
    ppermute x3, starting transfers between devices: 3.79 us -> 2.17 us  [body(): lax.ppermute(mine, 'narrow', [(i, (i + d) % 4) for i in range(4)])]
    ppermute x7 -> x8, waiting for transfers between devices: 5.05 us -> 5.02 us  [the longest x7 5.02 us: body(): lax.ppermute(sent[p], WIDE, [(i, holder(p, i)) for i in range(NP)])]
  transfers between devices with their start and end apart: 14 -> 14, of which waited for: 8 -> 6; matrix products, arithmetic and copies ran while one was open for 1% -> 0% of each run, Pallas kernels for 22% -> 24%
where the time goes in v1:
time: 120 us
  Pallas kernels  34 us (28%)
  starting transfers between devices  32.7 us (27%)
  blocking collectives  21.4 us (18%)
  between operations  14.2 us (12%)
  waiting for transfers between devices  13.9 us (12%)
  local copies, waits for them, and re-layouts  3.49 us (3%)
    all_to_all x1, blocking collectives, body(): lax.all_to_all(copies, ('chip', 'narrow'), 0, 0)  21.4 us
    ppermute x7, starting transfers between devices, body(): lax.ppermute(sent[p], WIDE, [(i, holder(p, i)) for i in range(NP)])  14.3 us
    pallas_call x1, Pallas kernels, body(): pl.pallas_call(update_kernel, out_shape=jax.ShapeDtypeStruct((NR, BS, NC,...  10.6 us
    ppermute x3, waiting for transfers between devices, body(): lax.ppermute(mine, 'narrow', [(i, (i + d) % 4) for i in range(4)])  8.53 us
    all_to_all x1, starting transfers between devices, body(): xall = lax.all_to_all(xg, ('narrow', *WIDE), 0, 0)  8.1 us
    pallas_call x1, Pallas kernels, body(): pl.pallas_call(combine_kernel, out_shape=jax.ShapeDtypeStruct((8, NR * BS...  5.52 us
    pallas_call x1, Pallas kernels, body(): pl.pallas_call(panel_kernel, out_shape=(jax.ShapeDtypeStruct((NR * BS, NP...  5.36 us
    ppermute x7, waiting for transfers between devices, body(): lax.ppermute(sent[p], WIDE, [(i, holder(p, i)) for i in range(NP)])  5.02 us
  transfers between devices with their start and end apart: 14, of which 6 were waited for; matrix products, arithmetic and copies ran while one was open for 0% of the time, Pallas kernels for 24%

profile of v1, /device:TPU:1, one launch (start us, length us, event | category | flops | bytes accessed | tf_op | source)
XLA Modules:
  0.0 119.7 jit_solution(3310918122104469501)
XLA Ops:
  7.2 0.0 all-gather.3.cloned.1.call-start
  7.2 3.3 %prep.1 = (bf16[544,128]{1,0:T(8,128)(2,1)}, bf16[544,128]{1,0:T(8,128)(2,1)}, bf16[544,128]{1,0:T(8,128)(2,1)}, bf16[544,128]{1,0:T(8,128)(2,1)}, bf16[544,128]...) custom-call(bf16[4,128,32,128]{3,2,1,0:T(8,128)(2,1)} %bitcast.15, ...), custom_call_target="tpu_custom_call" | custom-call | tf_op jit(solution)/shard_map/prep/pallas_call | solution.py:268
  10.5 6.5 %collective-permute-start.3 = (bf16[544,128]{1,0:T(8,128)(2,1)}, bf16[544,128]{1,0:T(8,128)(2,1)S(1)}, u32[]{:S(2)}, u32[]{:S(2)}) collective-permute-start(bf16[544,128]{1,0:T(8,128)(2,1)} %get-tuple-element.25), channel_id=1, source_target_pairs={{0,24},{4,28},{8,16},{12,20},{1,25},{5,29},{9,17},{13,21},{2,26},{... | collective-permute-start | bytes 417800 | tf_op jit(solution)/shard_map/ppermute | solution.py:280
  17.0 1.3 %collective-permute-start.4 = (bf16[544,128]{1,0:T(8,128)(2,1)}, bf16[544,128]{1,0:T(8,128)(2,1)S(1)}, u32[]{:S(2)}, u32[]{:S(2)}) collective-permute-start(bf16[544,128]{1,0:T(8,128)(2,1)} %get-tuple-element.26), channel_id=1, source_target_pairs={{0,32},{4,36},{8,40},{12,44},{1,33},{5,37},{9,41},{13,45},{2,34},{... | collective-permute-start | bytes 417800 | tf_op jit(solution)/shard_map/ppermute | solution.py:280
  18.3 1.3 %collective-permute-start.5 = (bf16[544,128]{1,0:T(8,128)(2,1)}, bf16[544,128]{1,0:T(8,128)(2,1)S(1)}, u32[]{:S(2)}, u32[]{:S(2)}) collective-permute-start(bf16[544,128]{1,0:T(8,128)(2,1)} %get-tuple-element.27), channel_id=1, source_target_pairs={{0,56},{4,60},{8,48},{12,52},{1,57},{5,61},{9,49},{13,53},{2,58},{... | collective-permute-start | bytes 417800 | tf_op jit(solution)/shard_map/ppermute | solution.py:280
  19.6 1.3 %collective-permute-start.6 = (bf16[544,128]{1,0:T(8,128)(2,1)}, bf16[544,128]{1,0:T(8,128)(2,1)S(1)}, u32[]{:S(2)}, u32[]{:S(2)}) collective-permute-start(bf16[544,128]{1,0:T(8,128)(2,1)} %get-tuple-element.28), channel_id=1, source_target_pairs={{0,64},{4,68},{8,72},{12,76},{1,65},{5,69},{9,73},{13,77},{2,66},{... | collective-permute-start | bytes 417800 | tf_op jit(solution)/shard_map/ppermute | solution.py:280
  20.9 1.3 %collective-permute-start.7 = (bf16[544,128]{1,0:T(8,128)(2,1)}, bf16[544,128]{1,0:T(8,128)(2,1)S(1)}, u32[]{:S(2)}, u32[]{:S(2)}) collective-permute-start(bf16[544,128]{1,0:T(8,128)(2,1)} %get-tuple-element.29), channel_id=1, source_target_pairs={{0,88},{4,92},{8,80},{12,84},{1,89},{5,93},{9,81},{13,85},{2,90},{... | collective-permute-start | bytes 417800 | tf_op jit(solution)/shard_map/ppermute | solution.py:280
  22.2 0.0 collective-permute-done.3.refs_1_
  22.2 0.0 copy-start.3
  22.2 1.3 %collective-permute-start.8 = (bf16[544,128]{1,0:T(8,128)(2,1)}, bf16[544,128]{1,0:T(8,128)(2,1)S(1)}, u32[]{:S(2)}, u32[]{:S(2)}) collective-permute-start(bf16[544,128]{1,0:T(8,128)(2,1)} %get-tuple-element.30), channel_id=1, source_target_pairs={{0,96},{4,100},{8,104},{12,108},{1,97},{5,101},{9,105},{13,109},{2... | collective-permute-start | bytes 417800 | tf_op jit(solution)/shard_map/ppermute | solution.py:280
  23.5 0.0 collective-permute-done.4.refs_2_
  23.6 1.3 %collective-permute-start.9 = (bf16[544,128]{1,0:T(8,128)(2,1)}, bf16[544,128]{1,0:T(8,128)(2,1)S(1)}, u32[]{:S(2)}, u32[]{:S(2)}) collective-permute-start(bf16[544,128]{1,0:T(8,128)(2,1)} %get-tuple-element.31), channel_id=1, source_target_pairs={{0,120},{4,124},{8,112},{12,116},{1,121},{5,125},{9,113},{13,117},... | collective-permute-start | bytes 417800 | tf_op jit(solution)/shard_map/ppermute | solution.py:280
  24.9 0.0 collective-permute-done.5.refs_3_
  24.9 0.0 copy-start.5
  24.9 2.0 %collective-permute-done.6.refs_4_ = bf16[544,128]{1,0:T(8,128)(2,1)S(1)} collective-permute-done((bf16[544,128]{1,0:T(8,128)(2,1)}, bf16[544,128]{1,0:T(8,128)(2,1)S(1)}, u32[]{:S(2)}, u32[]{:S(2)}) %collective-permute-start.6) | collective-permute-done | bytes 139296 | tf_op jit(solution)/shard_map/ppermute | solution.py:280
  26.9 3.0 %collective-permute-done.7.refs_5_ = bf16[544,128]{1,0:T(8,128)(2,1)S(1)} collective-permute-done((bf16[544,128]{1,0:T(8,128)(2,1)}, bf16[544,128]{1,0:T(8,128)(2,1)S(1)}, u32[]{:S(2)}, u32[]{:S(2)}) %collective-permute-start.7) | collective-permute-done | bytes 139296 | tf_op jit(solution)/shard_map/ppermute | solution.py:280
  29.9 0.0 collective-permute-done.8.refs_6_
  29.9 0.0 collective-permute-done.9.refs_7_
  30.0 0.6 copy-done.7
  30.5 0.1 copy-done.8
  30.6 0.0 copy-done.9
  30.6 2.3 %merge.1 = (bf16[512,128]{1,0:T(8,128)(2,1)}, bf16[64,32,128]{2,1,0:T(8,128)(2,1)}) custom-call(bf16[544,128]{1,0:T(8,128)(2,1)} %get-tuple-element.24.refs_0_, bf16[544,128]{1,0:T(8,128)(2,1)} %copy-done.3, bf16[544,128]{1,0:T(8,128)(2,1)} %copy-done.4, bf16[544,128]{1,0:T(8,128)(2,1)} %copy-done.5, bf16[544,128]{1,0:T(8,128)(2,1)} %copy-done.6, ...), custom_call_target="tpu_custom_call" | custom-call | tf_op jit(solution)/shard_map/merge/pallas_call | solution.py:282
  32.9 0.0 all-gather.3.cloned.1.call-update
  32.9 21.4 %all_to_all.15 = bf16[64,32,128]{2,1,0:T(8,128)(2,1)S(1)} all-to-all(bf16[64,32,128]{2,1,0:T(8,128)(2,1)} %get-tuple-element.32), channel_id=1, replica_groups=mesh['chip'=16,'core'=2,'narrow'=4] {'chip','narrow'}, dimensions={0} | all-to-all | bytes 1048576 | tf_op jit(solution)/shard_map/all_to_all | solution.py:295
  54.3 4.1 %collective-permute-start.10 = (bf16[16,4,32,128]{3,2,1,0:T(8,128)(2,1)S(1)}, bf16[16,4,32,128]{3,2,1,0:T(8,128)(2,1)S(1)}, u32[]{:S(2)}, u32[]{:S(2)}) collective-permute-start(bf16[16,4,32,128]{3,2,1,0:T(8,128)(2,1)S(1)} %bitcast.18), channel_id=1, source_target_pairs={{0,4},{4,0},{1,5},{5,1},{2,6},{6,2},{3,7},{7,3},{8,12},{12,8},{9,1... | collective-permute-start | bytes 1572872 | tf_op jit(solution)/shard_map/ppermute | solution.py:296
  58.4 0.7 collective-permute-start.2
  59.1 1.5 %collective-permute-start.1 = (bf16[520,128]{1,0:T(8,128)(2,1)}, bf16[520,128]{1,0:T(8,128)(2,1)S(1)}, u32[]{:S(2)}, u32[]{:S(2)}) collective-permute-start(bf16[520,128]{1,0:T(8,128)(2,1)} %get-tuple-element.23.own), channel_id=1, source_target_pairs={{0,2},{1,3},{2,0},{3,1},{4,6},{5,7},{6,4},{7,5},{8,10},{9,11},{10,... | collective-permute-start | bytes 399368 | tf_op jit(solution)/shard_map/ppermute | solution.py:277
  60.6 0.0 collective-permute-start
  60.6 3.1 %collective-permute-done.2.d3 = bf16[520,128]{1,0:T(8,128)(2,1)S(1)} collective-permute-done((bf16[520,128]{1,0:T(8,128)(2,1)}, bf16[520,128]{1,0:T(8,128)(2,1)S(1)}, u32[]{:S(2)}, u32[]{:S(2)}) %collective-permute-start.2) | collective-permute-done | bytes 133152 | tf_op jit(solution)/shard_map/ppermute | solution.py:277
  63.7 1.9 %collective-permute-done.1.d2 = bf16[520,128]{1,0:T(8,128)(2,1)S(1)} collective-permute-done((bf16[520,128]{1,0:T(8,128)(2,1)}, bf16[520,128]{1,0:T(8,128)(2,1)S(1)}, u32[]{:S(2)}, u32[]{:S(2)}) %collective-permute-start.1) | collective-permute-done | bytes 133152 | tf_op jit(solution)/shard_map/ppermute | solution.py:277
  65.7 3.5 %collective-permute-done.d1 = bf16[520,128]{1,0:T(8,128)(2,1)S(1)} collective-permute-done((bf16[520,128]{1,0:T(8,128)(2,1)}, bf16[520,128]{1,0:T(8,128)(2,1)S(1)}, u32[]{:S(2)}, u32[]{:S(2)}) %collective-permute-start) | collective-permute-done | bytes 133152 | tf_op jit(solution)/shard_map/ppermute | solution.py:277
  69.2 0.0 collective-permute-done.10.far
  69.2 0.0 copy-done.10
  69.2 0.6 copy-done.12
  69.8 0.2 copy-done.1
  70.0 5.4 %panel.1 = (bf16[512,512]{1,0:T(8,128)(2,1)}, bf16[4,512,128]{2,1,0:T(8,128)(2,1)}, f32[32,8,128]{2,1,0:T(8,128)}, bf16[512,128]{1,0:T(8,128)(2,1)}, s32[4,128]{1,0:T(4,128)}) custom-call(s32[4]{0:T(128)} %order.9, bf16[520,128]{1,0:T(8,128)(2,1)} %get-tuple-element.23.own, bf16[520,128]{1,0:T(8,128)(2,1)} %copy-done.12, bf16[520,128]{1,0:T(8,128)(2,1)} %copy-done.11, ...), custom_call_target="tpu_custom_call" | custom-call | tf_op jit(solution)/shard_map/panel/pallas_call | solution.py:298
  75.4 4.0 %all-to-all-start.1 = ((f32[32,8,128]{2,1,0:T(8,128)}), f32[32,8,128]{2,1,0:T(8,128)S(1)}, u32[]{:S(2)}, u32[]{:S(2)}) async-start(f32[32,8,128]{2,1,0:T(8,128)} %get-tuple-element.38), calls=%async_computation.1 | async-start | bytes 262144 | tf_op jit(solution)/shard_map/all_to_all | solution.py:341
  79.4 5.5 %combine.1.h = bf16[8,512,512]{2,1,0:T(8,128)(2,1)} custom-call(s32[4]{0:T(128)} %order.9, bf16[512,512]{1,0:T(8,128)(2,1)} %get-tuple-element.35.lown, bf16[4,512,128]{2,1,0:T(8,128)(2,1)} %get-tuple-element.36.lpiv, bf16[4,128,128]{2,1,0:T(8,128)(2,1)} %w_ref.7), custom_call_target="tpu_custom_call" | custom-call | tf_op jit(solution)/shard_map/combine/pallas_call | solution.py:333
  84.9 4.2 %forward.1 = (f32[8,128]{1,0:T(8,128)}, bf16[4,128,256]{2,1,0:T(8,128)(2,1)}) custom-call(s32[4]{0:T(128)} %order.9, bf16[16,4,32,128]{3,2,1,0:T(8,128)(2,1)} %bitcast.20, bf16[16,4,32,128]{3,2,1,0:T(8,128)(2,1)} %copy-done.1, bf16[4,128,128]{2,1,0:T(8,128)(2,1)} %w_ref.7, bf16[4,128,256]{2,1,0:T(8,128)(2,1)} %bitcast.25, ...), custom_call_target="tpu_custom_call" | custom-call | tf_op jit(solution)/shard_map/forward/pallas_call | solution.py:318
  89.2 0.0 all-to-all-done.1.parts
  89.2 0.7 copy-done.2
  89.8 2.8 %solve.1 = bf16[128,8,128]{2,1,0:T(8,128)(2,1)} custom-call(s32[4]{0:T(128)} %order.9, f32[32,8,128]{2,1,0:T(8,128)} %copy-done.2, f32[8,128]{1,0:T(8,128)} %get-tuple-element.39.zt, bf16[4,512,128]{2,1,0:T(8,128)(2,1)} %get-tuple-element.36.lpiv, bf16[4,128,128]{2,1,0:T(8,128)(2,1)} %w_ref.7, bf16[8,512,512]{2,1,0:T(8,128)(2,1)} %combine.1.h), custom_call_target="tpu_custom_call" | custom-call | tf_op jit(solution)/shard_map/solve/pallas_call | solution.py:342
  92.6 8.1 %all-to-all-start.2 = ((bf16[128,8,128]{2,1,0:T(8,128)(2,1)}), bf16[128,8,128]{2,1,0:T(8,128)(2,1)S(1)}, u32[]{:S(2)}, u32[]{:S(2)}) async-start(bf16[128,8,128]{2,1,0:T(8,128)(2,1)} %solve.1), calls=%async_computation.2 | async-start | bytes 524288 | tf_op jit(solution)/shard_map/all_to_all | solution.py:350
  100.7 0.0 all-gather.3.cloned.1.call-done
  100.8 10.6 %update.1 = bf16[4,128,32,128]{3,2,1,0:T(8,128)(2,1)} custom-call(s32[4]{0:T(128)} %order.9, s32[4,32]{1,0:T(4,128)} %bitcast.28, s32[4,128]{1,0:T(4,128)} %get-tuple-element.33.mpiv, bf16[4,128,32,128]{3,2,1,0:T(8,128)(2,1)} %bitcast.17, bf16[32,512,128]{2,1,0:T(8,128)(2,1)} %bitcast.21, bf16[8,512,512]{2,1,0:T(8,128)(2,1)} %combine.1.h, ...), custom_call_target="tpu_custom_call" | custom-call | tf_op jit(solution)/shard_map/update/pallas_call | solution.py:352
  111.3 0.3 all-to-all-done.2
  111.6 0.4 copy.9
  112.0 0.9 reshape.41
  (17 shorter events, 0.0 us)
Async XLA Ops:
  7.2 93.6 %all-gather.3.cloned.1.call-start = ((), (), s32[]{:S(2)}) async-start(), calls=%async_computation.3 | async-start | bytes 4325376 | tf_op jit(solution)/shard_map/all_gather | solution.py:293
  10.5 11.7 %collective-permute-start.3 = (bf16[544,128]{1,0:T(8,128)(2,1)}, bf16[544,128]{1,0:T(8,128)(2,1)S(1)}, u32[]{:S(2)}, u32[]{:S(2)}) collective-permute-start(bf16[544,128]{1,0:T(8,128)(2,1)} %get-tuple-element.25), channel_id=1, source_target_pairs={{0,24},{4,28},{8,16},{12,20},{1,25},{5,29},{9,17},{13,21},{2,26},{... | collective-permute-start | bytes 417800 | tf_op jit(solution)/shard_map/ppermute | solution.py:280
  17.0 6.6 %collective-permute-start.4 = (bf16[544,128]{1,0:T(8,128)(2,1)}, bf16[544,128]{1,0:T(8,128)(2,1)S(1)}, u32[]{:S(2)}, u32[]{:S(2)}) collective-permute-start(bf16[544,128]{1,0:T(8,128)(2,1)} %get-tuple-element.26), channel_id=1, source_target_pairs={{0,32},{4,36},{8,40},{12,44},{1,33},{5,37},{9,41},{13,45},{2,34},{... | collective-permute-start | bytes 417800 | tf_op jit(solution)/shard_map/ppermute | solution.py:280
  18.3 6.6 %collective-permute-start.5 = (bf16[544,128]{1,0:T(8,128)(2,1)}, bf16[544,128]{1,0:T(8,128)(2,1)S(1)}, u32[]{:S(2)}, u32[]{:S(2)}) collective-permute-start(bf16[544,128]{1,0:T(8,128)(2,1)} %get-tuple-element.27), channel_id=1, source_target_pairs={{0,56},{4,60},{8,48},{12,52},{1,57},{5,61},{9,49},{13,53},{2,58},{... | collective-permute-start | bytes 417800 | tf_op jit(solution)/shard_map/ppermute | solution.py:280
  19.6 7.3 %collective-permute-start.6 = (bf16[544,128]{1,0:T(8,128)(2,1)}, bf16[544,128]{1,0:T(8,128)(2,1)S(1)}, u32[]{:S(2)}, u32[]{:S(2)}) collective-permute-start(bf16[544,128]{1,0:T(8,128)(2,1)} %get-tuple-element.28), channel_id=1, source_target_pairs={{0,64},{4,68},{8,72},{12,76},{1,65},{5,69},{9,73},{13,77},{2,66},{... | collective-permute-start | bytes 417800 | tf_op jit(solution)/shard_map/ppermute | solution.py:280
  20.9 9.0 %collective-permute-start.7 = (bf16[544,128]{1,0:T(8,128)(2,1)}, bf16[544,128]{1,0:T(8,128)(2,1)S(1)}, u32[]{:S(2)}, u32[]{:S(2)}) collective-permute-start(bf16[544,128]{1,0:T(8,128)(2,1)} %get-tuple-element.29), channel_id=1, source_target_pairs={{0,88},{4,92},{8,80},{12,84},{1,89},{5,93},{9,81},{13,85},{2,90},{... | collective-permute-start | bytes 417800 | tf_op jit(solution)/shard_map/ppermute | solution.py:280
  22.2 7.7 %copy-start.3 = (bf16[544,128]{1,0:T(8,128)(2,1)}, bf16[544,128]{1,0:T(8,128)(2,1)S(1)}, u32[]{:S(2)}) copy-start(bf16[544,128]{1,0:T(8,128)(2,1)S(1)} %collective-permute-done.3.refs_1_) | copy-start | bytes 417796
  22.2 7.7 %collective-permute-start.8 = (bf16[544,128]{1,0:T(8,128)(2,1)}, bf16[544,128]{1,0:T(8,128)(2,1)S(1)}, u32[]{:S(2)}, u32[]{:S(2)}) collective-permute-start(bf16[544,128]{1,0:T(8,128)(2,1)} %get-tuple-element.30), channel_id=1, source_target_pairs={{0,96},{4,100},{8,104},{12,108},{1,97},{5,101},{9,105},{13,109},{2... | collective-permute-start | bytes 417800 | tf_op jit(solution)/shard_map/ppermute | solution.py:280
  23.5 6.4 %copy-start.4 = (bf16[544,128]{1,0:T(8,128)(2,1)}, bf16[544,128]{1,0:T(8,128)(2,1)S(1)}, u32[]{:S(2)}) copy-start(bf16[544,128]{1,0:T(8,128)(2,1)S(1)} %collective-permute-done.4.refs_2_) | copy-start | bytes 417796
  23.6 6.3 %collective-permute-start.9 = (bf16[544,128]{1,0:T(8,128)(2,1)}, bf16[544,128]{1,0:T(8,128)(2,1)S(1)}, u32[]{:S(2)}, u32[]{:S(2)}) collective-permute-start(bf16[544,128]{1,0:T(8,128)(2,1)} %get-tuple-element.31), channel_id=1, source_target_pairs={{0,120},{4,124},{8,112},{12,116},{1,121},{5,125},{9,113},{13,117},... | collective-permute-start | bytes 417800 | tf_op jit(solution)/shard_map/ppermute | solution.py:280
  24.9 5.1 %copy-start.5 = (bf16[544,128]{1,0:T(8,128)(2,1)}, bf16[544,128]{1,0:T(8,128)(2,1)S(1)}, u32[]{:S(2)}) copy-start(bf16[544,128]{1,0:T(8,128)(2,1)S(1)} %collective-permute-done.5.refs_3_) | copy-start | bytes 417796
  26.9 3.0 %copy-start.6 = (bf16[544,128]{1,0:T(8,128)(2,1)}, bf16[544,128]{1,0:T(8,128)(2,1)S(1)}, u32[]{:S(2)}) copy-start(bf16[544,128]{1,0:T(8,128)(2,1)S(1)} %collective-permute-done.6.refs_4_) | copy-start | bytes 417796
  29.9 0.6 copy-start.7
  29.9 0.7 copy-start.8
  29.9 0.7 copy-start.9
  54.3 14.9 %copy-start = (bf16[64,32,128]{2,1,0:T(8,128)(2,1)}, bf16[64,32,128]{2,1,0:T(8,128)(2,1)S(1)}, u32[]{:S(2)}) copy-start(bf16[64,32,128]{2,1,0:T(8,128)(2,1)S(1)} %all_to_all.15) | copy-start | bytes 1572868
  54.3 14.9 %collective-permute-start.10 = (bf16[16,4,32,128]{3,2,1,0:T(8,128)(2,1)S(1)}, bf16[16,4,32,128]{3,2,1,0:T(8,128)(2,1)S(1)}, u32[]{:S(2)}, u32[]{:S(2)}) collective-permute-start(bf16[16,4,32,128]{3,2,1,0:T(8,128)(2,1)S(1)} %bitcast.18), channel_id=1, source_target_pairs={{0,4},{4,0},{1,5},{5,1},{2,6},{6,2},{3,7},{7,3},{8,12},{12,8},{9,1... | collective-permute-start | bytes 1572872 | tf_op jit(solution)/shard_map/ppermute | solution.py:296
  58.4 5.3 %collective-permute-start.2 = (bf16[520,128]{1,0:T(8,128)(2,1)}, bf16[520,128]{1,0:T(8,128)(2,1)S(1)}, u32[]{:S(2)}, u32[]{:S(2)}) collective-permute-start(bf16[520,128]{1,0:T(8,128)(2,1)} %get-tuple-element.23.own), channel_id=1, source_target_pairs={{0,3},{1,0},{2,1},{3,2},{4,7},{5,4},{6,5},{7,6},{8,11},{9,8},{10,9... | collective-permute-start | bytes 399368 | tf_op jit(solution)/shard_map/ppermute | solution.py:277
  59.1 6.5 %collective-permute-start.1 = (bf16[520,128]{1,0:T(8,128)(2,1)}, bf16[520,128]{1,0:T(8,128)(2,1)S(1)}, u32[]{:S(2)}, u32[]{:S(2)}) collective-permute-start(bf16[520,128]{1,0:T(8,128)(2,1)} %get-tuple-element.23.own), channel_id=1, source_target_pairs={{0,2},{1,3},{2,0},{3,1},{4,6},{5,7},{6,4},{7,5},{8,10},{9,11},{10,... | collective-permute-start | bytes 399368 | tf_op jit(solution)/shard_map/ppermute | solution.py:277
  60.6 8.5 %collective-permute-start = (bf16[520,128]{1,0:T(8,128)(2,1)}, bf16[520,128]{1,0:T(8,128)(2,1)S(1)}, u32[]{:S(2)}, u32[]{:S(2)}) collective-permute-start(bf16[520,128]{1,0:T(8,128)(2,1)} %get-tuple-element.23.own), channel_id=1, source_target_pairs={{0,1},{1,2},{2,3},{3,0},{4,5},{5,6},{6,7},{7,4},{8,9},{9,10},{10,1... | collective-permute-start | bytes 399368 | tf_op jit(solution)/shard_map/ppermute | solution.py:277
  63.7 5.4 %copy-start.10 = (bf16[520,128]{1,0:T(8,128)(2,1)}, bf16[520,128]{1,0:T(8,128)(2,1)S(1)}, u32[]{:S(2)}) copy-start(bf16[520,128]{1,0:T(8,128)(2,1)S(1)} %collective-permute-done.2.d3) | copy-start | bytes 399364
  65.6 3.5 %copy-start.11 = (bf16[520,128]{1,0:T(8,128)(2,1)}, bf16[520,128]{1,0:T(8,128)(2,1)S(1)}, u32[]{:S(2)}) copy-start(bf16[520,128]{1,0:T(8,128)(2,1)S(1)} %collective-permute-done.1.d2) | copy-start | bytes 399364
  69.1 0.7 copy-start.12
  69.2 0.9 copy-start.1
  75.4 13.8 %all-to-all-start.1 = ((f32[32,8,128]{2,1,0:T(8,128)}), f32[32,8,128]{2,1,0:T(8,128)S(1)}, u32[]{:S(2)}, u32[]{:S(2)}) async-start(f32[32,8,128]{2,1,0:T(8,128)} %get-tuple-element.38), calls=%async_computation.1 | async-start | bytes 262144 | tf_op jit(solution)/shard_map/all_to_all | solution.py:341
  89.2 0.7 copy-start.2
  92.6 19.0 %all-to-all-start.2 = ((bf16[128,8,128]{2,1,0:T(8,128)(2,1)}), bf16[128,8,128]{2,1,0:T(8,128)(2,1)S(1)}, u32[]{:S(2)}, u32[]{:S(2)}) async-start(bf16[128,8,128]{2,1,0:T(8,128)(2,1)} %solve.1), calls=%async_computation.2 | async-start | bytes 524288 | tf_op jit(solution)/shard_map/all_to_all | solution.py:350
Sparse Core Ops, SparseCore 0:
  33.0 51.8 all-gather.2

commit v2 on v1

--- a/solution.py
+++ b/solution.py
@@ -18,6 +18,7 @@
 WIDE = ("chip", "core")
 PIECES = 8
 CPP = NC // PIECES
+SCATTER_ORDER = (4, 5, 2, 3, 6, 7, 1)
 SUB = 16
 EXTRA = SUB + 8 + 8
 
@@ -45,9 +46,8 @@
     return jnp.where(fn(r) == c, 1.0, 0.0).astype(BF)
 
 
-def prep_kernel(row_ref, col_ref, b_ref, mask_ref, *outs):
+def row_kernel(row_ref, b_ref, mask_ref, *sent):
     q = lax.axis_index("narrow")
-    sent, mine = outs[:PIECES], outs[PIECES]
     gather = one_hot(BS, lambda r: (r % SUB) * 8 + r // SUB)
     for ct in range(NC // 8):
         for ag in range(BS // SUB):
@@ -59,11 +59,6 @@
                 sent[p][cc * BS + ag * SUB : cc * BS + (ag + 1) * SUB] = blocks[e * SUB : (e + 1) * SUB]
             if ct == 0:
                 sent[ag][CPP * BS : CPP * BS + SUB] = blocks[:SUB]
-    pick = one_hot(SUB, lambda r: r * 8)
-    for r in range(NR):
-        for ag in range(BS // SUB):
-            native = col_ref[r, ag * SUB : (ag + 1) * SUB].astype(F32).reshape(BS, BS).astype(BF)
-            mine[r * BS + ag * SUB : r * BS + (ag + 1) * SUB] = dot(pick, native).astype(BF)
     mask = mask_ref[...].astype(F32)
     widen = one_hot(NC, lambda r: r)
     line = jnp.broadcast_to(dot(mask.astype(BF), widen)[0:1], (8, BS)).astype(BF)
@@ -73,7 +68,15 @@
         rows = jnp.where((q & 1) != 0, rows[:, BS:], rows[:, :BS])
         sent[p][CPP * BS + SUB : CPP * BS + SUB + 8] = rows.astype(BF)
         sent[p][CPP * BS + SUB + 8 :] = line
-    first = jnp.broadcast_to(mask[:, 0:1], (NR, BS))
+
+
+def column_kernel(col_ref, mask_ref, mine):
+    pick = one_hot(SUB, lambda r: r * 8)
+    for r in range(NR):
+        for ag in range(BS // SUB):
+            native = col_ref[r, ag * SUB : (ag + 1) * SUB].astype(F32).reshape(BS, BS).astype(BF)
+            mine[r * BS + ag * SUB : r * BS + (ag + 1) * SUB] = dot(pick, native).astype(BF)
+    first = jnp.broadcast_to(mask_ref[...].astype(F32)[:, 0:1], (NR, BS))
     mine[NR * BS :] = jnp.concatenate([first, jnp.zeros((8 - NR, BS), F32)], axis=0).astype(BF)
 
 
@@ -167,10 +170,13 @@
         ztall[...] = dot(bk, weight, 0, 0).astype(BF).astype(F32)
         for j in range(2):
             zt[s * 2 + j : s * 2 + j + 1] = ztall[pl.ds(j * BS + q * NW + w, 1), :]
-        for ref, base, part in ((lown[:, s * BS : (s + 1) * BS], 0, NR), (lpiv[s], NR, NP)):
-            elim = dot(ref, z)
-            for i in range(part):
-                bs[base + i] = (bs[base + i] - elim[i * BS : (i + 1) * BS]).astype(BF).astype(F32)
+        elim = dot(lown[:, s * BS : (s + 1) * BS], z)
+        for i in range(NR):
+            bs[i] = (bs[i] - elim[i * BS : (i + 1) * BS]).astype(BF).astype(F32)
+        for t in range(s + 1, NP):
+            i = order[t]
+            elim = dot(lpiv[s, pl.ds(pl.multiple_of(i * BS, BS), BS), :], z)
+            bs[NR + i] = (bs[NR + i] - elim).astype(BF).astype(F32)
     for r in range(NR):
         frhs[r] = bs[r].astype(BF)
 
@@ -199,20 +205,21 @@
 
     base = [lown[:, s * BS : (s + 1) * BS].astype(F32) for s in range(NP)]
     r3 = right(base[3], 3)
+    h[14] = r3
     r3_low = [dot(r3, low(3, s)) for s in range(3)]
     for m3 in range(2):
         c3 = [base[s] - r3_low[s] if m3 else base[s] for s in range(3)]
         r2 = right(c3[2], 2)
+        h[12 + m3] = r2
         r2_low = [dot(r2, low(2, s)) for s in range(2)]
         for m2 in range(2):
             c2 = [c3[s] - r2_low[s] if m2 else c3[s] for s in range(2)]
             r1 = right(c2[1], 1)
+            h[8 + m2 + 2 * m3] = r1
             r1_low = dot(r1, low(1, 0))
             for m1 in range(2):
                 r0 = right(c2[0] - r1_low if m1 else c2[0], 0)
-                pat = m1 + 2 * m2 + 4 * m3
-                for s, block in enumerate((r0, r1, r2, r3)):
-                    h[pat, :, pl.ds(pl.multiple_of(order[s] * BS, BS), BS)] = block
+                h[m1 + 2 * m2 + 4 * m3] = r0
 
 
 GC = 8
@@ -226,11 +233,15 @@
     cols_out = []
     for col in range(GC):
         c = g * GC + col
-        pat = mpiv[order[1], c] + 2 * mpiv[order[2], c] + 4 * mpiv[order[3], c]
+        m1, m2, m3 = (mpiv[order[s], c] for s in range(1, NP))
+        left = [h[m1 + 2 * m2 + 4 * m3], h[8 + m2 + 2 * m3], h[12 + m3], h[14]]
         p, cc = divmod(col, CPP)
-        raw = [u_ref[holder(p, k), cc * BS : (cc + 1) * BS] for k in range(NP)]
-        raw = jnp.concatenate(raw, axis=0)
-        lu = dot(h[pat], raw)
+        raw = []
+        for s in range(NP):
+            zg, core = order[s] >> 1, order[s] & 1
+            z = zg if p == 0 else 3 - zg
+            raw.append(u_ref[2 * z + core, cc * BS : (cc + 1) * BS])
+        lu = dot(jnp.concatenate(left, axis=1), jnp.concatenate(raw, axis=0))
         parts = []
         for r in range(NR):
             parts.append(jnp.where(mown[r, c] != 0, lu[r * BS : (r + 1) * BS], 0.0).astype(BF))
@@ -264,21 +275,29 @@
     y = trail_sol.reshape(NR, BS, NRHS)
 
     fixed = lambda shape: pl.BlockSpec(shape, lambda g: (0,) * len(shape))
-    shapes = [(CPP * BS + EXTRA, BS)] * PIECES + [(NR * BS + 8, BS)]
-    *sent, mine = pl.pallas_call(
-        prep_kernel,
-        out_shape=tuple(jax.ShapeDtypeStruct(shape, BF) for shape in shapes),
+    sent = pl.pallas_call(
+        row_kernel,
+        out_shape=(jax.ShapeDtypeStruct((CPP * BS + EXTRA, BS), BF),) * PIECES,
         grid=(1,),
-        in_specs=[fixed((1, BS, NC, BS)), fixed((NR, BS, 8, BS)), fixed((1, BS, NRHS)), fixed((NR, NC))],
-        out_specs=tuple(fixed(shape) for shape in shapes),
-        name="prep",
-    )(blocks, blocks, b, mask)
-
+        in_specs=[fixed((1, BS, NC, BS)), fixed((1, BS, NRHS)), fixed((NR, NC))],
+        out_specs=(fixed((CPP * BS + EXTRA, BS)),) * PIECES,
+        name="row",
+    )(blocks, b, mask)
+
+    pieces = []
+    for p in SCATTER_ORDER:
+        pieces.append(lax.ppermute(sent[p], WIDE, [(i, holder(p, i)) for i in range(NP)]))
+
+    mine = pl.pallas_call(
+        column_kernel,
+        out_shape=jax.ShapeDtypeStruct((NR * BS + 8, BS), BF),
+        grid=(1,),
+        in_specs=[fixed((NR, BS, 8, BS)), fixed((NR, NC))],
+        out_specs=fixed((NR * BS + 8, BS)),
+        name="own",
+    )(blocks, mask)
     others = [lax.ppermute(mine, "narrow", [(i, (i + d) % 4) for i in range(4)]) for d in (1, 2, 3)]
 
-    pieces = [
-        lax.ppermute(sent[p], WIDE, [(i, holder(p, i)) for i in range(NP)]) for p in range(1, PIECES)
-    ]
     piece, copies = pl.pallas_call(
         merge_kernel,
         out_shape=(
@@ -332,7 +351,7 @@
 
     h = pl.pallas_call(
         combine_kernel,
-        out_shape=jax.ShapeDtypeStruct((8, NR * BS, NP * BS), BF),
+        out_shape=jax.ShapeDtypeStruct((15, NR * BS, BS), BF),
         in_specs=smem(1) + vmem(3),
         out_specs=vmem(1)[0],
         name="combine",
@@ -357,7 +376,7 @@
         + [
             pl.BlockSpec((NR, BS, GC, BS), lambda g: (0, 0, g, 0)),
             pl.BlockSpec((8, CPP * BS, BS), lambda g: (g, 0, 0)),
-            fixed((8, NR * BS, NP * BS)),
+            fixed((15, NR * BS, BS)),
             fixed((NR * BS, BS)),
         ],
         out_specs=pl.BlockSpec((NR, BS, GC, BS), lambda g: (0, 0, g, 0)),

time: 120 us -> 120 us (level)
  starting transfers between devices: 32.7 us -> 34.6 us
  waiting for transfers between devices: 13.9 us -> 12.3 us
    ppermute x7, waiting for transfers between devices: 5.02 us -> 2.96 us  [body(): lax.ppermute(sent[p], WIDE, [(i, holder(p, i)) for i in range(NP)])]
    ppermute x7, starting transfers between devices: 14.3 us -> 16.1 us  [body(): lax.ppermute(sent[p], WIDE, [(i, holder(p, i)) for i in range(NP)])]
    pallas_call x2 -> x3, Pallas kernels: 8.81 us -> 9.24 us  [the longest x1 4.29 us: body(): pl.pallas_call(combine_kernel, out_shape=jax.ShapeDtypeStruct((15, NR * B...]
where the time goes in v2:
time: 120 us
  starting transfers between devices  34.6 us (29%)
  Pallas kernels  33.9 us (28%)
  blocking collectives  21.1 us (18%)
  between operations  14.2 us (12%)
  waiting for transfers between devices  12.3 us (10%)
  local copies, waits for them, and re-layouts  3.41 us (3%)
    all_to_all x1, blocking collectives, body(): lax.all_to_all(copies, ('chip', 'narrow'), 0, 0)  21.1 us
    ppermute x7, starting transfers between devices, body(): lax.ppermute(sent[p], WIDE, [(i, holder(p, i)) for i in range(NP)])  16.1 us
    pallas_call x1, Pallas kernels, body(): pl.pallas_call(update_kernel, out_shape=jax.ShapeDtypeStruct((NR, BS, NC,...  9.93 us
    ppermute x3, waiting for transfers between devices, body(): lax.ppermute(mine, 'narrow', [(i, (i + d) % 4) for i in range(4)])  8.39 us
    all_to_all x1, starting transfers between devices, body(): xall = lax.all_to_all(xg, ('narrow', *WIDE), 0, 0)  8.08 us
    pallas_call x1, Pallas kernels, body(): pl.pallas_call(panel_kernel, out_shape=(jax.ShapeDtypeStruct((NR * BS, NP...  5.46 us
    pallas_call x1, Pallas kernels, body(): pl.pallas_call(combine_kernel, out_shape=jax.ShapeDtypeStruct((15, NR * B...  4.29 us
    pallas_call x1, Pallas kernels, body(): pl.pallas_call(forward_kernel, out_shape=(jax.ShapeDtypeStruct((8, BS), F...  4.25 us
  transfers between devices with their start and end apart: 14, of which 6 were waited for; matrix products, arithmetic and copies ran while one was open for 0% of the time, Pallas kernels for 24%

profile of v2, /device:TPU:1, one launch (start us, length us, event | category | flops | bytes accessed | tf_op | source)
XLA Modules:
  0.0 119.6 jit_solution(10541913215629249293)
XLA Ops:
  7.2 0.0 all-gather.3.cloned.1.call-start
  7.2 2.7 %row.1 = (bf16[544,128]{1,0:T(8,128)(2,1)}, bf16[544,128]{1,0:T(8,128)(2,1)}, bf16[544,128]{1,0:T(8,128)(2,1)}, bf16[544,128]{1,0:T(8,128)(2,1)}, bf16[544,128]{...) custom-call(bf16[4,128,32,128]{3,2,1,0:T(8,128)(2,1)} %bitcast.15, ...), custom_call_target="tpu_custom_call" | custom-call | tf_op jit(solution)/shard_map/row/pallas_call | solution.py:278
  9.9 5.5 %collective-permute-start.3 = (bf16[544,128]{1,0:T(8,128)(2,1)}, bf16[544,128]{1,0:T(8,128)(2,1)S(1)}, u32[]{:S(2)}, u32[]{:S(2)}) collective-permute-start(bf16[544,128]{1,0:T(8,128)(2,1)} %get-tuple-element.23), channel_id=1, source_target_pairs={{0,64},{4,68},{8,72},{12,76},{1,65},{5,69},{9,73},{13,77},{2,66},{... | collective-permute-start | bytes 417800 | tf_op jit(solution)/shard_map/ppermute | solution.py:289
  15.4 4.1 %collective-permute-start.4 = (bf16[544,128]{1,0:T(8,128)(2,1)}, bf16[544,128]{1,0:T(8,128)(2,1)S(1)}, u32[]{:S(2)}, u32[]{:S(2)}) collective-permute-start(bf16[544,128]{1,0:T(8,128)(2,1)} %get-tuple-element.24), channel_id=1, source_target_pairs={{0,88},{4,92},{8,80},{12,84},{1,89},{5,93},{9,81},{13,85},{2,90},{... | collective-permute-start | bytes 417800 | tf_op jit(solution)/shard_map/ppermute | solution.py:289
  19.5 1.3 %collective-permute-start.5 = (bf16[544,128]{1,0:T(8,128)(2,1)}, bf16[544,128]{1,0:T(8,128)(2,1)S(1)}, u32[]{:S(2)}, u32[]{:S(2)}) collective-permute-start(bf16[544,128]{1,0:T(8,128)(2,1)} %get-tuple-element.25), channel_id=1, source_target_pairs={{0,32},{4,36},{8,40},{12,44},{1,33},{5,37},{9,41},{13,45},{2,34},{... | collective-permute-start | bytes 417800 | tf_op jit(solution)/shard_map/ppermute | solution.py:289
  20.8 1.3 %collective-permute-start.6 = (bf16[544,128]{1,0:T(8,128)(2,1)}, bf16[544,128]{1,0:T(8,128)(2,1)S(1)}, u32[]{:S(2)}, u32[]{:S(2)}) collective-permute-start(bf16[544,128]{1,0:T(8,128)(2,1)} %get-tuple-element.26), channel_id=1, source_target_pairs={{0,56},{4,60},{8,48},{12,52},{1,57},{5,61},{9,49},{13,53},{2,58},{... | collective-permute-start | bytes 417800 | tf_op jit(solution)/shard_map/ppermute | solution.py:289
  22.1 1.3 %collective-permute-start.7 = (bf16[544,128]{1,0:T(8,128)(2,1)}, bf16[544,128]{1,0:T(8,128)(2,1)S(1)}, u32[]{:S(2)}, u32[]{:S(2)}) collective-permute-start(bf16[544,128]{1,0:T(8,128)(2,1)} %get-tuple-element.27), channel_id=1, source_target_pairs={{0,96},{4,100},{8,104},{12,108},{1,97},{5,101},{9,105},{13,109},{2... | collective-permute-start | bytes 417800 | tf_op jit(solution)/shard_map/ppermute | solution.py:289
  23.4 0.0 collective-permute-done.3.refs_1_
  23.4 0.0 copy-start.3
  23.4 1.3 %collective-permute-start.8 = (bf16[544,128]{1,0:T(8,128)(2,1)}, bf16[544,128]{1,0:T(8,128)(2,1)S(1)}, u32[]{:S(2)}, u32[]{:S(2)}) collective-permute-start(bf16[544,128]{1,0:T(8,128)(2,1)} %get-tuple-element.28), channel_id=1, source_target_pairs={{0,120},{4,124},{8,112},{12,116},{1,121},{5,125},{9,113},{13,117},... | collective-permute-start | bytes 417800 | tf_op jit(solution)/shard_map/ppermute | solution.py:289
  24.7 0.0 collective-permute-done.4.refs_2_
  24.8 1.3 %collective-permute-start.9 = (bf16[544,128]{1,0:T(8,128)(2,1)}, bf16[544,128]{1,0:T(8,128)(2,1)S(1)}, u32[]{:S(2)}, u32[]{:S(2)}) collective-permute-start(bf16[544,128]{1,0:T(8,128)(2,1)} %get-tuple-element.29), channel_id=1, source_target_pairs={{0,24},{4,28},{8,16},{12,20},{1,25},{5,29},{9,17},{13,21},{2,26},{... | collective-permute-start | bytes 417800 | tf_op jit(solution)/shard_map/ppermute | solution.py:289
  26.1 0.0 collective-permute-done.5.refs_3_
  26.1 0.0 copy-start.5
  26.1 2.0 %collective-permute-done.6.refs_4_ = bf16[544,128]{1,0:T(8,128)(2,1)S(1)} collective-permute-done((bf16[544,128]{1,0:T(8,128)(2,1)}, bf16[544,128]{1,0:T(8,128)(2,1)S(1)}, u32[]{:S(2)}, u32[]{:S(2)}) %collective-permute-start.6) | collective-permute-done | bytes 139296 | tf_op jit(solution)/shard_map/ppermute | solution.py:289
  28.1 0.0 collective-permute-done.7.refs_5_
  28.1 0.9 collective-permute-done.8.refs_6_
  29.1 0.0 collective-permute-done.9.refs_7_
  29.1 0.0 copy-done.4
  29.1 0.6 copy-done.8
  29.7 0.1 copy-done.9
  29.8 2.3 %merge.1 = (bf16[512,128]{1,0:T(8,128)(2,1)}, bf16[64,32,128]{2,1,0:T(8,128)(2,1)}) custom-call(bf16[544,128]{1,0:T(8,128)(2,1)} %get-tuple-element.22.refs_0_, bf16[544,128]{1,0:T(8,128)(2,1)} %copy-done.3, bf16[544,128]{1,0:T(8,128)(2,1)} %copy-done.4, bf16[544,128]{1,0:T(8,128)(2,1)} %copy-done.5, bf16[544,128]{1,0:T(8,128)(2,1)} %copy-done.6, ...), custom_call_target="tpu_custom_call" | custom-call | tf_op jit(solution)/shard_map/merge/pallas_call | solution.py:301
  32.0 0.0 all-gather.3.cloned.1.call-update
  32.0 21.1 %all_to_all.15 = bf16[64,32,128]{2,1,0:T(8,128)(2,1)S(1)} all-to-all(bf16[64,32,128]{2,1,0:T(8,128)(2,1)} %get-tuple-element.30), channel_id=1, replica_groups=mesh['chip'=16,'core'=2,'narrow'=4] {'chip','narrow'}, dimensions={0} | all-to-all | bytes 1048576 | tf_op jit(solution)/shard_map/all_to_all | solution.py:314
  53.1 4.2 %collective-permute-start.10 = (bf16[16,4,32,128]{3,2,1,0:T(8,128)(2,1)S(1)}, bf16[16,4,32,128]{3,2,1,0:T(8,128)(2,1)S(1)}, u32[]{:S(2)}, u32[]{:S(2)}) collective-permute-start(bf16[16,4,32,128]{3,2,1,0:T(8,128)(2,1)S(1)} %bitcast.18), channel_id=1, source_target_pairs={{0,4},{4,0},{1,5},{5,1},{2,6},{6,2},{3,7},{7,3},{8,12},{12,8},{9,1... | collective-permute-start | bytes 1572872 | tf_op jit(solution)/shard_map/ppermute | solution.py:315
  57.3 2.3 %own.1 = bf16[520,128]{1,0:T(8,128)(2,1)} custom-call(bf16[4,128,32,128]{3,2,1,0:T(8,128)(2,1)} %bitcast.16, s32[4,32]{1,0:T(4,128)} %bitcast.28), custom_call_target="tpu_custom_call" | custom-call | tf_op jit(solution)/shard_map/own/pallas_call | solution.py:291
  59.5 0.7 collective-permute-start.2
  60.2 1.5 %collective-permute-start.1 = (bf16[520,128]{1,0:T(8,128)(2,1)}, bf16[520,128]{1,0:T(8,128)(2,1)S(1)}, u32[]{:S(2)}, u32[]{:S(2)}) collective-permute-start(bf16[520,128]{1,0:T(8,128)(2,1)} %own.1), channel_id=1, source_target_pairs={{0,2},{1,3},{2,0},{3,1},{4,6},{5,7},{6,4},{7,5},{8,10},{9,11},{10,... | collective-permute-start | bytes 399368 | tf_op jit(solution)/shard_map/ppermute | solution.py:299
  61.7 0.0 collective-permute-start
  61.7 2.9 %collective-permute-done.2.d3 = bf16[520,128]{1,0:T(8,128)(2,1)S(1)} collective-permute-done((bf16[520,128]{1,0:T(8,128)(2,1)}, bf16[520,128]{1,0:T(8,128)(2,1)S(1)}, u32[]{:S(2)}, u32[]{:S(2)}) %collective-permute-start.2) | collective-permute-done | bytes 133152 | tf_op jit(solution)/shard_map/ppermute | solution.py:299
  64.6 1.9 %collective-permute-done.1.d2 = bf16[520,128]{1,0:T(8,128)(2,1)S(1)} collective-permute-done((bf16[520,128]{1,0:T(8,128)(2,1)}, bf16[520,128]{1,0:T(8,128)(2,1)S(1)}, u32[]{:S(2)}, u32[]{:S(2)}) %collective-permute-start.1) | collective-permute-done | bytes 133152 | tf_op jit(solution)/shard_map/ppermute | solution.py:299
  66.6 3.5 %collective-permute-done.d1 = bf16[520,128]{1,0:T(8,128)(2,1)S(1)} collective-permute-done((bf16[520,128]{1,0:T(8,128)(2,1)}, bf16[520,128]{1,0:T(8,128)(2,1)S(1)}, u32[]{:S(2)}, u32[]{:S(2)}) %collective-permute-start) | collective-permute-done | bytes 133152 | tf_op jit(solution)/shard_map/ppermute | solution.py:299
  70.1 0.0 collective-permute-done.10.far
  70.1 0.6 copy-done.12
  70.8 0.2 copy-done.1
  70.9 5.5 %panel.1 = (bf16[512,512]{1,0:T(8,128)(2,1)}, bf16[4,512,128]{2,1,0:T(8,128)(2,1)}, f32[32,8,128]{2,1,0:T(8,128)}, bf16[512,128]{1,0:T(8,128)(2,1)}, s32[4,128]{1,0:T(4,128)}) custom-call(s32[4]{0:T(128)} %order.9, bf16[520,128]{1,0:T(8,128)(2,1)} %own.1, bf16[520,128]{1,0:T(8,128)(2,1)} %copy-done.12, bf16[520,128]{1,0:T(8,128)(2,1)} %copy-done.11, ...), custom_call_target="tpu_custom_call" | custom-call | tf_op jit(solution)/shard_map/panel/pallas_call | solution.py:317
  76.4 4.1 %all-to-all-start.1 = ((f32[32,8,128]{2,1,0:T(8,128)}), f32[32,8,128]{2,1,0:T(8,128)S(1)}, u32[]{:S(2)}, u32[]{:S(2)}) async-start(f32[32,8,128]{2,1,0:T(8,128)} %get-tuple-element.36), calls=%async_computation.1 | async-start | bytes 262144 | tf_op jit(solution)/shard_map/all_to_all | solution.py:360
  80.5 4.3 %combine.1.h = bf16[15,512,128]{2,1,0:T(8,128)(2,1)} custom-call(s32[4]{0:T(128)} %order.9, bf16[512,512]{1,0:T(8,128)(2,1)} %get-tuple-element.33.lown, bf16[4,512,128]{2,1,0:T(8,128)(2,1)} %get-tuple-element.34.lpiv, bf16[4,128,128]{2,1,0:T(8,128)(2,1)} %w_ref.7), custom_call_target="tpu_custom_call" | custom-call | tf_op jit(solution)/shard_map/combine/pallas_call | solution.py:352
  84.8 4.3 %forward.1 = (f32[8,128]{1,0:T(8,128)}, bf16[4,128,256]{2,1,0:T(8,128)(2,1)}) custom-call(s32[4]{0:T(128)} %order.9, bf16[16,4,32,128]{3,2,1,0:T(8,128)(2,1)} %bitcast.20, bf16[16,4,32,128]{3,2,1,0:T(8,128)(2,1)} %copy-done.1, bf16[4,128,128]{2,1,0:T(8,128)(2,1)} %w_ref.7, bf16[4,128,256]{2,1,0:T(8,128)(2,1)} %bitcast.25, ...), custom_call_target="tpu_custom_call" | custom-call | tf_op jit(solution)/shard_map/forward/pallas_call | solution.py:337
  89.0 0.0 all-to-all-done.1.parts
  89.0 0.7 copy-done.2
  89.7 2.8 %solve.1 = bf16[128,8,128]{2,1,0:T(8,128)(2,1)} custom-call(s32[4]{0:T(128)} %order.9, f32[32,8,128]{2,1,0:T(8,128)} %copy-done.2, f32[8,128]{1,0:T(8,128)} %get-tuple-element.37.zt, bf16[4,512,128]{2,1,0:T(8,128)(2,1)} %get-tuple-element.34.lpiv, bf16[4,128,128]{2,1,0:T(8,128)(2,1)} %w_ref.7, bf16[15,512,128]{2,1,0:T(8,128)(2,1)} %combine.1.h), custom_call_target="tpu_custom_call" | custom-call | tf_op jit(solution)/shard_map/solve/pallas_call | solution.py:361
  92.5 8.1 %all-to-all-start.2 = ((bf16[128,8,128]{2,1,0:T(8,128)(2,1)}), bf16[128,8,128]{2,1,0:T(8,128)(2,1)S(1)}, u32[]{:S(2)}, u32[]{:S(2)}) async-start(bf16[128,8,128]{2,1,0:T(8,128)(2,1)} %solve.1), calls=%async_computation.2 | async-start | bytes 524288 | tf_op jit(solution)/shard_map/all_to_all | solution.py:369
  100.6 0.0 all-gather.3.cloned.1.call-done
  100.6 9.9 %update.1 = bf16[4,128,32,128]{3,2,1,0:T(8,128)(2,1)} custom-call(s32[4]{0:T(128)} %order.9, s32[4,32]{1,0:T(4,128)} %bitcast.29, s32[4,128]{1,0:T(4,128)} %get-tuple-element.31.mpiv, bf16[4,128,32,128]{3,2,1,0:T(8,128)(2,1)} %bitcast.17, bf16[32,512,128]{2,1,0:T(8,128)(2,1)} %bitcast.21, bf16[15,512,128]{2,1,0:T(8,128)(2,1)} %combine.1.h, ...), custom_call_target="tpu_custom_call" | custom-call | tf_op jit(solution)/shard_map/update/pallas_call | solution.py:371
  110.5 0.9 all-to-all-done.2
  111.5 0.4 copy.9
  111.9 0.9 reshape.41
  (18 shorter events, 0.0 us)
Async XLA Ops:
  7.2 93.4 %all-gather.3.cloned.1.call-start = ((), (), s32[]{:S(2)}) async-start(), calls=%async_computation.3 | async-start | bytes 4325376 | tf_op jit(solution)/shard_map/all_gather | solution.py:312
  9.9 13.5 %collective-permute-start.3 = (bf16[544,128]{1,0:T(8,128)(2,1)}, bf16[544,128]{1,0:T(8,128)(2,1)S(1)}, u32[]{:S(2)}, u32[]{:S(2)}) collective-permute-start(bf16[544,128]{1,0:T(8,128)(2,1)} %get-tuple-element.23), channel_id=1, source_target_pairs={{0,64},{4,68},{8,72},{12,76},{1,65},{5,69},{9,73},{13,77},{2,66},{... | collective-permute-start | bytes 417800 | tf_op jit(solution)/shard_map/ppermute | solution.py:289
  15.4 9.4 %collective-permute-start.4 = (bf16[544,128]{1,0:T(8,128)(2,1)}, bf16[544,128]{1,0:T(8,128)(2,1)S(1)}, u32[]{:S(2)}, u32[]{:S(2)}) collective-permute-start(bf16[544,128]{1,0:T(8,128)(2,1)} %get-tuple-element.24), channel_id=1, source_target_pairs={{0,88},{4,92},{8,80},{12,84},{1,89},{5,93},{9,81},{13,85},{2,90},{... | collective-permute-start | bytes 417800 | tf_op jit(solution)/shard_map/ppermute | solution.py:289
  19.5 6.6 %collective-permute-start.5 = (bf16[544,128]{1,0:T(8,128)(2,1)}, bf16[544,128]{1,0:T(8,128)(2,1)S(1)}, u32[]{:S(2)}, u32[]{:S(2)}) collective-permute-start(bf16[544,128]{1,0:T(8,128)(2,1)} %get-tuple-element.25), channel_id=1, source_target_pairs={{0,32},{4,36},{8,40},{12,44},{1,33},{5,37},{9,41},{13,45},{2,34},{... | collective-permute-start | bytes 417800 | tf_op jit(solution)/shard_map/ppermute | solution.py:289
  20.8 7.3 %collective-permute-start.6 = (bf16[544,128]{1,0:T(8,128)(2,1)}, bf16[544,128]{1,0:T(8,128)(2,1)S(1)}, u32[]{:S(2)}, u32[]{:S(2)}) collective-permute-start(bf16[544,128]{1,0:T(8,128)(2,1)} %get-tuple-element.26), channel_id=1, source_target_pairs={{0,56},{4,60},{8,48},{12,52},{1,57},{5,61},{9,49},{13,53},{2,58},{... | collective-permute-start | bytes 417800 | tf_op jit(solution)/shard_map/ppermute | solution.py:289
  22.1 6.0 %collective-permute-start.7 = (bf16[544,128]{1,0:T(8,128)(2,1)}, bf16[544,128]{1,0:T(8,128)(2,1)S(1)}, u32[]{:S(2)}, u32[]{:S(2)}) collective-permute-start(bf16[544,128]{1,0:T(8,128)(2,1)} %get-tuple-element.27), channel_id=1, source_target_pairs={{0,96},{4,100},{8,104},{12,108},{1,97},{5,101},{9,105},{13,109},{2... | collective-permute-start | bytes 417800 | tf_op jit(solution)/shard_map/ppermute | solution.py:289
  23.4 5.6 %copy-start.3 = (bf16[544,128]{1,0:T(8,128)(2,1)}, bf16[544,128]{1,0:T(8,128)(2,1)S(1)}, u32[]{:S(2)}) copy-start(bf16[544,128]{1,0:T(8,128)(2,1)S(1)} %collective-permute-done.3.refs_1_) | copy-start | bytes 417796
  23.4 5.6 %collective-permute-start.8 = (bf16[544,128]{1,0:T(8,128)(2,1)}, bf16[544,128]{1,0:T(8,128)(2,1)S(1)}, u32[]{:S(2)}, u32[]{:S(2)}) collective-permute-start(bf16[544,128]{1,0:T(8,128)(2,1)} %get-tuple-element.28), channel_id=1, source_target_pairs={{0,120},{4,124},{8,112},{12,116},{1,121},{5,125},{9,113},{13,117},... | collective-permute-start | bytes 417800 | tf_op jit(solution)/shard_map/ppermute | solution.py:289
  24.8 4.3 %copy-start.4 = (bf16[544,128]{1,0:T(8,128)(2,1)}, bf16[544,128]{1,0:T(8,128)(2,1)S(1)}, u32[]{:S(2)}) copy-start(bf16[544,128]{1,0:T(8,128)(2,1)S(1)} %collective-permute-done.4.refs_2_) | copy-start | bytes 417796
  24.8 4.3 %collective-permute-start.9 = (bf16[544,128]{1,0:T(8,128)(2,1)}, bf16[544,128]{1,0:T(8,128)(2,1)S(1)}, u32[]{:S(2)}, u32[]{:S(2)}) collective-permute-start(bf16[544,128]{1,0:T(8,128)(2,1)} %get-tuple-element.29), channel_id=1, source_target_pairs={{0,24},{4,28},{8,16},{12,20},{1,25},{5,29},{9,17},{13,21},{2,26},{... | collective-permute-start | bytes 417800 | tf_op jit(solution)/shard_map/ppermute | solution.py:289
  26.1 3.0 %copy-start.5 = (bf16[544,128]{1,0:T(8,128)(2,1)}, bf16[544,128]{1,0:T(8,128)(2,1)S(1)}, u32[]{:S(2)}) copy-start(bf16[544,128]{1,0:T(8,128)(2,1)S(1)} %collective-permute-done.5.refs_3_) | copy-start | bytes 417796
  28.1 1.0 copy-start.6
  28.1 1.0 copy-start.7
  29.0 0.7 copy-start.8
  29.1 0.7 copy-start.9
  53.1 17.0 %copy-start = (bf16[64,32,128]{2,1,0:T(8,128)(2,1)}, bf16[64,32,128]{2,1,0:T(8,128)(2,1)S(1)}, u32[]{:S(2)}) copy-start(bf16[64,32,128]{2,1,0:T(8,128)(2,1)S(1)} %all_to_all.15) | copy-start | bytes 1572868
  53.1 17.0 %collective-permute-start.10 = (bf16[16,4,32,128]{3,2,1,0:T(8,128)(2,1)S(1)}, bf16[16,4,32,128]{3,2,1,0:T(8,128)(2,1)S(1)}, u32[]{:S(2)}, u32[]{:S(2)}) collective-permute-start(bf16[16,4,32,128]{3,2,1,0:T(8,128)(2,1)S(1)} %bitcast.18), channel_id=1, source_target_pairs={{0,4},{4,0},{1,5},{5,1},{2,6},{6,2},{3,7},{7,3},{8,12},{12,8},{9,1... | collective-permute-start | bytes 1572872 | tf_op jit(solution)/shard_map/ppermute | solution.py:315
  59.5 5.1 %collective-permute-start.2 = (bf16[520,128]{1,0:T(8,128)(2,1)}, bf16[520,128]{1,0:T(8,128)(2,1)S(1)}, u32[]{:S(2)}, u32[]{:S(2)}) collective-permute-start(bf16[520,128]{1,0:T(8,128)(2,1)} %own.1), channel_id=1, source_target_pairs={{0,3},{1,0},{2,1},{3,2},{4,7},{5,4},{6,5},{7,6},{8,11},{9,8},{10,9... | collective-permute-start | bytes 399368 | tf_op jit(solution)/shard_map/ppermute | solution.py:299
  60.2 6.3 %collective-permute-start.1 = (bf16[520,128]{1,0:T(8,128)(2,1)}, bf16[520,128]{1,0:T(8,128)(2,1)S(1)}, u32[]{:S(2)}, u32[]{:S(2)}) collective-permute-start(bf16[520,128]{1,0:T(8,128)(2,1)} %own.1), channel_id=1, source_target_pairs={{0,2},{1,3},{2,0},{3,1},{4,6},{5,7},{6,4},{7,5},{8,10},{9,11},{10,... | collective-permute-start | bytes 399368 | tf_op jit(solution)/shard_map/ppermute | solution.py:299
  61.7 8.4 %collective-permute-start = (bf16[520,128]{1,0:T(8,128)(2,1)}, bf16[520,128]{1,0:T(8,128)(2,1)S(1)}, u32[]{:S(2)}, u32[]{:S(2)}) collective-permute-start(bf16[520,128]{1,0:T(8,128)(2,1)} %own.1), channel_id=1, source_target_pairs={{0,1},{1,2},{2,3},{3,0},{4,5},{5,6},{6,7},{7,4},{8,9},{9,10},{10,1... | collective-permute-start | bytes 399368 | tf_op jit(solution)/shard_map/ppermute | solution.py:299
  64.6 5.5 %copy-start.10 = (bf16[520,128]{1,0:T(8,128)(2,1)}, bf16[520,128]{1,0:T(8,128)(2,1)S(1)}, u32[]{:S(2)}) copy-start(bf16[520,128]{1,0:T(8,128)(2,1)S(1)} %collective-permute-done.2.d3) | copy-start | bytes 399364
  66.6 3.6 %copy-start.11 = (bf16[520,128]{1,0:T(8,128)(2,1)}, bf16[520,128]{1,0:T(8,128)(2,1)S(1)}, u32[]{:S(2)}) copy-start(bf16[520,128]{1,0:T(8,128)(2,1)S(1)} %collective-permute-done.1.d2) | copy-start | bytes 399364
  70.1 0.7 copy-start.12
  70.1 0.8 copy-start.1
  76.4 12.6 %all-to-all-start.1 = ((f32[32,8,128]{2,1,0:T(8,128)}), f32[32,8,128]{2,1,0:T(8,128)S(1)}, u32[]{:S(2)}, u32[]{:S(2)}) async-start(f32[32,8,128]{2,1,0:T(8,128)} %get-tuple-element.36), calls=%async_computation.1 | async-start | bytes 262144 | tf_op jit(solution)/shard_map/all_to_all | solution.py:360
  89.0 0.7 copy-start.2
  92.5 19.0 %all-to-all-start.2 = ((bf16[128,8,128]{2,1,0:T(8,128)(2,1)}), bf16[128,8,128]{2,1,0:T(8,128)(2,1)S(1)}, u32[]{:S(2)}, u32[]{:S(2)}) async-start(bf16[128,8,128]{2,1,0:T(8,128)(2,1)} %solve.1), calls=%async_computation.2 | async-start | bytes 524288 | tf_op jit(solution)/shard_map/all_to_all | solution.py:369
Sparse Core Ops, SparseCore 0:
  32.1 51.5 all-gather.2

commit v3 on v2

--- a/solution.py
+++ b/solution.py
@@ -18,7 +18,7 @@
 WIDE = ("chip", "core")
 PIECES = 8
 CPP = NC // PIECES
-SCATTER_ORDER = (4, 5, 2, 3, 6, 7, 1)
+SCATTER_ORDER = (2, 4, 3, 5, 6, 7, 1)
 SUB = 16
 EXTRA = SUB + 8 + 8
 
@@ -222,6 +222,12 @@
                 h[m1 + 2 * m2 + 4 * m3] = r0
 
 
+def window_kernel(x, out):
+    for k in range(NP):
+        for j in range(2):
+            out[k, :, j * BS : (j + 1) * BS] = x[:, k * 2 + j, :].astype(F32).T.astype(BF)
+
+
 GC = 8
 
 
@@ -312,6 +318,7 @@
     ugath = lax.all_gather(piece, WIDE)
 
     near = lax.all_to_all(copies, ("chip", "narrow"), 0, 0).reshape(NW // 2, 4, EXTRA, BS)
+    near, others = lax.optimization_barrier((near, others))
     far = lax.ppermute(near, "core", [(0, 1), (1, 0)])
 
     lown, lpiv, tpart, delta, mpiv = pl.pallas_call(
@@ -383,7 +390,13 @@
         name="update",
     )(panel_order, mask, mpiv, blocks, ugath.reshape(NW, CPP * BS, BS), h, delta)
     front_out, xall = lax.optimization_barrier((front_out, xall))
-    window = xall.reshape(NW * 4, NP, 2, BS).transpose(1, 3, 2, 0).reshape(NP, BS, NRHS)
+    window = pl.pallas_call(
+        window_kernel,
+        out_shape=jax.ShapeDtypeStruct((NP, BS, NRHS), BF),
+        in_specs=vmem(1),
+        out_specs=vmem(1)[0],
+        name="window",
+    )(xall)
     return front_out.reshape(front.shape), frhs.reshape(rhs.shape), window
 
 

time: 120 us -> 113 us (0.942)
  blocking collectives: 21.1 us -> 0 us
  starting transfers between devices: 34.6 us -> 42.1 us
  waiting for transfers between devices: 12.3 us -> 16.6 us
  Pallas kernels: 33.9 us -> 36 us
    all_to_all x1 -> x0, blocking collectives: 21.1 us -> none  [body(): lax.all_to_all(copies, ('chip', 'narrow'), 0, 0)]
    all_to_all x0 -> x1, starting transfers between devices: none -> 10.3 us  [body(): lax.all_to_all(copies, ('chip', 'narrow'), 0, 0)]
    ppermute x1, starting transfers between devices: 4.15 us -> 0.53 us  [body(): far = lax.ppermute(near, 'core', [(0, 1), (1, 0)])]
    all_to_all x1, starting transfers between devices: 4.06 us -> 6.41 us  [body(): tparts = lax.all_to_all(tpart, WIDE, 0, 0)]
    ppermute x3, waiting for transfers between devices: 8.39 us -> 10.7 us  [body(): lax.ppermute(mine, 'narrow', [(i, (i + d) % 4) for i in range(4)])]
    pallas_call x0 -> x1, Pallas kernels: none -> 2.04 us  [body(): pl.pallas_call(window_kernel, out_shape=jax.ShapeDtypeStruct((NP, BS, NRH...]
    ppermute x1, waiting for transfers between devices: 0.01 us -> 1.54 us  [body(): far = lax.ppermute(near, 'core', [(0, 1), (1, 0)])]
    all_to_all x1, starting transfers between devices: 8.08 us -> 6.59 us  [body(): xall = lax.all_to_all(xg, ('narrow', *WIDE), 0, 0)]
  transfers between devices with their start and end apart: 14 -> 15, of which waited for: 6 -> 8; matrix products, arithmetic and copies ran while one was open for 0% -> 0% of each run, Pallas kernels for 24% -> 26%
where the time goes in v3:
time: 113 us; the launch traced here: 112 us
  starting transfers between devices  42.1 us (37%)
  Pallas kernels  36 us (32%)
  waiting for transfers between devices  16.6 us (15%)
  between operations  14.2 us (13%)
  local copies, waits for them, and re-layouts  2.82 us (2%)
    ppermute x7, starting transfers between devices, body(): lax.ppermute(sent[p], WIDE, [(i, holder(p, i)) for i in range(NP)])  14.8 us
    ppermute x3, waiting for transfers between devices, body(): lax.ppermute(mine, 'narrow', [(i, (i + d) % 4) for i in range(4)])  10.7 us
    all_to_all x1, starting transfers between devices, body(): lax.all_to_all(copies, ('chip', 'narrow'), 0, 0)  10.3 us
    pallas_call x1, Pallas kernels, body(): pl.pallas_call(update_kernel, out_shape=jax.ShapeDtypeStruct((NR, BS, NC,...  9.93 us
    all_to_all x1, starting transfers between devices, body(): xall = lax.all_to_all(xg, ('narrow', *WIDE), 0, 0)  6.59 us
    all_to_all x1, starting transfers between devices, body(): tparts = lax.all_to_all(tpart, WIDE, 0, 0)  6.41 us
    pallas_call x1, Pallas kernels, body(): pl.pallas_call(panel_kernel, out_shape=(jax.ShapeDtypeStruct((NR * BS, NP...  5.39 us
    pallas_call x1, Pallas kernels, body(): pl.pallas_call(combine_kernel, out_shape=jax.ShapeDtypeStruct((15, NR * B...  4.36 us
  transfers between devices with their start and end apart: 15, of which 8 were waited for; matrix products, arithmetic and copies ran while one was open for 0% of the time, Pallas kernels for 26%

profile of v3, /device:TPU:1, one launch (start us, length us, event | category | flops | bytes accessed | tf_op | source)
XLA Modules:
  0.0 111.8 jit_solution(5445584944366929590)
XLA Ops:
  7.2 0.0 all-gather.3.cloned.1.call-start
  7.2 2.7 %row.1 = (bf16[544,128]{1,0:T(8,128)(2,1)}, bf16[544,128]{1,0:T(8,128)(2,1)}, bf16[544,128]{1,0:T(8,128)(2,1)}, bf16[544,128]{1,0:T(8,128)(2,1)}, bf16[544,128]{...) custom-call(bf16[4,128,32,128]{3,2,1,0:T(8,128)(2,1)} %bitcast.12, ...), custom_call_target="tpu_custom_call" | custom-call | tf_op jit(solution)/shard_map/row/pallas_call | solution.py:284
  9.9 3.9 %collective-permute-start = (bf16[544,128]{1,0:T(8,128)(2,1)}, bf16[544,128]{1,0:T(8,128)(2,1)S(1)}, u32[]{:S(2)}, u32[]{:S(2)}) collective-permute-start(bf16[544,128]{1,0:T(8,128)(2,1)} %get-tuple-element.27), channel_id=1, source_target_pairs={{0,32},{4,36},{8,40},{12,44},{1,33},{5,37},{9,41},{13,45},{2,34},{... | collective-permute-start | bytes 417800 | tf_op jit(solution)/shard_map/ppermute | solution.py:295
  13.8 2.2 %collective-permute-start.1 = (bf16[544,128]{1,0:T(8,128)(2,1)}, bf16[544,128]{1,0:T(8,128)(2,1)S(1)}, u32[]{:S(2)}, u32[]{:S(2)}) collective-permute-start(bf16[544,128]{1,0:T(8,128)(2,1)} %get-tuple-element.28), channel_id=1, source_target_pairs={{0,64},{4,68},{8,72},{12,76},{1,65},{5,69},{9,73},{13,77},{2,66},{... | collective-permute-start | bytes 417800 | tf_op jit(solution)/shard_map/ppermute | solution.py:295
  16.0 2.6 %collective-permute-start.2 = (bf16[544,128]{1,0:T(8,128)(2,1)}, bf16[544,128]{1,0:T(8,128)(2,1)S(1)}, u32[]{:S(2)}, u32[]{:S(2)}) collective-permute-start(bf16[544,128]{1,0:T(8,128)(2,1)} %get-tuple-element.29), channel_id=1, source_target_pairs={{0,56},{4,60},{8,48},{12,52},{1,57},{5,61},{9,49},{13,53},{2,58},{... | collective-permute-start | bytes 417800 | tf_op jit(solution)/shard_map/ppermute | solution.py:295
  18.7 2.2 %collective-permute-start.3 = (bf16[544,128]{1,0:T(8,128)(2,1)}, bf16[544,128]{1,0:T(8,128)(2,1)S(1)}, u32[]{:S(2)}, u32[]{:S(2)}) collective-permute-start(bf16[544,128]{1,0:T(8,128)(2,1)} %get-tuple-element.30), channel_id=1, source_target_pairs={{0,88},{4,92},{8,80},{12,84},{1,89},{5,93},{9,81},{13,85},{2,90},{... | collective-permute-start | bytes 417800 | tf_op jit(solution)/shard_map/ppermute | solution.py:295
  20.9 1.3 %collective-permute-start.4 = (bf16[544,128]{1,0:T(8,128)(2,1)}, bf16[544,128]{1,0:T(8,128)(2,1)S(1)}, u32[]{:S(2)}, u32[]{:S(2)}) collective-permute-start(bf16[544,128]{1,0:T(8,128)(2,1)} %get-tuple-element.31), channel_id=1, source_target_pairs={{0,96},{4,100},{8,104},{12,108},{1,97},{5,101},{9,105},{13,109},{2... | collective-permute-start | bytes 417800 | tf_op jit(solution)/shard_map/ppermute | solution.py:295
  22.2 0.0 collective-permute-done.refs_1_
  22.2 1.3 %collective-permute-start.5 = (bf16[544,128]{1,0:T(8,128)(2,1)}, bf16[544,128]{1,0:T(8,128)(2,1)S(1)}, u32[]{:S(2)}, u32[]{:S(2)}) collective-permute-start(bf16[544,128]{1,0:T(8,128)(2,1)} %get-tuple-element.32), channel_id=1, source_target_pairs={{0,120},{4,124},{8,112},{12,116},{1,121},{5,125},{9,113},{13,117},... | collective-permute-start | bytes 417800 | tf_op jit(solution)/shard_map/ppermute | solution.py:295
  23.5 0.0 collective-permute-done.1.refs_2_
  23.5 1.3 %collective-permute-start.6 = (bf16[544,128]{1,0:T(8,128)(2,1)}, bf16[544,128]{1,0:T(8,128)(2,1)S(1)}, u32[]{:S(2)}, u32[]{:S(2)}) collective-permute-start(bf16[544,128]{1,0:T(8,128)(2,1)} %get-tuple-element.33), channel_id=1, source_target_pairs={{0,24},{4,28},{8,16},{12,20},{1,25},{5,29},{9,17},{13,21},{2,26},{... | collective-permute-start | bytes 417800 | tf_op jit(solution)/shard_map/ppermute | solution.py:295
  24.8 0.0 collective-permute-done.2.refs_3_
  24.8 0.9 collective-permute-done.3.refs_4_
  25.8 0.0 collective-permute-done.4.refs_5_
  25.8 2.0 %collective-permute-done.5.refs_6_ = bf16[544,128]{1,0:T(8,128)(2,1)S(1)} collective-permute-done((bf16[544,128]{1,0:T(8,128)(2,1)}, bf16[544,128]{1,0:T(8,128)(2,1)S(1)}, u32[]{:S(2)}, u32[]{:S(2)}) %collective-permute-start.5) | collective-permute-done | bytes 139296 | tf_op jit(solution)/shard_map/ppermute | solution.py:295
  27.8 0.0 collective-permute-done.6.refs_7_
  27.8 0.0 copy-done.5
  27.8 0.0 copy-done.6
  27.8 0.0 copy-done.7
  27.9 0.6 copy-done.9
  28.5 0.0 copy-done.10
  28.5 2.3 %merge.1 = (bf16[512,128]{1,0:T(8,128)(2,1)}, bf16[64,32,128]{2,1,0:T(8,128)(2,1)}) custom-call(bf16[544,128]{1,0:T(8,128)(2,1)} %get-tuple-element.26.refs_0_, bf16[544,128]{1,0:T(8,128)(2,1)} %copy-done.4, bf16[544,128]{1,0:T(8,128)(2,1)} %copy-done.5, bf16[544,128]{1,0:T(8,128)(2,1)} %copy-done.6, bf16[544,128]{1,0:T(8,128)(2,1)} %copy-done.7, ...), custom_call_target="tpu_custom_call" | custom-call | tf_op jit(solution)/shard_map/merge/pallas_call | solution.py:307
  30.8 0.0 all-gather.3.cloned.1.call-update
  30.8 10.3 %all-to-all-start = ((bf16[64,32,128]{2,1,0:T(8,128)(2,1)}), bf16[64,32,128]{2,1,0:T(8,128)(2,1)S(1)}, u32[]{:S(2)}, u32[]{:S(2)}) async-start(bf16[64,32,128]{2,1,0:T(8,128)(2,1)} %get-tuple-element.34), calls=%async_computation | async-start | bytes 1048576 | tf_op jit(solution)/shard_map/all_to_all | solution.py:320
  41.1 2.3 %own.1 = bf16[520,128]{1,0:T(8,128)(2,1)} custom-call(bf16[4,128,32,128]{3,2,1,0:T(8,128)(2,1)} %bitcast.13, s32[4,32]{1,0:T(4,128)} %bitcast.24), custom_call_target="tpu_custom_call" | custom-call | tf_op jit(solution)/shard_map/own/pallas_call | solution.py:297
  43.4 2.2 %collective-permute-start.9 = (bf16[520,128]{1,0:T(8,128)(2,1)}, bf16[520,128]{1,0:T(8,128)(2,1)S(1)}, u32[]{:S(2)}, u32[]{:S(2)}) collective-permute-start(bf16[520,128]{1,0:T(8,128)(2,1)} %own.1), channel_id=1, source_target_pairs={{0,3},{1,0},{2,1},{3,2},{4,7},{5,4},{6,5},{7,6},{8,11},{9,8},{10,9... | collective-permute-start | bytes 399368 | tf_op jit(solution)/shard_map/ppermute | solution.py:305
  45.6 0.6 collective-permute-start.8
  46.2 0.6 collective-permute-start.7
  46.8 5.8 %collective-permute-done.9.d3 = bf16[520,128]{1,0:T(8,128)(2,1)S(1)} collective-permute-done((bf16[520,128]{1,0:T(8,128)(2,1)}, bf16[520,128]{1,0:T(8,128)(2,1)S(1)}, u32[]{:S(2)}, u32[]{:S(2)}) %collective-permute-start.9) | collective-permute-done | bytes 133152 | tf_op jit(solution)/shard_map/ppermute | solution.py:305
  52.5 0.6 collective-permute-done.8.d2
  53.1 4.4 %collective-permute-done.7.d1 = bf16[520,128]{1,0:T(8,128)(2,1)S(1)} collective-permute-done((bf16[520,128]{1,0:T(8,128)(2,1)}, bf16[520,128]{1,0:T(8,128)(2,1)S(1)}, u32[]{:S(2)}, u32[]{:S(2)}) %collective-permute-start.7) | collective-permute-done | bytes 133152 | tf_op jit(solution)/shard_map/ppermute | solution.py:305
  57.5 0.0 all-to-all-done
  57.5 0.5 collective-permute-start.10
  58.0 1.5 %collective-permute-done.10.far = bf16[16,4,32,128]{3,2,1,0:T(8,128)(2,1)S(1)} collective-permute-done((bf16[16,4,32,128]{3,2,1,0:T(8,128)(2,1)S(1)}, bf16[16,4,32,128]{3,2,1,0:T(8,128)(2,1)S(1)}, u32[]{:S(2)}, u32[]{:S(2)}) %collective-permute-start.10) | collective-permute-done | bytes 524320 | tf_op jit(solution)/shard_map/ppermute | solution.py:322
  59.6 0.8 copy-done.1
  60.3 5.4 %panel.1 = (bf16[512,512]{1,0:T(8,128)(2,1)}, bf16[4,512,128]{2,1,0:T(8,128)(2,1)}, f32[32,8,128]{2,1,0:T(8,128)}, bf16[512,128]{1,0:T(8,128)(2,1)}, s32[4,128]{1,0:T(4,128)}) custom-call(s32[4]{0:T(128)} %order.9, bf16[520,128]{1,0:T(8,128)(2,1)} %own.1, bf16[520,128]{1,0:T(8,128)(2,1)} %copy-done.13, bf16[520,128]{1,0:T(8,128)(2,1)} %copy-done.12, ...), custom_call_target="tpu_custom_call" | custom-call | tf_op jit(solution)/shard_map/panel/pallas_call | solution.py:324
  65.7 6.4 %all-to-all-start.1 = ((f32[32,8,128]{2,1,0:T(8,128)}), f32[32,8,128]{2,1,0:T(8,128)S(1)}, u32[]{:S(2)}, u32[]{:S(2)}) async-start(f32[32,8,128]{2,1,0:T(8,128)} %get-tuple-element.44), calls=%async_computation.1 | async-start | bytes 262144 | tf_op jit(solution)/shard_map/all_to_all | solution.py:367
  72.2 4.4 %combine.1.h = bf16[15,512,128]{2,1,0:T(8,128)(2,1)} custom-call(s32[4]{0:T(128)} %order.9, bf16[512,512]{1,0:T(8,128)(2,1)} %get-tuple-element.41.lown, bf16[4,512,128]{2,1,0:T(8,128)(2,1)} %get-tuple-element.42.lpiv, bf16[4,128,128]{2,1,0:T(8,128)(2,1)} %w_ref.7), custom_call_target="tpu_custom_call" | custom-call | tf_op jit(solution)/shard_map/combine/pallas_call | solution.py:359
  76.5 4.3 %forward.1 = (f32[8,128]{1,0:T(8,128)}, bf16[4,128,256]{2,1,0:T(8,128)(2,1)}) custom-call(s32[4]{0:T(128)} %order.9, bf16[16,4,32,128]{3,2,1,0:T(8,128)(2,1)} %bitcast.17, bf16[16,4,32,128]{3,2,1,0:T(8,128)(2,1)} %copy-done.1, bf16[4,128,128]{2,1,0:T(8,128)(2,1)} %w_ref.7, bf16[4,128,256]{2,1,0:T(8,128)(2,1)} %bitcast.21, ...), custom_call_target="tpu_custom_call" | custom-call | tf_op jit(solution)/shard_map/forward/pallas_call | solution.py:344
  80.8 0.5 all-to-all-done.1.parts
  81.3 0.7 copy-done.3
  81.9 2.8 %solve.1 = bf16[128,8,128]{2,1,0:T(8,128)(2,1)} custom-call(s32[4]{0:T(128)} %order.9, f32[32,8,128]{2,1,0:T(8,128)} %copy-done.3, f32[8,128]{1,0:T(8,128)} %get-tuple-element.45.zt, bf16[4,512,128]{2,1,0:T(8,128)(2,1)} %get-tuple-element.42.lpiv, bf16[4,128,128]{2,1,0:T(8,128)(2,1)} %w_ref.7, bf16[15,512,128]{2,1,0:T(8,128)(2,1)} %combine.1.h), custom_call_target="tpu_custom_call" | custom-call | tf_op jit(solution)/shard_map/solve/pallas_call | solution.py:368
  84.7 6.6 %all-to-all-start.2 = ((bf16[128,8,128]{2,1,0:T(8,128)(2,1)}), bf16[128,8,128]{2,1,0:T(8,128)(2,1)S(1)}, u32[]{:S(2)}, u32[]{:S(2)}) async-start(bf16[128,8,128]{2,1,0:T(8,128)(2,1)} %solve.1), calls=%async_computation.2 | async-start | bytes 524288 | tf_op jit(solution)/shard_map/all_to_all | solution.py:376
  91.3 0.0 all-gather.3.cloned.1.call-done
  91.4 9.9 %update.1 = bf16[4,128,32,128]{3,2,1,0:T(8,128)(2,1)} custom-call(s32[4]{0:T(128)} %order.9, s32[4,32]{1,0:T(4,128)} %bitcast.25, s32[4,128]{1,0:T(4,128)} %get-tuple-element.39.mpiv, bf16[4,128,32,128]{3,2,1,0:T(8,128)(2,1)} %bitcast.14, bf16[32,512,128]{2,1,0:T(8,128)(2,1)} %bitcast.18, bf16[15,512,128]{2,1,0:T(8,128)(2,1)} %combine.1.h, ...), custom_call_target="tpu_custom_call" | custom-call | tf_op jit(solution)/shard_map/update/pallas_call | solution.py:378
  101.3 0.9 all-to-all-done.2.x
  102.2 0.7 copy-done.2
  102.9 2.0 %window.1 = bf16[4,128,256]{2,1,0:T(8,128)(2,1)} custom-call(bf16[128,8,128]{2,1,0:T(8,128)(2,1)} %copy-done.2), custom_call_target="tpu_custom_call" | custom-call | tf_op jit(solution)/shard_map/window/pallas_call | solution.py:393
  (20 shorter events, 0.0 us)
Async XLA Ops:
  7.2 84.2 %all-gather.3.cloned.1.call-start = ((), (), s32[]{:S(2)}) async-start(), calls=%async_computation.3 | async-start | bytes 4325376 | tf_op jit(solution)/shard_map/all_gather | solution.py:318
  9.9 12.3 %collective-permute-start = (bf16[544,128]{1,0:T(8,128)(2,1)}, bf16[544,128]{1,0:T(8,128)(2,1)S(1)}, u32[]{:S(2)}, u32[]{:S(2)}) collective-permute-start(bf16[544,128]{1,0:T(8,128)(2,1)} %get-tuple-element.27), channel_id=1, source_target_pairs={{0,32},{4,36},{8,40},{12,44},{1,33},{5,37},{9,41},{13,45},{2,34},{... | collective-permute-start | bytes 417800 | tf_op jit(solution)/shard_map/ppermute | solution.py:295
  13.8 9.7 %collective-permute-start.1 = (bf16[544,128]{1,0:T(8,128)(2,1)}, bf16[544,128]{1,0:T(8,128)(2,1)S(1)}, u32[]{:S(2)}, u32[]{:S(2)}) collective-permute-start(bf16[544,128]{1,0:T(8,128)(2,1)} %get-tuple-element.28), channel_id=1, source_target_pairs={{0,64},{4,68},{8,72},{12,76},{1,65},{5,69},{9,73},{13,77},{2,66},{... | collective-permute-start | bytes 417800 | tf_op jit(solution)/shard_map/ppermute | solution.py:295
  16.0 8.8 %collective-permute-start.2 = (bf16[544,128]{1,0:T(8,128)(2,1)}, bf16[544,128]{1,0:T(8,128)(2,1)S(1)}, u32[]{:S(2)}, u32[]{:S(2)}) collective-permute-start(bf16[544,128]{1,0:T(8,128)(2,1)} %get-tuple-element.29), channel_id=1, source_target_pairs={{0,56},{4,60},{8,48},{12,52},{1,57},{5,61},{9,49},{13,53},{2,58},{... | collective-permute-start | bytes 417800 | tf_op jit(solution)/shard_map/ppermute | solution.py:295
  18.7 7.1 %collective-permute-start.3 = (bf16[544,128]{1,0:T(8,128)(2,1)}, bf16[544,128]{1,0:T(8,128)(2,1)S(1)}, u32[]{:S(2)}, u32[]{:S(2)}) collective-permute-start(bf16[544,128]{1,0:T(8,128)(2,1)} %get-tuple-element.30), channel_id=1, source_target_pairs={{0,88},{4,92},{8,80},{12,84},{1,89},{5,93},{9,81},{13,85},{2,90},{... | collective-permute-start | bytes 417800 | tf_op jit(solution)/shard_map/ppermute | solution.py:295
  20.9 4.9 %collective-permute-start.4 = (bf16[544,128]{1,0:T(8,128)(2,1)}, bf16[544,128]{1,0:T(8,128)(2,1)S(1)}, u32[]{:S(2)}, u32[]{:S(2)}) collective-permute-start(bf16[544,128]{1,0:T(8,128)(2,1)} %get-tuple-element.31), channel_id=1, source_target_pairs={{0,96},{4,100},{8,104},{12,108},{1,97},{5,101},{9,105},{13,109},{2... | collective-permute-start | bytes 417800 | tf_op jit(solution)/shard_map/ppermute | solution.py:295
  22.2 5.6 %copy-start.4 = (bf16[544,128]{1,0:T(8,128)(2,1)}, bf16[544,128]{1,0:T(8,128)(2,1)S(1)}, u32[]{:S(2)}) copy-start(bf16[544,128]{1,0:T(8,128)(2,1)S(1)} %collective-permute-done.refs_1_) | copy-start | bytes 417796
  22.2 5.6 %collective-permute-start.5 = (bf16[544,128]{1,0:T(8,128)(2,1)}, bf16[544,128]{1,0:T(8,128)(2,1)S(1)}, u32[]{:S(2)}, u32[]{:S(2)}) collective-permute-start(bf16[544,128]{1,0:T(8,128)(2,1)} %get-tuple-element.32), channel_id=1, source_target_pairs={{0,120},{4,124},{8,112},{12,116},{1,121},{5,125},{9,113},{13,117},... | collective-permute-start | bytes 417800 | tf_op jit(solution)/shard_map/ppermute | solution.py:295
  23.5 4.3 %copy-start.5 = (bf16[544,128]{1,0:T(8,128)(2,1)}, bf16[544,128]{1,0:T(8,128)(2,1)S(1)}, u32[]{:S(2)}) copy-start(bf16[544,128]{1,0:T(8,128)(2,1)S(1)} %collective-permute-done.1.refs_2_) | copy-start | bytes 417796
  23.5 4.3 %collective-permute-start.6 = (bf16[544,128]{1,0:T(8,128)(2,1)}, bf16[544,128]{1,0:T(8,128)(2,1)S(1)}, u32[]{:S(2)}, u32[]{:S(2)}) collective-permute-start(bf16[544,128]{1,0:T(8,128)(2,1)} %get-tuple-element.33), channel_id=1, source_target_pairs={{0,24},{4,28},{8,16},{12,20},{1,25},{5,29},{9,17},{13,21},{2,26},{... | collective-permute-start | bytes 417800 | tf_op jit(solution)/shard_map/ppermute | solution.py:295
  24.8 3.0 %copy-start.6 = (bf16[544,128]{1,0:T(8,128)(2,1)}, bf16[544,128]{1,0:T(8,128)(2,1)S(1)}, u32[]{:S(2)}) copy-start(bf16[544,128]{1,0:T(8,128)(2,1)S(1)} %collective-permute-done.2.refs_3_) | copy-start | bytes 417796
  25.8 2.0 %copy-start.7 = (bf16[544,128]{1,0:T(8,128)(2,1)}, bf16[544,128]{1,0:T(8,128)(2,1)S(1)}, u32[]{:S(2)}) copy-start(bf16[544,128]{1,0:T(8,128)(2,1)S(1)} %collective-permute-done.3.refs_4_) | copy-start | bytes 417796
  25.8 2.1 %copy-start.8 = (bf16[544,128]{1,0:T(8,128)(2,1)}, bf16[544,128]{1,0:T(8,128)(2,1)S(1)}, u32[]{:S(2)}) copy-start(bf16[544,128]{1,0:T(8,128)(2,1)S(1)} %collective-permute-done.4.refs_5_) | copy-start | bytes 417796
  27.8 0.7 copy-start.9
  27.8 0.7 copy-start.10
  30.8 26.7 %all-to-all-start = ((bf16[64,32,128]{2,1,0:T(8,128)(2,1)}), bf16[64,32,128]{2,1,0:T(8,128)(2,1)S(1)}, u32[]{:S(2)}, u32[]{:S(2)}) async-start(bf16[64,32,128]{2,1,0:T(8,128)(2,1)} %get-tuple-element.34), calls=%async_computation | async-start | bytes 1048576 | tf_op jit(solution)/shard_map/all_to_all | solution.py:320
  43.4 9.1 %collective-permute-start.9 = (bf16[520,128]{1,0:T(8,128)(2,1)}, bf16[520,128]{1,0:T(8,128)(2,1)S(1)}, u32[]{:S(2)}, u32[]{:S(2)}) collective-permute-start(bf16[520,128]{1,0:T(8,128)(2,1)} %own.1), channel_id=1, source_target_pairs={{0,3},{1,0},{2,1},{3,2},{4,7},{5,4},{6,5},{7,6},{8,11},{9,8},{10,9... | collective-permute-start | bytes 399368 | tf_op jit(solution)/shard_map/ppermute | solution.py:305
  45.6 7.5 %collective-permute-start.8 = (bf16[520,128]{1,0:T(8,128)(2,1)}, bf16[520,128]{1,0:T(8,128)(2,1)S(1)}, u32[]{:S(2)}, u32[]{:S(2)}) collective-permute-start(bf16[520,128]{1,0:T(8,128)(2,1)} %own.1), channel_id=1, source_target_pairs={{0,2},{1,3},{2,0},{3,1},{4,6},{5,7},{6,4},{7,5},{8,10},{9,11},{10,... | collective-permute-start | bytes 399368 | tf_op jit(solution)/shard_map/ppermute | solution.py:305
  46.2 11.3 %collective-permute-start.7 = (bf16[520,128]{1,0:T(8,128)(2,1)}, bf16[520,128]{1,0:T(8,128)(2,1)S(1)}, u32[]{:S(2)}, u32[]{:S(2)}) collective-permute-start(bf16[520,128]{1,0:T(8,128)(2,1)} %own.1), channel_id=1, source_target_pairs={{0,1},{1,2},{2,3},{3,0},{4,5},{5,6},{6,7},{7,4},{8,9},{9,10},{10,1... | collective-permute-start | bytes 399368 | tf_op jit(solution)/shard_map/ppermute | solution.py:305
  52.5 7.0 %copy-start.11 = (bf16[520,128]{1,0:T(8,128)(2,1)}, bf16[520,128]{1,0:T(8,128)(2,1)S(1)}, u32[]{:S(2)}) copy-start(bf16[520,128]{1,0:T(8,128)(2,1)S(1)} %collective-permute-done.9.d3) | copy-start | bytes 399364
  53.1 6.4 %copy-start.12 = (bf16[520,128]{1,0:T(8,128)(2,1)}, bf16[520,128]{1,0:T(8,128)(2,1)S(1)}, u32[]{:S(2)}) copy-start(bf16[520,128]{1,0:T(8,128)(2,1)S(1)} %collective-permute-done.8.d2) | copy-start | bytes 399364
  57.5 2.1 %copy-start.13 = (bf16[520,128]{1,0:T(8,128)(2,1)}, bf16[520,128]{1,0:T(8,128)(2,1)S(1)}, u32[]{:S(2)}) copy-start(bf16[520,128]{1,0:T(8,128)(2,1)S(1)} %collective-permute-done.7.d1) | copy-start | bytes 399364
  57.5 2.1 %copy-start = (bf16[64,32,128]{2,1,0:T(8,128)(2,1)}, bf16[64,32,128]{2,1,0:T(8,128)(2,1)S(1)}, u32[]{:S(2)}) copy-start(bf16[64,32,128]{2,1,0:T(8,128)(2,1)S(1)} %all-to-all-done) | copy-start | bytes 1572868
  57.5 2.1 %collective-permute-start.10 = (bf16[16,4,32,128]{3,2,1,0:T(8,128)(2,1)S(1)}, bf16[16,4,32,128]{3,2,1,0:T(8,128)(2,1)S(1)}, u32[]{:S(2)}, u32[]{:S(2)}) collective-permute-start(bf16[16,4,32,128]{3,2,1,0:T(8,128)(2,1)S(1)} %bitcast.15), channel_id=1, source_target_pairs={{0,4},{4,0},{1,5},{5,1},{2,6},{6,2},{3,7},{7,3},{8,12},{12,8},{9,1... | collective-permute-start | bytes 1572872 | tf_op jit(solution)/shard_map/ppermute | solution.py:322
  59.5 0.8 copy-start.1
  65.7 15.5 %all-to-all-start.1 = ((f32[32,8,128]{2,1,0:T(8,128)}), f32[32,8,128]{2,1,0:T(8,128)S(1)}, u32[]{:S(2)}, u32[]{:S(2)}) async-start(f32[32,8,128]{2,1,0:T(8,128)} %get-tuple-element.44), calls=%async_computation.1 | async-start | bytes 262144 | tf_op jit(solution)/shard_map/all_to_all | solution.py:367
  81.3 0.7 copy-start.3
  84.7 17.5 %all-to-all-start.2 = ((bf16[128,8,128]{2,1,0:T(8,128)(2,1)}), bf16[128,8,128]{2,1,0:T(8,128)(2,1)S(1)}, u32[]{:S(2)}, u32[]{:S(2)}) async-start(bf16[128,8,128]{2,1,0:T(8,128)(2,1)} %solve.1), calls=%async_computation.2 | async-start | bytes 524288 | tf_op jit(solution)/shard_map/all_to_all | solution.py:376
  102.2 0.7 copy-start.2
Sparse Core Ops, SparseCore 0:
  30.9 53.2 all-gather.2

commit v4 on v2

--- a/solution.py
+++ b/solution.py
@@ -18,7 +18,7 @@
 WIDE = ("chip", "core")
 PIECES = 8
 CPP = NC // PIECES
-SCATTER_ORDER = (4, 5, 2, 3, 6, 7, 1)
+SCATTER_ORDER = (2, 4, 3, 5, 6, 7, 1)
 SUB = 16
 EXTRA = SUB + 8 + 8
 
@@ -46,8 +46,9 @@
     return jnp.where(fn(r) == c, 1.0, 0.0).astype(BF)
 
 
-def row_kernel(row_ref, b_ref, mask_ref, *sent):
+def prep_kernel(row_ref, col_ref, b_ref, mask_ref, *outs):
     q = lax.axis_index("narrow")
+    sent, mine = outs[:PIECES], outs[PIECES]
     gather = one_hot(BS, lambda r: (r % SUB) * 8 + r // SUB)
     for ct in range(NC // 8):
         for ag in range(BS // SUB):
@@ -68,15 +69,12 @@
         rows = jnp.where((q & 1) != 0, rows[:, BS:], rows[:, :BS])
         sent[p][CPP * BS + SUB : CPP * BS + SUB + 8] = rows.astype(BF)
         sent[p][CPP * BS + SUB + 8 :] = line
-
-
-def column_kernel(col_ref, mask_ref, mine):
     pick = one_hot(SUB, lambda r: r * 8)
     for r in range(NR):
         for ag in range(BS // SUB):
             native = col_ref[r, ag * SUB : (ag + 1) * SUB].astype(F32).reshape(BS, BS).astype(BF)
             mine[r * BS + ag * SUB : r * BS + (ag + 1) * SUB] = dot(pick, native).astype(BF)
-    first = jnp.broadcast_to(mask_ref[...].astype(F32)[:, 0:1], (NR, BS))
+    first = jnp.broadcast_to(mask[:, 0:1], (NR, BS))
     mine[NR * BS :] = jnp.concatenate([first, jnp.zeros((8 - NR, BS), F32)], axis=0).astype(BF)
 
 
@@ -275,27 +273,20 @@
     y = trail_sol.reshape(NR, BS, NRHS)
 
     fixed = lambda shape: pl.BlockSpec(shape, lambda g: (0,) * len(shape))
-    sent = pl.pallas_call(
-        row_kernel,
-        out_shape=(jax.ShapeDtypeStruct((CPP * BS + EXTRA, BS), BF),) * PIECES,
+    shapes = [(CPP * BS + EXTRA, BS)] * PIECES + [(NR * BS + 8, BS)]
+    *sent, mine = pl.pallas_call(
+        prep_kernel,
+        out_shape=tuple(jax.ShapeDtypeStruct(shape, BF) for shape in shapes),
         grid=(1,),
-        in_specs=[fixed((1, BS, NC, BS)), fixed((1, BS, NRHS)), fixed((NR, NC))],
-        out_specs=(fixed((CPP * BS + EXTRA, BS)),) * PIECES,
-        name="row",
-    )(blocks, b, mask)
+        in_specs=[fixed((1, BS, NC, BS)), fixed((NR, BS, 8, BS)), fixed((1, BS, NRHS)), fixed((NR, NC))],
+        out_specs=tuple(fixed(shape) for shape in shapes),
+        name="prep",
+    )(blocks, blocks, b, mask)
 
     pieces = []
     for p in SCATTER_ORDER:
         pieces.append(lax.ppermute(sent[p], WIDE, [(i, holder(p, i)) for i in range(NP)]))
 
-    mine = pl.pallas_call(
-        column_kernel,
-        out_shape=jax.ShapeDtypeStruct((NR * BS + 8, BS), BF),
-        grid=(1,),
-        in_specs=[fixed((NR, BS, 8, BS)), fixed((NR, NC))],
-        out_specs=fixed((NR * BS + 8, BS)),
-        name="own",
-    )(blocks, mask)
     others = [lax.ppermute(mine, "narrow", [(i, (i + d) % 4) for i in range(4)]) for d in (1, 2, 3)]
 
     piece, copies = pl.pallas_call(

time: 120 us -> 117 us (0.975)
  Pallas kernels: 33.9 us -> 31.9 us
  starting transfers between devices: 34.6 us -> 33.3 us
    pallas_call x2 -> x1, Pallas kernels: 4.95 us -> 3.03 us  [body(): pl.pallas_call(prep_kernel, out_shape=tuple((jax.ShapeDtypeStruct(shape,...]
    ppermute x7, starting transfers between devices: 16.1 us -> 14.8 us  [body(): lax.ppermute(sent[p], WIDE, [(i, holder(p, i)) for i in range(NP)])]
  transfers between devices with their start and end apart: 14 -> 14, of which waited for: 6 -> 6; matrix products, arithmetic and copies ran while one was open for 0% -> 0% of each run, Pallas kernels for 24% -> 23%
where the time goes in v4:
time: 117 us; the launch traced here: 116 us
  starting transfers between devices  33.3 us (28%)
  Pallas kernels  31.9 us (27%)
  blocking collectives  21.1 us (18%)
  between operations  14.2 us (12%)
  waiting for transfers between devices  12.5 us (11%)
  local copies, waits for them, and re-layouts  3.41 us (3%)
    all_to_all x1, blocking collectives, body(): lax.all_to_all(copies, ('chip', 'narrow'), 0, 0)  21.1 us
    ppermute x7, starting transfers between devices, body(): lax.ppermute(sent[p], WIDE, [(i, holder(p, i)) for i in range(NP)])  14.8 us
    pallas_call x1, Pallas kernels, body(): pl.pallas_call(update_kernel, out_shape=jax.ShapeDtypeStruct((NR, BS, NC,...  9.93 us
    ppermute x3, waiting for transfers between devices, body(): lax.ppermute(mine, 'narrow', [(i, (i + d) % 4) for i in range(4)])  8.53 us
    all_to_all x1, starting transfers between devices, body(): xall = lax.all_to_all(xg, ('narrow', *WIDE), 0, 0)  8.11 us
    pallas_call x1, Pallas kernels, body(): pl.pallas_call(panel_kernel, out_shape=(jax.ShapeDtypeStruct((NR * BS, NP...  5.38 us
    pallas_call x1, Pallas kernels, body(): pl.pallas_call(combine_kernel, out_shape=jax.ShapeDtypeStruct((15, NR * B...  4.27 us
    pallas_call x1, Pallas kernels, body(): pl.pallas_call(forward_kernel, out_shape=(jax.ShapeDtypeStruct((8, BS), F...  4.25 us
  transfers between devices with their start and end apart: 14, of which 6 were waited for; matrix products, arithmetic and copies ran while one was open for 0% of the time, Pallas kernels for 23%

profile of v4, /device:TPU:1, one launch (start us, length us, event | category | flops | bytes accessed | tf_op | source)
XLA Modules:
  0.0 116.4 jit_solution(7263777510524613927)
XLA Ops:
  7.2 0.0 all-gather.3.cloned.1.call-start
  7.2 3.0 %prep.1 = (bf16[544,128]{1,0:T(8,128)(2,1)}, bf16[544,128]{1,0:T(8,128)(2,1)}, bf16[544,128]{1,0:T(8,128)(2,1)}, bf16[544,128]{1,0:T(8,128)(2,1)}, bf16[544,128]...) custom-call(bf16[4,128,32,128]{3,2,1,0:T(8,128)(2,1)} %bitcast.15, ...), custom_call_target="tpu_custom_call" | custom-call | tf_op jit(solution)/shard_map/prep/pallas_call | solution.py:277
  10.2 3.9 %collective-permute-start.3 = (bf16[544,128]{1,0:T(8,128)(2,1)}, bf16[544,128]{1,0:T(8,128)(2,1)S(1)}, u32[]{:S(2)}, u32[]{:S(2)}) collective-permute-start(bf16[544,128]{1,0:T(8,128)(2,1)} %get-tuple-element.25), channel_id=1, source_target_pairs={{0,32},{4,36},{8,40},{12,44},{1,33},{5,37},{9,41},{13,45},{2,34},{... | collective-permute-start | bytes 417800 | tf_op jit(solution)/shard_map/ppermute | solution.py:288
  14.2 2.2 %collective-permute-start.4 = (bf16[544,128]{1,0:T(8,128)(2,1)}, bf16[544,128]{1,0:T(8,128)(2,1)S(1)}, u32[]{:S(2)}, u32[]{:S(2)}) collective-permute-start(bf16[544,128]{1,0:T(8,128)(2,1)} %get-tuple-element.26), channel_id=1, source_target_pairs={{0,64},{4,68},{8,72},{12,76},{1,65},{5,69},{9,73},{13,77},{2,66},{... | collective-permute-start | bytes 417800 | tf_op jit(solution)/shard_map/ppermute | solution.py:288
  16.4 2.6 %collective-permute-start.5 = (bf16[544,128]{1,0:T(8,128)(2,1)}, bf16[544,128]{1,0:T(8,128)(2,1)S(1)}, u32[]{:S(2)}, u32[]{:S(2)}) collective-permute-start(bf16[544,128]{1,0:T(8,128)(2,1)} %get-tuple-element.27), channel_id=1, source_target_pairs={{0,56},{4,60},{8,48},{12,52},{1,57},{5,61},{9,49},{13,53},{2,58},{... | collective-permute-start | bytes 417800 | tf_op jit(solution)/shard_map/ppermute | solution.py:288
  19.0 2.2 %collective-permute-start.6 = (bf16[544,128]{1,0:T(8,128)(2,1)}, bf16[544,128]{1,0:T(8,128)(2,1)S(1)}, u32[]{:S(2)}, u32[]{:S(2)}) collective-permute-start(bf16[544,128]{1,0:T(8,128)(2,1)} %get-tuple-element.28), channel_id=1, source_target_pairs={{0,88},{4,92},{8,80},{12,84},{1,89},{5,93},{9,81},{13,85},{2,90},{... | collective-permute-start | bytes 417800 | tf_op jit(solution)/shard_map/ppermute | solution.py:288
  21.2 1.3 %collective-permute-start.7 = (bf16[544,128]{1,0:T(8,128)(2,1)}, bf16[544,128]{1,0:T(8,128)(2,1)S(1)}, u32[]{:S(2)}, u32[]{:S(2)}) collective-permute-start(bf16[544,128]{1,0:T(8,128)(2,1)} %get-tuple-element.29), channel_id=1, source_target_pairs={{0,96},{4,100},{8,104},{12,108},{1,97},{5,101},{9,105},{13,109},{2... | collective-permute-start | bytes 417800 | tf_op jit(solution)/shard_map/ppermute | solution.py:288
  22.5 0.0 collective-permute-done.3.refs_1_
  22.5 0.0 copy-start.3
  22.5 1.3 %collective-permute-start.8 = (bf16[544,128]{1,0:T(8,128)(2,1)}, bf16[544,128]{1,0:T(8,128)(2,1)S(1)}, u32[]{:S(2)}, u32[]{:S(2)}) collective-permute-start(bf16[544,128]{1,0:T(8,128)(2,1)} %get-tuple-element.30), channel_id=1, source_target_pairs={{0,120},{4,124},{8,112},{12,116},{1,121},{5,125},{9,113},{13,117},... | collective-permute-start | bytes 417800 | tf_op jit(solution)/shard_map/ppermute | solution.py:288
  23.8 0.0 collective-permute-done.4.refs_2_
  23.9 0.0 copy-start.4
  23.9 1.3 %collective-permute-start.9 = (bf16[544,128]{1,0:T(8,128)(2,1)}, bf16[544,128]{1,0:T(8,128)(2,1)S(1)}, u32[]{:S(2)}, u32[]{:S(2)}) collective-permute-start(bf16[544,128]{1,0:T(8,128)(2,1)} %get-tuple-element.31), channel_id=1, source_target_pairs={{0,24},{4,28},{8,16},{12,20},{1,25},{5,29},{9,17},{13,21},{2,26},{... | collective-permute-start | bytes 417800 | tf_op jit(solution)/shard_map/ppermute | solution.py:288
  25.2 0.0 collective-permute-done.5.refs_3_
  25.2 0.0 copy-start.5
  25.2 0.9 collective-permute-done.6.refs_4_
  26.1 0.0 collective-permute-done.7.refs_5_
  26.1 2.0 %collective-permute-done.8.refs_6_ = bf16[544,128]{1,0:T(8,128)(2,1)S(1)} collective-permute-done((bf16[544,128]{1,0:T(8,128)(2,1)}, bf16[544,128]{1,0:T(8,128)(2,1)S(1)}, u32[]{:S(2)}, u32[]{:S(2)}) %collective-permute-start.8) | collective-permute-done | bytes 139296 | tf_op jit(solution)/shard_map/ppermute | solution.py:288
  28.1 0.0 collective-permute-done.9.refs_7_
  28.2 0.0 copy-done.3
  28.2 0.6 copy-done.8
  28.8 0.1 copy-done.9
  28.8 2.3 %merge.1 = (bf16[512,128]{1,0:T(8,128)(2,1)}, bf16[64,32,128]{2,1,0:T(8,128)(2,1)}) custom-call(bf16[544,128]{1,0:T(8,128)(2,1)} %get-tuple-element.24.refs_0_, bf16[544,128]{1,0:T(8,128)(2,1)} %copy-done.3, bf16[544,128]{1,0:T(8,128)(2,1)} %copy-done.4, bf16[544,128]{1,0:T(8,128)(2,1)} %copy-done.5, bf16[544,128]{1,0:T(8,128)(2,1)} %copy-done.6, ...), custom_call_target="tpu_custom_call" | custom-call | tf_op jit(solution)/shard_map/merge/pallas_call | solution.py:292
  31.1 0.0 all-gather.3.cloned.1.call-update
  31.1 21.1 %all_to_all.15 = bf16[64,32,128]{2,1,0:T(8,128)(2,1)S(1)} all-to-all(bf16[64,32,128]{2,1,0:T(8,128)(2,1)} %get-tuple-element.32), channel_id=1, replica_groups=mesh['chip'=16,'core'=2,'narrow'=4] {'chip','narrow'}, dimensions={0} | all-to-all | bytes 1048576 | tf_op jit(solution)/shard_map/all_to_all | solution.py:305
  52.2 4.1 %collective-permute-start.10 = (bf16[16,4,32,128]{3,2,1,0:T(8,128)(2,1)S(1)}, bf16[16,4,32,128]{3,2,1,0:T(8,128)(2,1)S(1)}, u32[]{:S(2)}, u32[]{:S(2)}) collective-permute-start(bf16[16,4,32,128]{3,2,1,0:T(8,128)(2,1)S(1)} %bitcast.18), channel_id=1, source_target_pairs={{0,4},{4,0},{1,5},{5,1},{2,6},{6,2},{3,7},{7,3},{8,12},{12,8},{9,1... | collective-permute-start | bytes 1572872 | tf_op jit(solution)/shard_map/ppermute | solution.py:306
  56.4 0.7 collective-permute-start.2
  57.0 1.5 %collective-permute-start.1 = (bf16[520,128]{1,0:T(8,128)(2,1)}, bf16[520,128]{1,0:T(8,128)(2,1)S(1)}, u32[]{:S(2)}, u32[]{:S(2)}) collective-permute-start(bf16[520,128]{1,0:T(8,128)(2,1)} %get-tuple-element.23.own), channel_id=1, source_target_pairs={{0,2},{1,3},{2,0},{3,1},{4,6},{5,7},{6,4},{7,5},{8,10},{9,11},{10,... | collective-permute-start | bytes 399368 | tf_op jit(solution)/shard_map/ppermute | solution.py:290
  58.5 0.0 collective-permute-start
  58.5 3.1 %collective-permute-done.2.d3 = bf16[520,128]{1,0:T(8,128)(2,1)S(1)} collective-permute-done((bf16[520,128]{1,0:T(8,128)(2,1)}, bf16[520,128]{1,0:T(8,128)(2,1)S(1)}, u32[]{:S(2)}, u32[]{:S(2)}) %collective-permute-start.2) | collective-permute-done | bytes 133152 | tf_op jit(solution)/shard_map/ppermute | solution.py:290
  61.7 1.9 %collective-permute-done.1.d2 = bf16[520,128]{1,0:T(8,128)(2,1)S(1)} collective-permute-done((bf16[520,128]{1,0:T(8,128)(2,1)}, bf16[520,128]{1,0:T(8,128)(2,1)S(1)}, u32[]{:S(2)}, u32[]{:S(2)}) %collective-permute-start.1) | collective-permute-done | bytes 133152 | tf_op jit(solution)/shard_map/ppermute | solution.py:290
  63.6 3.5 %collective-permute-done.d1 = bf16[520,128]{1,0:T(8,128)(2,1)S(1)} collective-permute-done((bf16[520,128]{1,0:T(8,128)(2,1)}, bf16[520,128]{1,0:T(8,128)(2,1)S(1)}, u32[]{:S(2)}, u32[]{:S(2)}) %collective-permute-start) | collective-permute-done | bytes 133152 | tf_op jit(solution)/shard_map/ppermute | solution.py:290
  67.1 0.0 collective-permute-done.10.far
  67.1 0.6 copy-done.12
  67.7 0.2 copy-done.1
  67.9 5.4 %panel.1 = (bf16[512,512]{1,0:T(8,128)(2,1)}, bf16[4,512,128]{2,1,0:T(8,128)(2,1)}, f32[32,8,128]{2,1,0:T(8,128)}, bf16[512,128]{1,0:T(8,128)(2,1)}, s32[4,128]{1,0:T(4,128)}) custom-call(s32[4]{0:T(128)} %order.9, bf16[520,128]{1,0:T(8,128)(2,1)} %get-tuple-element.23.own, bf16[520,128]{1,0:T(8,128)(2,1)} %copy-done.12, bf16[520,128]{1,0:T(8,128)(2,1)} %copy-done.11, ...), custom_call_target="tpu_custom_call" | custom-call | tf_op jit(solution)/shard_map/panel/pallas_call | solution.py:308
  73.3 4.0 %all-to-all-start.1 = ((f32[32,8,128]{2,1,0:T(8,128)}), f32[32,8,128]{2,1,0:T(8,128)S(1)}, u32[]{:S(2)}, u32[]{:S(2)}) async-start(f32[32,8,128]{2,1,0:T(8,128)} %get-tuple-element.38), calls=%async_computation.1 | async-start | bytes 262144 | tf_op jit(solution)/shard_map/all_to_all | solution.py:351
  77.3 4.3 %combine.1.h = bf16[15,512,128]{2,1,0:T(8,128)(2,1)} custom-call(s32[4]{0:T(128)} %order.9, bf16[512,512]{1,0:T(8,128)(2,1)} %get-tuple-element.35.lown, bf16[4,512,128]{2,1,0:T(8,128)(2,1)} %get-tuple-element.36.lpiv, bf16[4,128,128]{2,1,0:T(8,128)(2,1)} %w_ref.7), custom_call_target="tpu_custom_call" | custom-call | tf_op jit(solution)/shard_map/combine/pallas_call | solution.py:343
  81.6 4.2 %forward.1 = (f32[8,128]{1,0:T(8,128)}, bf16[4,128,256]{2,1,0:T(8,128)(2,1)}) custom-call(s32[4]{0:T(128)} %order.9, bf16[16,4,32,128]{3,2,1,0:T(8,128)(2,1)} %bitcast.20, bf16[16,4,32,128]{3,2,1,0:T(8,128)(2,1)} %copy-done.1, bf16[4,128,128]{2,1,0:T(8,128)(2,1)} %w_ref.7, bf16[4,128,256]{2,1,0:T(8,128)(2,1)} %bitcast.25, ...), custom_call_target="tpu_custom_call" | custom-call | tf_op jit(solution)/shard_map/forward/pallas_call | solution.py:328
  85.8 0.0 all-to-all-done.1.parts
  85.8 0.7 copy-done.2
  86.5 2.8 %solve.1 = bf16[128,8,128]{2,1,0:T(8,128)(2,1)} custom-call(s32[4]{0:T(128)} %order.9, f32[32,8,128]{2,1,0:T(8,128)} %copy-done.2, f32[8,128]{1,0:T(8,128)} %get-tuple-element.39.zt, bf16[4,512,128]{2,1,0:T(8,128)(2,1)} %get-tuple-element.36.lpiv, bf16[4,128,128]{2,1,0:T(8,128)(2,1)} %w_ref.7, bf16[15,512,128]{2,1,0:T(8,128)(2,1)} %combine.1.h), custom_call_target="tpu_custom_call" | custom-call | tf_op jit(solution)/shard_map/solve/pallas_call | solution.py:352
  89.3 8.1 %all-to-all-start.2 = ((bf16[128,8,128]{2,1,0:T(8,128)(2,1)}), bf16[128,8,128]{2,1,0:T(8,128)(2,1)S(1)}, u32[]{:S(2)}, u32[]{:S(2)}) async-start(bf16[128,8,128]{2,1,0:T(8,128)(2,1)} %solve.1), calls=%async_computation.2 | async-start | bytes 524288 | tf_op jit(solution)/shard_map/all_to_all | solution.py:360
  97.4 0.0 all-gather.3.cloned.1.call-done
  97.4 9.9 %update.1 = bf16[4,128,32,128]{3,2,1,0:T(8,128)(2,1)} custom-call(s32[4]{0:T(128)} %order.9, s32[4,32]{1,0:T(4,128)} %bitcast.28, s32[4,128]{1,0:T(4,128)} %get-tuple-element.33.mpiv, bf16[4,128,32,128]{3,2,1,0:T(8,128)(2,1)} %bitcast.17, bf16[32,512,128]{2,1,0:T(8,128)(2,1)} %bitcast.21, bf16[15,512,128]{2,1,0:T(8,128)(2,1)} %combine.1.h, ...), custom_call_target="tpu_custom_call" | custom-call | tf_op jit(solution)/shard_map/update/pallas_call | solution.py:362
  107.4 0.9 all-to-all-done.2
  108.3 0.4 copy.9
  108.7 0.9 reshape.41
  (17 shorter events, 0.0 us)
Async XLA Ops:
  7.2 90.3 %all-gather.3.cloned.1.call-start = ((), (), s32[]{:S(2)}) async-start(), calls=%async_computation.3 | async-start | bytes 4325376 | tf_op jit(solution)/shard_map/all_gather | solution.py:303
  10.2 12.3 %collective-permute-start.3 = (bf16[544,128]{1,0:T(8,128)(2,1)}, bf16[544,128]{1,0:T(8,128)(2,1)S(1)}, u32[]{:S(2)}, u32[]{:S(2)}) collective-permute-start(bf16[544,128]{1,0:T(8,128)(2,1)} %get-tuple-element.25), channel_id=1, source_target_pairs={{0,32},{4,36},{8,40},{12,44},{1,33},{5,37},{9,41},{13,45},{2,34},{... | collective-permute-start | bytes 417800 | tf_op jit(solution)/shard_map/ppermute | solution.py:288
  14.2 9.7 %collective-permute-start.4 = (bf16[544,128]{1,0:T(8,128)(2,1)}, bf16[544,128]{1,0:T(8,128)(2,1)S(1)}, u32[]{:S(2)}, u32[]{:S(2)}) collective-permute-start(bf16[544,128]{1,0:T(8,128)(2,1)} %get-tuple-element.26), channel_id=1, source_target_pairs={{0,64},{4,68},{8,72},{12,76},{1,65},{5,69},{9,73},{13,77},{2,66},{... | collective-permute-start | bytes 417800 | tf_op jit(solution)/shard_map/ppermute | solution.py:288
  16.4 8.8 %collective-permute-start.5 = (bf16[544,128]{1,0:T(8,128)(2,1)}, bf16[544,128]{1,0:T(8,128)(2,1)S(1)}, u32[]{:S(2)}, u32[]{:S(2)}) collective-permute-start(bf16[544,128]{1,0:T(8,128)(2,1)} %get-tuple-element.27), channel_id=1, source_target_pairs={{0,56},{4,60},{8,48},{12,52},{1,57},{5,61},{9,49},{13,53},{2,58},{... | collective-permute-start | bytes 417800 | tf_op jit(solution)/shard_map/ppermute | solution.py:288
  19.0 7.1 %collective-permute-start.6 = (bf16[544,128]{1,0:T(8,128)(2,1)}, bf16[544,128]{1,0:T(8,128)(2,1)S(1)}, u32[]{:S(2)}, u32[]{:S(2)}) collective-permute-start(bf16[544,128]{1,0:T(8,128)(2,1)} %get-tuple-element.28), channel_id=1, source_target_pairs={{0,88},{4,92},{8,80},{12,84},{1,89},{5,93},{9,81},{13,85},{2,90},{... | collective-permute-start | bytes 417800 | tf_op jit(solution)/shard_map/ppermute | solution.py:288
  21.2 4.9 %collective-permute-start.7 = (bf16[544,128]{1,0:T(8,128)(2,1)}, bf16[544,128]{1,0:T(8,128)(2,1)S(1)}, u32[]{:S(2)}, u32[]{:S(2)}) collective-permute-start(bf16[544,128]{1,0:T(8,128)(2,1)} %get-tuple-element.29), channel_id=1, source_target_pairs={{0,96},{4,100},{8,104},{12,108},{1,97},{5,101},{9,105},{13,109},{2... | collective-permute-start | bytes 417800 | tf_op jit(solution)/shard_map/ppermute | solution.py:288
  22.5 5.6 %copy-start.3 = (bf16[544,128]{1,0:T(8,128)(2,1)}, bf16[544,128]{1,0:T(8,128)(2,1)S(1)}, u32[]{:S(2)}) copy-start(bf16[544,128]{1,0:T(8,128)(2,1)S(1)} %collective-permute-done.3.refs_1_) | copy-start | bytes 417796
  22.5 5.6 %collective-permute-start.8 = (bf16[544,128]{1,0:T(8,128)(2,1)}, bf16[544,128]{1,0:T(8,128)(2,1)S(1)}, u32[]{:S(2)}, u32[]{:S(2)}) collective-permute-start(bf16[544,128]{1,0:T(8,128)(2,1)} %get-tuple-element.30), channel_id=1, source_target_pairs={{0,120},{4,124},{8,112},{12,116},{1,121},{5,125},{9,113},{13,117},... | collective-permute-start | bytes 417800 | tf_op jit(solution)/shard_map/ppermute | solution.py:288
  23.9 4.3 %copy-start.4 = (bf16[544,128]{1,0:T(8,128)(2,1)}, bf16[544,128]{1,0:T(8,128)(2,1)S(1)}, u32[]{:S(2)}) copy-start(bf16[544,128]{1,0:T(8,128)(2,1)S(1)} %collective-permute-done.4.refs_2_) | copy-start | bytes 417796
  23.9 4.3 %collective-permute-start.9 = (bf16[544,128]{1,0:T(8,128)(2,1)}, bf16[544,128]{1,0:T(8,128)(2,1)S(1)}, u32[]{:S(2)}, u32[]{:S(2)}) collective-permute-start(bf16[544,128]{1,0:T(8,128)(2,1)} %get-tuple-element.31), channel_id=1, source_target_pairs={{0,24},{4,28},{8,16},{12,20},{1,25},{5,29},{9,17},{13,21},{2,26},{... | collective-permute-start | bytes 417800 | tf_op jit(solution)/shard_map/ppermute | solution.py:288
  25.2 3.0 %copy-start.5 = (bf16[544,128]{1,0:T(8,128)(2,1)}, bf16[544,128]{1,0:T(8,128)(2,1)S(1)}, u32[]{:S(2)}) copy-start(bf16[544,128]{1,0:T(8,128)(2,1)S(1)} %collective-permute-done.5.refs_3_) | copy-start | bytes 417796
  26.1 2.0 %copy-start.6 = (bf16[544,128]{1,0:T(8,128)(2,1)}, bf16[544,128]{1,0:T(8,128)(2,1)S(1)}, u32[]{:S(2)}) copy-start(bf16[544,128]{1,0:T(8,128)(2,1)S(1)} %collective-permute-done.6.refs_4_) | copy-start | bytes 417796
  26.1 2.1 %copy-start.7 = (bf16[544,128]{1,0:T(8,128)(2,1)}, bf16[544,128]{1,0:T(8,128)(2,1)S(1)}, u32[]{:S(2)}) copy-start(bf16[544,128]{1,0:T(8,128)(2,1)S(1)} %collective-permute-done.7.refs_5_) | copy-start | bytes 417796
  28.1 0.7 copy-start.8
  28.1 0.7 copy-start.9
  52.2 14.9 %copy-start = (bf16[64,32,128]{2,1,0:T(8,128)(2,1)}, bf16[64,32,128]{2,1,0:T(8,128)(2,1)S(1)}, u32[]{:S(2)}) copy-start(bf16[64,32,128]{2,1,0:T(8,128)(2,1)S(1)} %all_to_all.15) | copy-start | bytes 1572868
  52.2 14.9 %collective-permute-start.10 = (bf16[16,4,32,128]{3,2,1,0:T(8,128)(2,1)S(1)}, bf16[16,4,32,128]{3,2,1,0:T(8,128)(2,1)S(1)}, u32[]{:S(2)}, u32[]{:S(2)}) collective-permute-start(bf16[16,4,32,128]{3,2,1,0:T(8,128)(2,1)S(1)} %bitcast.18), channel_id=1, source_target_pairs={{0,4},{4,0},{1,5},{5,1},{2,6},{6,2},{3,7},{7,3},{8,12},{12,8},{9,1... | collective-permute-start | bytes 1572872 | tf_op jit(solution)/shard_map/ppermute | solution.py:306
  56.4 5.3 %collective-permute-start.2 = (bf16[520,128]{1,0:T(8,128)(2,1)}, bf16[520,128]{1,0:T(8,128)(2,1)S(1)}, u32[]{:S(2)}, u32[]{:S(2)}) collective-permute-start(bf16[520,128]{1,0:T(8,128)(2,1)} %get-tuple-element.23.own), channel_id=1, source_target_pairs={{0,3},{1,0},{2,1},{3,2},{4,7},{5,4},{6,5},{7,6},{8,11},{9,8},{10,9... | collective-permute-start | bytes 399368 | tf_op jit(solution)/shard_map/ppermute | solution.py:290
  57.0 6.5 %collective-permute-start.1 = (bf16[520,128]{1,0:T(8,128)(2,1)}, bf16[520,128]{1,0:T(8,128)(2,1)S(1)}, u32[]{:S(2)}, u32[]{:S(2)}) collective-permute-start(bf16[520,128]{1,0:T(8,128)(2,1)} %get-tuple-element.23.own), channel_id=1, source_target_pairs={{0,2},{1,3},{2,0},{3,1},{4,6},{5,7},{6,4},{7,5},{8,10},{9,11},{10,... | collective-permute-start | bytes 399368 | tf_op jit(solution)/shard_map/ppermute | solution.py:290
  58.5 8.5 %collective-permute-start = (bf16[520,128]{1,0:T(8,128)(2,1)}, bf16[520,128]{1,0:T(8,128)(2,1)S(1)}, u32[]{:S(2)}, u32[]{:S(2)}) collective-permute-start(bf16[520,128]{1,0:T(8,128)(2,1)} %get-tuple-element.23.own), channel_id=1, source_target_pairs={{0,1},{1,2},{2,3},{3,0},{4,5},{5,6},{6,7},{7,4},{8,9},{9,10},{10,1... | collective-permute-start | bytes 399368 | tf_op jit(solution)/shard_map/ppermute | solution.py:290
  61.7 5.4 %copy-start.10 = (bf16[520,128]{1,0:T(8,128)(2,1)}, bf16[520,128]{1,0:T(8,128)(2,1)S(1)}, u32[]{:S(2)}) copy-start(bf16[520,128]{1,0:T(8,128)(2,1)S(1)} %collective-permute-done.2.d3) | copy-start | bytes 399364
  63.6 3.5 %copy-start.11 = (bf16[520,128]{1,0:T(8,128)(2,1)}, bf16[520,128]{1,0:T(8,128)(2,1)S(1)}, u32[]{:S(2)}) copy-start(bf16[520,128]{1,0:T(8,128)(2,1)S(1)} %collective-permute-done.1.d2) | copy-start | bytes 399364
  67.1 0.7 copy-start.12
  67.1 0.8 copy-start.1
  73.3 12.5 %all-to-all-start.1 = ((f32[32,8,128]{2,1,0:T(8,128)}), f32[32,8,128]{2,1,0:T(8,128)S(1)}, u32[]{:S(2)}, u32[]{:S(2)}) async-start(f32[32,8,128]{2,1,0:T(8,128)} %get-tuple-element.38), calls=%async_computation.1 | async-start | bytes 262144 | tf_op jit(solution)/shard_map/all_to_all | solution.py:351
  85.8 0.7 copy-start.2
  89.3 19.0 %all-to-all-start.2 = ((bf16[128,8,128]{2,1,0:T(8,128)(2,1)}), bf16[128,8,128]{2,1,0:T(8,128)(2,1)S(1)}, u32[]{:S(2)}, u32[]{:S(2)}) async-start(bf16[128,8,128]{2,1,0:T(8,128)(2,1)} %solve.1), calls=%async_computation.2 | async-start | bytes 524288 | tf_op jit(solution)/shard_map/all_to_all | solution.py:360
Sparse Core Ops, SparseCore 0:
  31.2 51.5 all-gather.2

commit v5 on v4

--- a/solution.py
+++ b/solution.py
@@ -82,9 +82,10 @@
     parts, (piece, copies) = refs[:PIECES], refs[PIECES:]
     first = parts[0][...]
     is_source = lax.axis_index("chip") < 2
-    total = jnp.where(is_source, first, jnp.zeros_like(first))
-    for part in parts[1:]:
+    total = parts[1][...]
+    for part in parts[2:]:
         total = total + part[...]
+    total = jnp.where(is_source, first, total)
     piece[...] = total[: CPP * BS]
     for d in range(NW * 2):
         copies[d] = total[CPP * BS :]
@@ -285,7 +286,8 @@
 
     pieces = []
     for p in SCATTER_ORDER:
-        pieces.append(lax.ppermute(sent[p], WIDE, [(i, holder(p, i)) for i in range(NP)]))
+        pairs = [(i, holder(p, i)) for i in range(NP)]
+        pieces.append(lax.ppermute(sent[p], WIDE, pairs + [(b, a) for a, b in pairs]))
 
     others = [lax.ppermute(mine, "narrow", [(i, (i + d) % 4) for i in range(4)]) for d in (1, 2, 3)]
 

time: 117 us -> 121 us (1.034)
  waiting for transfers between devices: 12.5 us -> 19.2 us
  blocking collectives: 21.1 us -> 17.5 us
    ppermute x7, waiting for transfers between devices: 2.96 us -> 9.78 us  [body(): lax.ppermute(sent[p], WIDE, pairs + [(b, a) for a, b in pairs])]
    all_to_all x1, blocking collectives: 21.1 us -> 17.5 us  [body(): lax.all_to_all(copies, ('chip', 'narrow'), 0, 0)]
    ppermute x7, starting transfers between devices: 14.8 us -> 16.7 us  [body(): lax.ppermute(sent[p], WIDE, pairs + [(b, a) for a, b in pairs])]
    ppermute x1, starting transfers between devices: 4.14 us -> 2.64 us  [body(): far = lax.ppermute(near, 'core', [(0, 1), (1, 0)])]
  transfers between devices with their start and end apart: 14 -> 14, of which waited for: 6 -> 7; matrix products, arithmetic and copies ran while one was open for 0% -> 0% of each run, Pallas kernels for 23% -> 22%
where the time goes in v5:
time: 121 us; the launch traced here: 120 us
  starting transfers between devices  33.7 us (28%)
  Pallas kernels  32 us (26%)
  waiting for transfers between devices  19.2 us (16%)
  blocking collectives  17.5 us (14%)
  between operations  14.2 us (12%)
  local copies, waits for them, and re-layouts  3.38 us (3%)
    all_to_all x1, blocking collectives, body(): lax.all_to_all(copies, ('chip', 'narrow'), 0, 0)  17.5 us
    ppermute x7, starting transfers between devices, body(): lax.ppermute(sent[p], WIDE, pairs + [(b, a) for a, b in pairs])  16.7 us
    pallas_call x1, Pallas kernels, body(): pl.pallas_call(update_kernel, out_shape=jax.ShapeDtypeStruct((NR, BS, NC,...  9.93 us
    ppermute x7, waiting for transfers between devices, body(): lax.ppermute(sent[p], WIDE, pairs + [(b, a) for a, b in pairs])  9.78 us
    ppermute x3, waiting for transfers between devices, body(): lax.ppermute(mine, 'narrow', [(i, (i + d) % 4) for i in range(4)])  8.49 us
    all_to_all x1, starting transfers between devices, body(): xall = lax.all_to_all(xg, ('narrow', *WIDE), 0, 0)  8.08 us
    pallas_call x1, Pallas kernels, body(): pl.pallas_call(panel_kernel, out_shape=(jax.ShapeDtypeStruct((NR * BS, NP...  5.37 us
    pallas_call x1, Pallas kernels, body(): pl.pallas_call(combine_kernel, out_shape=jax.ShapeDtypeStruct((15, NR * B...  4.31 us
  transfers between devices with their start and end apart: 14, of which 7 were waited for; matrix products, arithmetic and copies ran while one was open for 0% of the time, Pallas kernels for 22%

profile of v5, /device:TPU:1, one launch (start us, length us, event | category | flops | bytes accessed | tf_op | source)
XLA Modules:
  0.0 120.0 jit_solution(14017509382867017236)
XLA Ops:
  7.2 0.0 all-gather.3.cloned.1.call-start
  7.2 3.0 %prep.1 = (bf16[544,128]{1,0:T(8,128)(2,1)}, bf16[544,128]{1,0:T(8,128)(2,1)}, bf16[544,128]{1,0:T(8,128)(2,1)}, bf16[544,128]{1,0:T(8,128)(2,1)}, bf16[544,128]...) custom-call(bf16[4,128,32,128]{3,2,1,0:T(8,128)(2,1)} %bitcast.15, ...), custom_call_target="tpu_custom_call" | custom-call | tf_op jit(solution)/shard_map/prep/pallas_call | solution.py:278
  10.2 3.9 %collective-permute-start.3 = (bf16[544,128]{1,0:T(8,128)(2,1)}, bf16[544,128]{1,0:T(8,128)(2,1)S(1)}, u32[]{:S(2)}, u32[]{:S(2)}) collective-permute-start(bf16[544,128]{1,0:T(8,128)(2,1)} %get-tuple-element.25), channel_id=1, source_target_pairs={{0,32},{4,36},{8,40},{12,44},{32,0},{36,4},{40,8},{44,12},{1,33},{... | collective-permute-start | bytes 417800 | tf_op jit(solution)/shard_map/ppermute | solution.py:290
  14.2 2.2 %collective-permute-start.4 = (bf16[544,128]{1,0:T(8,128)(2,1)}, bf16[544,128]{1,0:T(8,128)(2,1)S(1)}, u32[]{:S(2)}, u32[]{:S(2)}) collective-permute-start(bf16[544,128]{1,0:T(8,128)(2,1)} %get-tuple-element.26), channel_id=1, source_target_pairs={{0,64},{4,68},{8,72},{12,76},{64,0},{68,4},{72,8},{76,12},{1,65},{... | collective-permute-start | bytes 417800 | tf_op jit(solution)/shard_map/ppermute | solution.py:290
  16.4 2.6 %collective-permute-start.5 = (bf16[544,128]{1,0:T(8,128)(2,1)}, bf16[544,128]{1,0:T(8,128)(2,1)S(1)}, u32[]{:S(2)}, u32[]{:S(2)}) collective-permute-start(bf16[544,128]{1,0:T(8,128)(2,1)} %get-tuple-element.27), channel_id=1, source_target_pairs={{0,56},{4,60},{8,48},{12,52},{56,0},{60,4},{48,8},{52,12},{1,57},{... | collective-permute-start | bytes 417800 | tf_op jit(solution)/shard_map/ppermute | solution.py:290
  19.0 2.2 %collective-permute-start.6 = (bf16[544,128]{1,0:T(8,128)(2,1)}, bf16[544,128]{1,0:T(8,128)(2,1)S(1)}, u32[]{:S(2)}, u32[]{:S(2)}) collective-permute-start(bf16[544,128]{1,0:T(8,128)(2,1)} %get-tuple-element.28), channel_id=1, source_target_pairs={{0,88},{4,92},{8,80},{12,84},{88,0},{92,4},{80,8},{84,12},{1,89},{... | collective-permute-start | bytes 417800 | tf_op jit(solution)/shard_map/ppermute | solution.py:290
  21.2 1.9 %collective-permute-start.7 = (bf16[544,128]{1,0:T(8,128)(2,1)}, bf16[544,128]{1,0:T(8,128)(2,1)S(1)}, u32[]{:S(2)}, u32[]{:S(2)}) collective-permute-start(bf16[544,128]{1,0:T(8,128)(2,1)} %get-tuple-element.29), channel_id=1, source_target_pairs={{0,96},{4,100},{8,104},{12,108},{96,0},{100,4},{104,8},{108,12},{1... | collective-permute-start | bytes 417800 | tf_op jit(solution)/shard_map/ppermute | solution.py:290
  23.1 0.0 collective-permute-done.3.refs_1_
  23.1 0.0 copy-start.3
  23.2 1.9 %collective-permute-start.8 = (bf16[544,128]{1,0:T(8,128)(2,1)}, bf16[544,128]{1,0:T(8,128)(2,1)S(1)}, u32[]{:S(2)}, u32[]{:S(2)}) collective-permute-start(bf16[544,128]{1,0:T(8,128)(2,1)} %get-tuple-element.30), channel_id=1, source_target_pairs={{0,120},{4,124},{8,112},{12,116},{120,0},{124,4},{112,8},{116,12},... | collective-permute-start | bytes 417800 | tf_op jit(solution)/shard_map/ppermute | solution.py:290
  25.1 0.0 collective-permute-done.4.refs_2_
  25.1 0.0 copy-start.4
  25.1 1.9 %collective-permute-start.9 = (bf16[544,128]{1,0:T(8,128)(2,1)}, bf16[544,128]{1,0:T(8,128)(2,1)S(1)}, u32[]{:S(2)}, u32[]{:S(2)}) collective-permute-start(bf16[544,128]{1,0:T(8,128)(2,1)} %get-tuple-element.31), channel_id=1, source_target_pairs={{0,24},{4,28},{8,16},{12,20},{24,0},{28,4},{16,8},{20,12},{1,25},{... | collective-permute-start | bytes 417800 | tf_op jit(solution)/shard_map/ppermute | solution.py:290
  27.0 0.0 collective-permute-done.5.refs_3_
  27.0 0.0 copy-start.5
  27.1 1.9 %collective-permute-done.6.refs_4_ = bf16[544,128]{1,0:T(8,128)(2,1)S(1)} collective-permute-done((bf16[544,128]{1,0:T(8,128)(2,1)}, bf16[544,128]{1,0:T(8,128)(2,1)S(1)}, u32[]{:S(2)}, u32[]{:S(2)}) %collective-permute-start.6) | collective-permute-done | bytes 139296 | tf_op jit(solution)/shard_map/ppermute | solution.py:290
  29.0 0.0 collective-permute-done.7.refs_5_
  29.0 3.9 %collective-permute-done.8.refs_6_ = bf16[544,128]{1,0:T(8,128)(2,1)S(1)} collective-permute-done((bf16[544,128]{1,0:T(8,128)(2,1)}, bf16[544,128]{1,0:T(8,128)(2,1)S(1)}, u32[]{:S(2)}, u32[]{:S(2)}) %collective-permute-start.8) | collective-permute-done | bytes 139296 | tf_op jit(solution)/shard_map/ppermute | solution.py:290
  32.9 4.0 %collective-permute-done.9.refs_7_ = bf16[544,128]{1,0:T(8,128)(2,1)S(1)} collective-permute-done((bf16[544,128]{1,0:T(8,128)(2,1)}, bf16[544,128]{1,0:T(8,128)(2,1)S(1)}, u32[]{:S(2)}, u32[]{:S(2)}) %collective-permute-start.9) | collective-permute-done | bytes 139296 | tf_op jit(solution)/shard_map/ppermute | solution.py:290
  36.8 0.0 copy-done.3
  36.9 0.6 copy-done.9
  37.5 2.3 %merge.1 = (bf16[512,128]{1,0:T(8,128)(2,1)}, bf16[64,32,128]{2,1,0:T(8,128)(2,1)}) custom-call(bf16[544,128]{1,0:T(8,128)(2,1)} %get-tuple-element.24.refs_0_, bf16[544,128]{1,0:T(8,128)(2,1)} %copy-done.3, bf16[544,128]{1,0:T(8,128)(2,1)} %copy-done.4, bf16[544,128]{1,0:T(8,128)(2,1)} %copy-done.5, bf16[544,128]{1,0:T(8,128)(2,1)} %copy-done.6, ...), custom_call_target="tpu_custom_call" | custom-call | tf_op jit(solution)/shard_map/merge/pallas_call | solution.py:294
  39.8 0.0 all-gather.3.cloned.1.call-update
  39.8 17.5 %all_to_all.15 = bf16[64,32,128]{2,1,0:T(8,128)(2,1)S(1)} all-to-all(bf16[64,32,128]{2,1,0:T(8,128)(2,1)} %get-tuple-element.32), channel_id=1, replica_groups=mesh['chip'=16,'core'=2,'narrow'=4] {'chip','narrow'}, dimensions={0} | all-to-all | bytes 1048576 | tf_op jit(solution)/shard_map/all_to_all | solution.py:307
  57.3 2.6 %collective-permute-start.10 = (bf16[16,4,32,128]{3,2,1,0:T(8,128)(2,1)S(1)}, bf16[16,4,32,128]{3,2,1,0:T(8,128)(2,1)S(1)}, u32[]{:S(2)}, u32[]{:S(2)}) collective-permute-start(bf16[16,4,32,128]{3,2,1,0:T(8,128)(2,1)S(1)} %bitcast.18), channel_id=1, source_target_pairs={{0,4},{4,0},{1,5},{5,1},{2,6},{6,2},{3,7},{7,3},{8,12},{12,8},{9,1... | collective-permute-start | bytes 1572872 | tf_op jit(solution)/shard_map/ppermute | solution.py:308
  60.0 0.7 collective-permute-start.2
  60.6 1.5 %collective-permute-start.1 = (bf16[520,128]{1,0:T(8,128)(2,1)}, bf16[520,128]{1,0:T(8,128)(2,1)S(1)}, u32[]{:S(2)}, u32[]{:S(2)}) collective-permute-start(bf16[520,128]{1,0:T(8,128)(2,1)} %get-tuple-element.23.own), channel_id=1, source_target_pairs={{0,2},{1,3},{2,0},{3,1},{4,6},{5,7},{6,4},{7,5},{8,10},{9,11},{10,... | collective-permute-start | bytes 399368 | tf_op jit(solution)/shard_map/ppermute | solution.py:292
  62.2 0.0 collective-permute-start
  62.2 3.1 %collective-permute-done.2.d3 = bf16[520,128]{1,0:T(8,128)(2,1)S(1)} collective-permute-done((bf16[520,128]{1,0:T(8,128)(2,1)}, bf16[520,128]{1,0:T(8,128)(2,1)S(1)}, u32[]{:S(2)}, u32[]{:S(2)}) %collective-permute-start.2) | collective-permute-done | bytes 133152 | tf_op jit(solution)/shard_map/ppermute | solution.py:292
  65.3 1.9 %collective-permute-done.1.d2 = bf16[520,128]{1,0:T(8,128)(2,1)S(1)} collective-permute-done((bf16[520,128]{1,0:T(8,128)(2,1)}, bf16[520,128]{1,0:T(8,128)(2,1)S(1)}, u32[]{:S(2)}, u32[]{:S(2)}) %collective-permute-start.1) | collective-permute-done | bytes 133152 | tf_op jit(solution)/shard_map/ppermute | solution.py:292
  67.2 3.5 %collective-permute-done.d1 = bf16[520,128]{1,0:T(8,128)(2,1)S(1)} collective-permute-done((bf16[520,128]{1,0:T(8,128)(2,1)}, bf16[520,128]{1,0:T(8,128)(2,1)S(1)}, u32[]{:S(2)}, u32[]{:S(2)}) %collective-permute-start) | collective-permute-done | bytes 133152 | tf_op jit(solution)/shard_map/ppermute | solution.py:292
  70.7 0.0 collective-permute-done.10.far
  70.7 0.0 copy-done
  70.7 0.6 copy-done.12
  71.3 0.2 copy-done.1
  71.5 5.4 %panel.1 = (bf16[512,512]{1,0:T(8,128)(2,1)}, bf16[4,512,128]{2,1,0:T(8,128)(2,1)}, f32[32,8,128]{2,1,0:T(8,128)}, bf16[512,128]{1,0:T(8,128)(2,1)}, s32[4,128]{1,0:T(4,128)}) custom-call(s32[4]{0:T(128)} %order.9, bf16[520,128]{1,0:T(8,128)(2,1)} %get-tuple-element.23.own, bf16[520,128]{1,0:T(8,128)(2,1)} %copy-done.12, bf16[520,128]{1,0:T(8,128)(2,1)} %copy-done.11, ...), custom_call_target="tpu_custom_call" | custom-call | tf_op jit(solution)/shard_map/panel/pallas_call | solution.py:310
  76.9 4.0 %all-to-all-start.1 = ((f32[32,8,128]{2,1,0:T(8,128)}), f32[32,8,128]{2,1,0:T(8,128)S(1)}, u32[]{:S(2)}, u32[]{:S(2)}) async-start(f32[32,8,128]{2,1,0:T(8,128)} %get-tuple-element.38), calls=%async_computation.1 | async-start | bytes 262144 | tf_op jit(solution)/shard_map/all_to_all | solution.py:353
  80.9 4.3 %combine.1.h = bf16[15,512,128]{2,1,0:T(8,128)(2,1)} custom-call(s32[4]{0:T(128)} %order.9, bf16[512,512]{1,0:T(8,128)(2,1)} %get-tuple-element.35.lown, bf16[4,512,128]{2,1,0:T(8,128)(2,1)} %get-tuple-element.36.lpiv, bf16[4,128,128]{2,1,0:T(8,128)(2,1)} %w_ref.7), custom_call_target="tpu_custom_call" | custom-call | tf_op jit(solution)/shard_map/combine/pallas_call | solution.py:345
  85.2 4.2 %forward.1 = (f32[8,128]{1,0:T(8,128)}, bf16[4,128,256]{2,1,0:T(8,128)(2,1)}) custom-call(s32[4]{0:T(128)} %order.9, bf16[16,4,32,128]{3,2,1,0:T(8,128)(2,1)} %bitcast.20, bf16[16,4,32,128]{3,2,1,0:T(8,128)(2,1)} %copy-done.1, bf16[4,128,128]{2,1,0:T(8,128)(2,1)} %w_ref.7, bf16[4,128,256]{2,1,0:T(8,128)(2,1)} %bitcast.25, ...), custom_call_target="tpu_custom_call" | custom-call | tf_op jit(solution)/shard_map/forward/pallas_call | solution.py:330
  89.5 0.0 all-to-all-done.1.parts
  89.5 0.7 copy-done.2
  90.1 2.8 %solve.1 = bf16[128,8,128]{2,1,0:T(8,128)(2,1)} custom-call(s32[4]{0:T(128)} %order.9, f32[32,8,128]{2,1,0:T(8,128)} %copy-done.2, f32[8,128]{1,0:T(8,128)} %get-tuple-element.39.zt, bf16[4,512,128]{2,1,0:T(8,128)(2,1)} %get-tuple-element.36.lpiv, bf16[4,128,128]{2,1,0:T(8,128)(2,1)} %w_ref.7, bf16[15,512,128]{2,1,0:T(8,128)(2,1)} %combine.1.h), custom_call_target="tpu_custom_call" | custom-call | tf_op jit(solution)/shard_map/solve/pallas_call | solution.py:354
  92.9 8.1 %all-to-all-start.2 = ((bf16[128,8,128]{2,1,0:T(8,128)(2,1)}), bf16[128,8,128]{2,1,0:T(8,128)(2,1)S(1)}, u32[]{:S(2)}, u32[]{:S(2)}) async-start(bf16[128,8,128]{2,1,0:T(8,128)(2,1)} %solve.1), calls=%async_computation.2 | async-start | bytes 524288 | tf_op jit(solution)/shard_map/all_to_all | solution.py:362
  101.0 0.0 all-gather.3.cloned.1.call-done
  101.0 9.9 %update.1 = bf16[4,128,32,128]{3,2,1,0:T(8,128)(2,1)} custom-call(s32[4]{0:T(128)} %order.9, s32[4,32]{1,0:T(4,128)} %bitcast.28, s32[4,128]{1,0:T(4,128)} %get-tuple-element.33.mpiv, bf16[4,128,32,128]{3,2,1,0:T(8,128)(2,1)} %bitcast.17, bf16[32,512,128]{2,1,0:T(8,128)(2,1)} %bitcast.21, bf16[15,512,128]{2,1,0:T(8,128)(2,1)} %combine.1.h, ...), custom_call_target="tpu_custom_call" | custom-call | tf_op jit(solution)/shard_map/update/pallas_call | solution.py:364
  111.0 0.9 all-to-all-done.2
  111.9 0.4 copy.9
  112.3 0.9 reshape.41
  (17 shorter events, 0.0 us)
Async XLA Ops:
  7.2 93.9 %all-gather.3.cloned.1.call-start = ((), (), s32[]{:S(2)}) async-start(), calls=%async_computation.3 | async-start | bytes 4325376 | tf_op jit(solution)/shard_map/all_gather | solution.py:305
  10.2 12.9 %collective-permute-start.3 = (bf16[544,128]{1,0:T(8,128)(2,1)}, bf16[544,128]{1,0:T(8,128)(2,1)S(1)}, u32[]{:S(2)}, u32[]{:S(2)}) collective-permute-start(bf16[544,128]{1,0:T(8,128)(2,1)} %get-tuple-element.25), channel_id=1, source_target_pairs={{0,32},{4,36},{8,40},{12,44},{32,0},{36,4},{40,8},{44,12},{1,33},{... | collective-permute-start | bytes 417800 | tf_op jit(solution)/shard_map/ppermute | solution.py:290
  14.2 10.9 %collective-permute-start.4 = (bf16[544,128]{1,0:T(8,128)(2,1)}, bf16[544,128]{1,0:T(8,128)(2,1)S(1)}, u32[]{:S(2)}, u32[]{:S(2)}) collective-permute-start(bf16[544,128]{1,0:T(8,128)(2,1)} %get-tuple-element.26), channel_id=1, source_target_pairs={{0,64},{4,68},{8,72},{12,76},{64,0},{68,4},{72,8},{76,12},{1,65},{... | collective-permute-start | bytes 417800 | tf_op jit(solution)/shard_map/ppermute | solution.py:290
  16.4 10.7 %collective-permute-start.5 = (bf16[544,128]{1,0:T(8,128)(2,1)}, bf16[544,128]{1,0:T(8,128)(2,1)S(1)}, u32[]{:S(2)}, u32[]{:S(2)}) collective-permute-start(bf16[544,128]{1,0:T(8,128)(2,1)} %get-tuple-element.27), channel_id=1, source_target_pairs={{0,56},{4,60},{8,48},{12,52},{56,0},{60,4},{48,8},{52,12},{1,57},{... | collective-permute-start | bytes 417800 | tf_op jit(solution)/shard_map/ppermute | solution.py:290
  19.0 10.0 %collective-permute-start.6 = (bf16[544,128]{1,0:T(8,128)(2,1)}, bf16[544,128]{1,0:T(8,128)(2,1)S(1)}, u32[]{:S(2)}, u32[]{:S(2)}) collective-permute-start(bf16[544,128]{1,0:T(8,128)(2,1)} %get-tuple-element.28), channel_id=1, source_target_pairs={{0,88},{4,92},{8,80},{12,84},{88,0},{92,4},{80,8},{84,12},{1,89},{... | collective-permute-start | bytes 417800 | tf_op jit(solution)/shard_map/ppermute | solution.py:290
  21.2 7.8 %collective-permute-start.7 = (bf16[544,128]{1,0:T(8,128)(2,1)}, bf16[544,128]{1,0:T(8,128)(2,1)S(1)}, u32[]{:S(2)}, u32[]{:S(2)}) collective-permute-start(bf16[544,128]{1,0:T(8,128)(2,1)} %get-tuple-element.29), channel_id=1, source_target_pairs={{0,96},{4,100},{8,104},{12,108},{96,0},{100,4},{104,8},{108,12},{1... | collective-permute-start | bytes 417800 | tf_op jit(solution)/shard_map/ppermute | solution.py:290
  23.1 13.7 %copy-start.3 = (bf16[544,128]{1,0:T(8,128)(2,1)}, bf16[544,128]{1,0:T(8,128)(2,1)S(1)}, u32[]{:S(2)}) copy-start(bf16[544,128]{1,0:T(8,128)(2,1)S(1)} %collective-permute-done.3.refs_1_) | copy-start | bytes 417796
  23.2 9.7 %collective-permute-start.8 = (bf16[544,128]{1,0:T(8,128)(2,1)}, bf16[544,128]{1,0:T(8,128)(2,1)S(1)}, u32[]{:S(2)}, u32[]{:S(2)}) collective-permute-start(bf16[544,128]{1,0:T(8,128)(2,1)} %get-tuple-element.30), channel_id=1, source_target_pairs={{0,120},{4,124},{8,112},{12,116},{120,0},{124,4},{112,8},{116,12},... | collective-permute-start | bytes 417800 | tf_op jit(solution)/shard_map/ppermute | solution.py:290
  25.1 11.7 %copy-start.4 = (bf16[544,128]{1,0:T(8,128)(2,1)}, bf16[544,128]{1,0:T(8,128)(2,1)S(1)}, u32[]{:S(2)}) copy-start(bf16[544,128]{1,0:T(8,128)(2,1)S(1)} %collective-permute-done.4.refs_2_) | copy-start | bytes 417796
  25.1 11.7 %collective-permute-start.9 = (bf16[544,128]{1,0:T(8,128)(2,1)}, bf16[544,128]{1,0:T(8,128)(2,1)S(1)}, u32[]{:S(2)}, u32[]{:S(2)}) collective-permute-start(bf16[544,128]{1,0:T(8,128)(2,1)} %get-tuple-element.31), channel_id=1, source_target_pairs={{0,24},{4,28},{8,16},{12,20},{24,0},{28,4},{16,8},{20,12},{1,25},{... | collective-permute-start | bytes 417800 | tf_op jit(solution)/shard_map/ppermute | solution.py:290
  27.0 9.8 %copy-start.5 = (bf16[544,128]{1,0:T(8,128)(2,1)}, bf16[544,128]{1,0:T(8,128)(2,1)S(1)}, u32[]{:S(2)}) copy-start(bf16[544,128]{1,0:T(8,128)(2,1)S(1)} %collective-permute-done.5.refs_3_) | copy-start | bytes 417796
  29.0 7.9 %copy-start.6 = (bf16[544,128]{1,0:T(8,128)(2,1)}, bf16[544,128]{1,0:T(8,128)(2,1)S(1)}, u32[]{:S(2)}) copy-start(bf16[544,128]{1,0:T(8,128)(2,1)S(1)} %collective-permute-done.6.refs_4_) | copy-start | bytes 417796
  29.0 7.9 %copy-start.7 = (bf16[544,128]{1,0:T(8,128)(2,1)}, bf16[544,128]{1,0:T(8,128)(2,1)S(1)}, u32[]{:S(2)}) copy-start(bf16[544,128]{1,0:T(8,128)(2,1)S(1)} %collective-permute-done.7.refs_5_) | copy-start | bytes 417796
  32.9 4.0 %copy-start.8 = (bf16[544,128]{1,0:T(8,128)(2,1)}, bf16[544,128]{1,0:T(8,128)(2,1)S(1)}, u32[]{:S(2)}) copy-start(bf16[544,128]{1,0:T(8,128)(2,1)S(1)} %collective-permute-done.8.refs_6_) | copy-start | bytes 417796
  36.8 0.7 copy-start.9
  57.3 13.4 %copy-start = (bf16[64,32,128]{2,1,0:T(8,128)(2,1)}, bf16[64,32,128]{2,1,0:T(8,128)(2,1)S(1)}, u32[]{:S(2)}) copy-start(bf16[64,32,128]{2,1,0:T(8,128)(2,1)S(1)} %all_to_all.15) | copy-start | bytes 1572868
  57.3 13.3 %collective-permute-start.10 = (bf16[16,4,32,128]{3,2,1,0:T(8,128)(2,1)S(1)}, bf16[16,4,32,128]{3,2,1,0:T(8,128)(2,1)S(1)}, u32[]{:S(2)}, u32[]{:S(2)}) collective-permute-start(bf16[16,4,32,128]{3,2,1,0:T(8,128)(2,1)S(1)} %bitcast.18), channel_id=1, source_target_pairs={{0,4},{4,0},{1,5},{5,1},{2,6},{6,2},{3,7},{7,3},{8,12},{12,8},{9,1... | collective-permute-start | bytes 1572872 | tf_op jit(solution)/shard_map/ppermute | solution.py:308
  60.0 5.3 %collective-permute-start.2 = (bf16[520,128]{1,0:T(8,128)(2,1)}, bf16[520,128]{1,0:T(8,128)(2,1)S(1)}, u32[]{:S(2)}, u32[]{:S(2)}) collective-permute-start(bf16[520,128]{1,0:T(8,128)(2,1)} %get-tuple-element.23.own), channel_id=1, source_target_pairs={{0,3},{1,0},{2,1},{3,2},{4,7},{5,4},{6,5},{7,6},{8,11},{9,8},{10,9... | collective-permute-start | bytes 399368 | tf_op jit(solution)/shard_map/ppermute | solution.py:292
  60.6 6.5 %collective-permute-start.1 = (bf16[520,128]{1,0:T(8,128)(2,1)}, bf16[520,128]{1,0:T(8,128)(2,1)S(1)}, u32[]{:S(2)}, u32[]{:S(2)}) collective-permute-start(bf16[520,128]{1,0:T(8,128)(2,1)} %get-tuple-element.23.own), channel_id=1, source_target_pairs={{0,2},{1,3},{2,0},{3,1},{4,6},{5,7},{6,4},{7,5},{8,10},{9,11},{10,... | collective-permute-start | bytes 399368 | tf_op jit(solution)/shard_map/ppermute | solution.py:292
  62.2 8.5 %collective-permute-start = (bf16[520,128]{1,0:T(8,128)(2,1)}, bf16[520,128]{1,0:T(8,128)(2,1)S(1)}, u32[]{:S(2)}, u32[]{:S(2)}) collective-permute-start(bf16[520,128]{1,0:T(8,128)(2,1)} %get-tuple-element.23.own), channel_id=1, source_target_pairs={{0,1},{1,2},{2,3},{3,0},{4,5},{5,6},{6,7},{7,4},{8,9},{9,10},{10,1... | collective-permute-start | bytes 399368 | tf_op jit(solution)/shard_map/ppermute | solution.py:292
  65.3 5.4 %copy-start.10 = (bf16[520,128]{1,0:T(8,128)(2,1)}, bf16[520,128]{1,0:T(8,128)(2,1)S(1)}, u32[]{:S(2)}) copy-start(bf16[520,128]{1,0:T(8,128)(2,1)S(1)} %collective-permute-done.2.d3) | copy-start | bytes 399364
  67.2 3.5 %copy-start.11 = (bf16[520,128]{1,0:T(8,128)(2,1)}, bf16[520,128]{1,0:T(8,128)(2,1)S(1)}, u32[]{:S(2)}) copy-start(bf16[520,128]{1,0:T(8,128)(2,1)S(1)} %collective-permute-done.1.d2) | copy-start | bytes 399364
  70.7 0.7 copy-start.12
  70.7 0.8 copy-start.1
  76.9 12.6 %all-to-all-start.1 = ((f32[32,8,128]{2,1,0:T(8,128)}), f32[32,8,128]{2,1,0:T(8,128)S(1)}, u32[]{:S(2)}, u32[]{:S(2)}) async-start(f32[32,8,128]{2,1,0:T(8,128)} %get-tuple-element.38), calls=%async_computation.1 | async-start | bytes 262144 | tf_op jit(solution)/shard_map/all_to_all | solution.py:353
  89.5 0.7 copy-start.2
  92.9 19.0 %all-to-all-start.2 = ((bf16[128,8,128]{2,1,0:T(8,128)(2,1)}), bf16[128,8,128]{2,1,0:T(8,128)(2,1)S(1)}, u32[]{:S(2)}, u32[]{:S(2)}) async-start(bf16[128,8,128]{2,1,0:T(8,128)(2,1)} %solve.1), calls=%async_computation.2 | async-start | bytes 524288 | tf_op jit(solution)/shard_map/all_to_all | solution.py:362
Sparse Core Ops, SparseCore 0:
  39.9 46.2 all-gather.2

commit v6 on v4

--- a/solution.py
+++ b/solution.py
@@ -49,45 +49,54 @@
 def prep_kernel(row_ref, col_ref, b_ref, mask_ref, *outs):
     q = lax.axis_index("narrow")
     sent, mine = outs[:PIECES], outs[PIECES]
+    g = pl.program_id(0)
     gather = one_hot(BS, lambda r: (r % SUB) * 8 + r // SUB)
     for ct in range(NC // 8):
-        for ag in range(BS // SUB):
-            native = row_ref[0, ag * SUB : (ag + 1) * SUB, ct * 8 : (ct + 1) * 8, :]
-            native = native.astype(F32).reshape(BS, BS).astype(BF)
-            blocks = dot(gather, native).astype(BF)
-            for e in range(8):
-                p, cc = divmod(ct * 8 + e, CPP)
-                sent[p][cc * BS + ag * SUB : cc * BS + (ag + 1) * SUB] = blocks[e * SUB : (e + 1) * SUB]
-            if ct == 0:
-                sent[ag][CPP * BS : CPP * BS + SUB] = blocks[:SUB]
-    mask = mask_ref[...].astype(F32)
-    widen = one_hot(NC, lambda r: r)
-    line = jnp.broadcast_to(dot(mask.astype(BF), widen)[0:1], (8, BS)).astype(BF)
-    for p in range(PIECES):
-        rows = b_ref[0, p * SUB : (p + 1) * SUB, :].astype(F32)
-        rows = jnp.where((q & 2) != 0, rows[8:], rows[:8])
-        rows = jnp.where((q & 1) != 0, rows[:, BS:], rows[:, :BS])
-        sent[p][CPP * BS + SUB : CPP * BS + SUB + 8] = rows.astype(BF)
-        sent[p][CPP * BS + SUB + 8 :] = line
+
+        @pl.when(g == ct)
+        def _():
+            for ag in range(BS // SUB):
+                native = row_ref[0, ag * SUB : (ag + 1) * SUB].astype(F32).reshape(BS, BS).astype(BF)
+                blocks = dot(gather, native).astype(BF)
+                for e in range(8):
+                    p, cc = divmod(ct * 8 + e, CPP)
+                    sent[p][cc * BS + ag * SUB : cc * BS + (ag + 1) * SUB] = blocks[e * SUB : (e + 1) * SUB]
+                if ct == 0:
+                    sent[ag][CPP * BS : CPP * BS + SUB] = blocks[:SUB]
+
+    @pl.when(g == 0)
+    def _():
+        mask = mask_ref[...].astype(F32)
+        widen = one_hot(NC, lambda r: r)
+        line = jnp.broadcast_to(dot(mask.astype(BF), widen)[0:1], (8, BS)).astype(BF)
+        for p in range(PIECES):
+            rows = b_ref[0, p * SUB : (p + 1) * SUB, :].astype(F32)
+            rows = jnp.where((q & 2) != 0, rows[8:], rows[:8])
+            rows = jnp.where((q & 1) != 0, rows[:, BS:], rows[:, :BS])
+            sent[p][CPP * BS + SUB : CPP * BS + SUB + 8] = rows.astype(BF)
+            sent[p][CPP * BS + SUB + 8 :] = line
+        first = jnp.broadcast_to(mask[:, 0:1], (NR, BS))
+        mine[NR * BS :] = jnp.concatenate([first, jnp.zeros((8 - NR, BS), F32)], axis=0).astype(BF)
+
     pick = one_hot(SUB, lambda r: r * 8)
-    for r in range(NR):
-        for ag in range(BS // SUB):
-            native = col_ref[r, ag * SUB : (ag + 1) * SUB].astype(F32).reshape(BS, BS).astype(BF)
-            mine[r * BS + ag * SUB : r * BS + (ag + 1) * SUB] = dot(pick, native).astype(BF)
-    first = jnp.broadcast_to(mask[:, 0:1], (NR, BS))
-    mine[NR * BS :] = jnp.concatenate([first, jnp.zeros((8 - NR, BS), F32)], axis=0).astype(BF)
+    for ag in range(BS // SUB):
+        native = col_ref[0, ag * SUB : (ag + 1) * SUB].astype(F32).reshape(BS, BS).astype(BF)
+        mine[pl.ds(pl.multiple_of(g * BS + ag * SUB, SUB), SUB), :] = dot(pick, native).astype(BF)
 
 
 def merge_kernel(*refs):
-    parts, (piece, copies) = refs[:PIECES], refs[PIECES:]
-    first = parts[0][...]
-    is_source = lax.axis_index("chip") < 2
-    total = jnp.where(is_source, first, jnp.zeros_like(first))
-    for part in parts[1:]:
-        total = total + part[...]
-    piece[...] = total[: CPP * BS]
+    parts, (piece, copies, buf) = refs[:PIECES], refs[PIECES:]
+    chip = lax.axis_index("chip")
+    place = (chip >> 2) * 2 + ((chip & 3) >> 1)
+    for p, part in zip((0, *SCATTER_ORDER), parts):
+
+        @pl.when(place == p)
+        def _():
+            pltpu.sync_copy(part, buf)
+
+    piece[...] = buf[: CPP * BS]
     for d in range(NW * 2):
-        copies[d] = total[CPP * BS :]
+        copies[d] = buf[CPP * BS :]
 
 
 def wide_index():
@@ -119,6 +128,8 @@
                 mkp[i, k] = tile[k, SUB + 8 : SUB + 16].astype(F32)
     for i in range(NP):
         mpiv[i : i + 1] = mkp[i, q, 0:1].astype(jnp.int32)
+    y0 = jnp.where(w < NP, jnp.zeros_like(y_ref[0]), y_ref[0])
+    y = jnp.concatenate([y0] + [y_ref[r] for r in range(1, NR)], axis=0)
     row_rank = [own_rank, None, None, None] + rank
     for s in range(NP):
         k = order[s]
@@ -133,6 +144,7 @@
         lb = jnp.concatenate(parts, axis=0)
         lown[:, s * BS : (s + 1) * BS] = lb[: NR * BS]
         lpiv[s] = lb[NR * BS :]
+        tall[:, s * BS : (s + 1) * BS] = dot(y, lb[: NR * BS], 0, 0)
         for t in range(s + 1, NP):
             j = order[t]
             akj = pan[j, pl.ds(pl.multiple_of(NR * BS + k * BS, BS), BS), :]
@@ -142,9 +154,6 @@
                 m = mk[j, i : i + 1, :] if i < NR else mkp[i - NR, j, 0:1, 0:1]
                 pan[j, sl] = (pan[j, sl].astype(F32) - m * prod[sl]).astype(BF)
     delta[...] = (own[0 : NR * BS].astype(F32) - pan[q, 0 : NR * BS].astype(F32)).astype(BF)
-    y0 = jnp.where(w < NP, jnp.zeros_like(y_ref[0]), y_ref[0])
-    y = jnp.concatenate([y0] + [y_ref[r] for r in range(1, NR)], axis=0)
-    tall[...] = dot(y, lown[...], 0, 0)
     for j in range(2):
         mine_cols = tall[pl.ds(pl.multiple_of(j * BS + q * NW, NW), NW), :]
         for s in range(NP):
@@ -277,8 +286,13 @@
     *sent, mine = pl.pallas_call(
         prep_kernel,
         out_shape=tuple(jax.ShapeDtypeStruct(shape, BF) for shape in shapes),
-        grid=(1,),
-        in_specs=[fixed((1, BS, NC, BS)), fixed((NR, BS, 8, BS)), fixed((1, BS, NRHS)), fixed((NR, NC))],
+        grid=(NC // 8,),
+        in_specs=[
+            pl.BlockSpec((1, BS, 8, BS), lambda g: (0, 0, g, 0)),
+            pl.BlockSpec((1, BS, 8, BS), lambda g: (g, 0, 0, 0)),
+            fixed((1, BS, NRHS)),
+            fixed((NR, NC)),
+        ],
         out_specs=tuple(fixed(shape) for shape in shapes),
         name="prep",
     )(blocks, blocks, b, mask)
@@ -295,8 +309,9 @@
             jax.ShapeDtypeStruct((CPP * BS, BS), BF),
             jax.ShapeDtypeStruct((NW * 2, EXTRA, BS), BF),
         ),
-        in_specs=vmem(PIECES),
+        in_specs=[pl.BlockSpec(memory_space=pl.ANY)] * PIECES,
         out_specs=tuple(vmem(2)),
+        scratch_shapes=[pltpu.VMEM((CPP * BS + EXTRA, BS), BF)],
         name="merge",
     )(sent[0], *pieces)
 

time: 117 us -> 119 us (1.017)
  Pallas kernels: 31.9 us -> 33.3 us
    pallas_call x1, Pallas kernels: 3.03 us -> 4.4 us  [body(): pl.pallas_call(prep_kernel, out_shape=tuple((jax.ShapeDtypeStruct(shape,...]
where the time goes in v6:
time: 119 us; the launch traced here: 118 us
  starting transfers between devices  33.3 us (28%)
  Pallas kernels  33.3 us (28%)
  blocking collectives  21.1 us (18%)
  between operations  14.2 us (12%)
  waiting for transfers between devices  12.5 us (11%)
  local copies, waits for them, and re-layouts  3.41 us (3%)
    all_to_all x1, blocking collectives, body(): lax.all_to_all(copies, ('chip', 'narrow'), 0, 0)  21.1 us
    ppermute x7, starting transfers between devices, body(): lax.ppermute(sent[p], WIDE, [(i, holder(p, i)) for i in range(NP)])  14.8 us
    pallas_call x1, Pallas kernels, body(): pl.pallas_call(update_kernel, out_shape=jax.ShapeDtypeStruct((NR, BS, NC,...  9.93 us
    ppermute x3, waiting for transfers between devices, body(): lax.ppermute(mine, 'narrow', [(i, (i + d) % 4) for i in range(4)])  8.53 us
    all_to_all x1, starting transfers between devices, body(): xall = lax.all_to_all(xg, ('narrow', *WIDE), 0, 0)  8.11 us
    pallas_call x1, Pallas kernels, body(): pl.pallas_call(panel_kernel, out_shape=(jax.ShapeDtypeStruct((NR * BS, NP...  5.9 us
    pallas_call x1, Pallas kernels, body(): pl.pallas_call(prep_kernel, out_shape=tuple((jax.ShapeDtypeStruct(shape,...  4.4 us
    pallas_call x1, Pallas kernels, body(): pl.pallas_call(combine_kernel, out_shape=jax.ShapeDtypeStruct((15, NR * B...  4.27 us
  transfers between devices with their start and end apart: 14, of which 6 were waited for; matrix products, arithmetic and copies ran while one was open for 0% of the time, Pallas kernels for 23%

profile of v6, /device:TPU:1, one launch (start us, length us, event | category | flops | bytes accessed | tf_op | source)
XLA Modules:
  0.0 117.8 jit_solution(9285863237460031147)
XLA Ops:
  7.2 0.0 all-gather.3.cloned.1.call-start
  7.2 4.4 %prep.1 = (bf16[544,128]{1,0:T(8,128)(2,1)}, bf16[544,128]{1,0:T(8,128)(2,1)}, bf16[544,128]{1,0:T(8,128)(2,1)}, bf16[544,128]{1,0:T(8,128)(2,1)}, bf16[544,128]...) custom-call(bf16[4,128,32,128]{3,2,1,0:T(8,128)(2,1)} %bitcast.15, ...), custom_call_target="tpu_custom_call" | custom-call | tf_op jit(solution)/shard_map/prep/pallas_call | solution.py:286
  11.6 3.9 %collective-permute-start.3 = (bf16[544,128]{1,0:T(8,128)(2,1)}, bf16[544,128]{1,0:T(8,128)(2,1)S(1)}, u32[]{:S(2)}, u32[]{:S(2)}) collective-permute-start(bf16[544,128]{1,0:T(8,128)(2,1)} %get-tuple-element.25), channel_id=1, source_target_pairs={{0,32},{4,36},{8,40},{12,44},{1,33},{5,37},{9,41},{13,45},{2,34},{... | collective-permute-start | bytes 417800 | tf_op jit(solution)/shard_map/ppermute | solution.py:302
  15.5 2.2 %collective-permute-start.4 = (bf16[544,128]{1,0:T(8,128)(2,1)}, bf16[544,128]{1,0:T(8,128)(2,1)S(1)}, u32[]{:S(2)}, u32[]{:S(2)}) collective-permute-start(bf16[544,128]{1,0:T(8,128)(2,1)} %get-tuple-element.26), channel_id=1, source_target_pairs={{0,64},{4,68},{8,72},{12,76},{1,65},{5,69},{9,73},{13,77},{2,66},{... | collective-permute-start | bytes 417800 | tf_op jit(solution)/shard_map/ppermute | solution.py:302
  17.8 2.6 %collective-permute-start.5 = (bf16[544,128]{1,0:T(8,128)(2,1)}, bf16[544,128]{1,0:T(8,128)(2,1)S(1)}, u32[]{:S(2)}, u32[]{:S(2)}) collective-permute-start(bf16[544,128]{1,0:T(8,128)(2,1)} %get-tuple-element.27), channel_id=1, source_target_pairs={{0,56},{4,60},{8,48},{12,52},{1,57},{5,61},{9,49},{13,53},{2,58},{... | collective-permute-start | bytes 417800 | tf_op jit(solution)/shard_map/ppermute | solution.py:302
  20.4 2.2 %collective-permute-start.6 = (bf16[544,128]{1,0:T(8,128)(2,1)}, bf16[544,128]{1,0:T(8,128)(2,1)S(1)}, u32[]{:S(2)}, u32[]{:S(2)}) collective-permute-start(bf16[544,128]{1,0:T(8,128)(2,1)} %get-tuple-element.28), channel_id=1, source_target_pairs={{0,88},{4,92},{8,80},{12,84},{1,89},{5,93},{9,81},{13,85},{2,90},{... | collective-permute-start | bytes 417800 | tf_op jit(solution)/shard_map/ppermute | solution.py:302
  22.6 1.3 %collective-permute-start.7 = (bf16[544,128]{1,0:T(8,128)(2,1)}, bf16[544,128]{1,0:T(8,128)(2,1)S(1)}, u32[]{:S(2)}, u32[]{:S(2)}) collective-permute-start(bf16[544,128]{1,0:T(8,128)(2,1)} %get-tuple-element.29), channel_id=1, source_target_pairs={{0,96},{4,100},{8,104},{12,108},{1,97},{5,101},{9,105},{13,109},{2... | collective-permute-start | bytes 417800 | tf_op jit(solution)/shard_map/ppermute | solution.py:302
  23.9 0.0 collective-permute-done.3.refs_1_
  23.9 0.0 copy-start.3
  23.9 1.3 %collective-permute-start.8 = (bf16[544,128]{1,0:T(8,128)(2,1)}, bf16[544,128]{1,0:T(8,128)(2,1)S(1)}, u32[]{:S(2)}, u32[]{:S(2)}) collective-permute-start(bf16[544,128]{1,0:T(8,128)(2,1)} %get-tuple-element.30), channel_id=1, source_target_pairs={{0,120},{4,124},{8,112},{12,116},{1,121},{5,125},{9,113},{13,117},... | collective-permute-start | bytes 417800 | tf_op jit(solution)/shard_map/ppermute | solution.py:302
  25.2 0.0 collective-permute-done.4.refs_2_
  25.2 0.0 copy-start.4
  25.2 1.3 %collective-permute-start.9 = (bf16[544,128]{1,0:T(8,128)(2,1)}, bf16[544,128]{1,0:T(8,128)(2,1)S(1)}, u32[]{:S(2)}, u32[]{:S(2)}) collective-permute-start(bf16[544,128]{1,0:T(8,128)(2,1)} %get-tuple-element.31), channel_id=1, source_target_pairs={{0,24},{4,28},{8,16},{12,20},{1,25},{5,29},{9,17},{13,21},{2,26},{... | collective-permute-start | bytes 417800 | tf_op jit(solution)/shard_map/ppermute | solution.py:302
  26.5 0.0 collective-permute-done.5.refs_3_
  26.5 0.0 copy-start.5
  26.6 0.9 collective-permute-done.6.refs_4_
  27.5 0.0 collective-permute-done.7.refs_5_
  27.5 2.0 %collective-permute-done.8.refs_6_ = bf16[544,128]{1,0:T(8,128)(2,1)S(1)} collective-permute-done((bf16[544,128]{1,0:T(8,128)(2,1)}, bf16[544,128]{1,0:T(8,128)(2,1)S(1)}, u32[]{:S(2)}, u32[]{:S(2)}) %collective-permute-start.8) | collective-permute-done | bytes 139296 | tf_op jit(solution)/shard_map/ppermute | solution.py:302
  29.5 0.0 collective-permute-done.9.refs_7_
  29.5 0.0 copy-done.3
  29.6 0.6 copy-done.8
  30.2 0.1 copy-done.9
  30.2 1.8 %merge.1 = (bf16[512,128]{1,0:T(8,128)(2,1)}, bf16[64,32,128]{2,1,0:T(8,128)(2,1)}) custom-call(bf16[544,128]{1,0:T(8,128)(2,1)} %get-tuple-element.24.refs_0_, bf16[544,128]{1,0:T(8,128)(2,1)} %copy-done.3, bf16[544,128]{1,0:T(8,128)(2,1)} %copy-done.4, bf16[544,128]{1,0:T(8,128)(2,1)} %copy-done.5, bf16[544,128]{1,0:T(8,128)(2,1)} %copy-done.6, ...), custom_call_target="tpu_custom_call" | custom-call | tf_op jit(solution)/shard_map/merge/pallas_call | solution.py:306
  32.0 0.0 all-gather.3.cloned.1.call-update
  32.0 21.1 %all_to_all.15 = bf16[64,32,128]{2,1,0:T(8,128)(2,1)S(1)} all-to-all(bf16[64,32,128]{2,1,0:T(8,128)(2,1)} %get-tuple-element.32), channel_id=1, replica_groups=mesh['chip'=16,'core'=2,'narrow'=4] {'chip','narrow'}, dimensions={0} | all-to-all | bytes 1048576 | tf_op jit(solution)/shard_map/all_to_all | solution.py:320
  53.1 4.1 %collective-permute-start.10 = (bf16[16,4,32,128]{3,2,1,0:T(8,128)(2,1)S(1)}, bf16[16,4,32,128]{3,2,1,0:T(8,128)(2,1)S(1)}, u32[]{:S(2)}, u32[]{:S(2)}) collective-permute-start(bf16[16,4,32,128]{3,2,1,0:T(8,128)(2,1)S(1)} %bitcast.18), channel_id=1, source_target_pairs={{0,4},{4,0},{1,5},{5,1},{2,6},{6,2},{3,7},{7,3},{8,12},{12,8},{9,1... | collective-permute-start | bytes 1572872 | tf_op jit(solution)/shard_map/ppermute | solution.py:321
  57.3 0.7 collective-permute-start.2
  57.9 1.5 %collective-permute-start.1 = (bf16[520,128]{1,0:T(8,128)(2,1)}, bf16[520,128]{1,0:T(8,128)(2,1)S(1)}, u32[]{:S(2)}, u32[]{:S(2)}) collective-permute-start(bf16[520,128]{1,0:T(8,128)(2,1)} %get-tuple-element.23.own), channel_id=1, source_target_pairs={{0,2},{1,3},{2,0},{3,1},{4,6},{5,7},{6,4},{7,5},{8,10},{9,11},{10,... | collective-permute-start | bytes 399368 | tf_op jit(solution)/shard_map/ppermute | solution.py:304
  59.4 0.0 collective-permute-start
  59.4 3.1 %collective-permute-done.2.d3 = bf16[520,128]{1,0:T(8,128)(2,1)S(1)} collective-permute-done((bf16[520,128]{1,0:T(8,128)(2,1)}, bf16[520,128]{1,0:T(8,128)(2,1)S(1)}, u32[]{:S(2)}, u32[]{:S(2)}) %collective-permute-start.2) | collective-permute-done | bytes 133152 | tf_op jit(solution)/shard_map/ppermute | solution.py:304
  62.6 1.9 %collective-permute-done.1.d2 = bf16[520,128]{1,0:T(8,128)(2,1)S(1)} collective-permute-done((bf16[520,128]{1,0:T(8,128)(2,1)}, bf16[520,128]{1,0:T(8,128)(2,1)S(1)}, u32[]{:S(2)}, u32[]{:S(2)}) %collective-permute-start.1) | collective-permute-done | bytes 133152 | tf_op jit(solution)/shard_map/ppermute | solution.py:304
  64.5 3.5 %collective-permute-done.d1 = bf16[520,128]{1,0:T(8,128)(2,1)S(1)} collective-permute-done((bf16[520,128]{1,0:T(8,128)(2,1)}, bf16[520,128]{1,0:T(8,128)(2,1)S(1)}, u32[]{:S(2)}, u32[]{:S(2)}) %collective-permute-start) | collective-permute-done | bytes 133152 | tf_op jit(solution)/shard_map/ppermute | solution.py:304
  68.0 0.0 collective-permute-done.10.far
  68.0 0.6 copy-done.12
  68.6 0.2 copy-done.1
  68.8 5.9 %panel.1 = (bf16[512,512]{1,0:T(8,128)(2,1)}, bf16[4,512,128]{2,1,0:T(8,128)(2,1)}, f32[32,8,128]{2,1,0:T(8,128)}, bf16[512,128]{1,0:T(8,128)(2,1)}, s32[4,128]{1,0:T(4,128)}) custom-call(s32[4]{0:T(128)} %order.9, bf16[520,128]{1,0:T(8,128)(2,1)} %get-tuple-element.23.own, bf16[520,128]{1,0:T(8,128)(2,1)} %copy-done.12, bf16[520,128]{1,0:T(8,128)(2,1)} %copy-done.11, ...), custom_call_target="tpu_custom_call" | custom-call | tf_op jit(solution)/shard_map/panel/pallas_call | solution.py:323
  74.7 4.0 %all-to-all-start.1 = ((f32[32,8,128]{2,1,0:T(8,128)}), f32[32,8,128]{2,1,0:T(8,128)S(1)}, u32[]{:S(2)}, u32[]{:S(2)}) async-start(f32[32,8,128]{2,1,0:T(8,128)} %get-tuple-element.38), calls=%async_computation.1 | async-start | bytes 262144 | tf_op jit(solution)/shard_map/all_to_all | solution.py:366
  78.7 4.3 %combine.1.h = bf16[15,512,128]{2,1,0:T(8,128)(2,1)} custom-call(s32[4]{0:T(128)} %order.9, bf16[512,512]{1,0:T(8,128)(2,1)} %get-tuple-element.35.lown, bf16[4,512,128]{2,1,0:T(8,128)(2,1)} %get-tuple-element.36.lpiv, bf16[4,128,128]{2,1,0:T(8,128)(2,1)} %w_ref.7), custom_call_target="tpu_custom_call" | custom-call | tf_op jit(solution)/shard_map/combine/pallas_call | solution.py:358
  83.0 4.3 %forward.1 = (f32[8,128]{1,0:T(8,128)}, bf16[4,128,256]{2,1,0:T(8,128)(2,1)}) custom-call(s32[4]{0:T(128)} %order.9, bf16[16,4,32,128]{3,2,1,0:T(8,128)(2,1)} %bitcast.20, bf16[16,4,32,128]{3,2,1,0:T(8,128)(2,1)} %copy-done.1, bf16[4,128,128]{2,1,0:T(8,128)(2,1)} %w_ref.7, bf16[4,128,256]{2,1,0:T(8,128)(2,1)} %bitcast.25, ...), custom_call_target="tpu_custom_call" | custom-call | tf_op jit(solution)/shard_map/forward/pallas_call | solution.py:343
  87.3 0.0 all-to-all-done.1.parts
  87.3 0.7 copy-done.2
  87.9 2.8 %solve.1 = bf16[128,8,128]{2,1,0:T(8,128)(2,1)} custom-call(s32[4]{0:T(128)} %order.9, f32[32,8,128]{2,1,0:T(8,128)} %copy-done.2, f32[8,128]{1,0:T(8,128)} %get-tuple-element.39.zt, bf16[4,512,128]{2,1,0:T(8,128)(2,1)} %get-tuple-element.36.lpiv, bf16[4,128,128]{2,1,0:T(8,128)(2,1)} %w_ref.7, bf16[15,512,128]{2,1,0:T(8,128)(2,1)} %combine.1.h), custom_call_target="tpu_custom_call" | custom-call | tf_op jit(solution)/shard_map/solve/pallas_call | solution.py:367
  90.7 8.1 %all-to-all-start.2 = ((bf16[128,8,128]{2,1,0:T(8,128)(2,1)}), bf16[128,8,128]{2,1,0:T(8,128)(2,1)S(1)}, u32[]{:S(2)}, u32[]{:S(2)}) async-start(bf16[128,8,128]{2,1,0:T(8,128)(2,1)} %solve.1), calls=%async_computation.2 | async-start | bytes 524288 | tf_op jit(solution)/shard_map/all_to_all | solution.py:375
  98.8 0.0 all-gather.3.cloned.1.call-done
  98.9 9.9 %update.1 = bf16[4,128,32,128]{3,2,1,0:T(8,128)(2,1)} custom-call(s32[4]{0:T(128)} %order.9, s32[4,32]{1,0:T(4,128)} %bitcast.28, s32[4,128]{1,0:T(4,128)} %get-tuple-element.33.mpiv, bf16[4,128,32,128]{3,2,1,0:T(8,128)(2,1)} %bitcast.17, bf16[32,512,128]{2,1,0:T(8,128)(2,1)} %bitcast.21, bf16[15,512,128]{2,1,0:T(8,128)(2,1)} %combine.1.h, ...), custom_call_target="tpu_custom_call" | custom-call | tf_op jit(solution)/shard_map/update/pallas_call | solution.py:377
  108.8 0.9 all-to-all-done.2
  109.7 0.4 copy.9
  110.1 0.9 reshape.41
  (17 shorter events, 0.0 us)
Async XLA Ops:
  7.2 91.7 %all-gather.3.cloned.1.call-start = ((), (), s32[]{:S(2)}) async-start(), calls=%async_computation.3 | async-start | bytes 4325376 | tf_op jit(solution)/shard_map/all_gather | solution.py:318
  11.6 12.3 %collective-permute-start.3 = (bf16[544,128]{1,0:T(8,128)(2,1)}, bf16[544,128]{1,0:T(8,128)(2,1)S(1)}, u32[]{:S(2)}, u32[]{:S(2)}) collective-permute-start(bf16[544,128]{1,0:T(8,128)(2,1)} %get-tuple-element.25), channel_id=1, source_target_pairs={{0,32},{4,36},{8,40},{12,44},{1,33},{5,37},{9,41},{13,45},{2,34},{... | collective-permute-start | bytes 417800 | tf_op jit(solution)/shard_map/ppermute | solution.py:302
  15.5 9.7 %collective-permute-start.4 = (bf16[544,128]{1,0:T(8,128)(2,1)}, bf16[544,128]{1,0:T(8,128)(2,1)S(1)}, u32[]{:S(2)}, u32[]{:S(2)}) collective-permute-start(bf16[544,128]{1,0:T(8,128)(2,1)} %get-tuple-element.26), channel_id=1, source_target_pairs={{0,64},{4,68},{8,72},{12,76},{1,65},{5,69},{9,73},{13,77},{2,66},{... | collective-permute-start | bytes 417800 | tf_op jit(solution)/shard_map/ppermute | solution.py:302
  17.8 8.8 %collective-permute-start.5 = (bf16[544,128]{1,0:T(8,128)(2,1)}, bf16[544,128]{1,0:T(8,128)(2,1)S(1)}, u32[]{:S(2)}, u32[]{:S(2)}) collective-permute-start(bf16[544,128]{1,0:T(8,128)(2,1)} %get-tuple-element.27), channel_id=1, source_target_pairs={{0,56},{4,60},{8,48},{12,52},{1,57},{5,61},{9,49},{13,53},{2,58},{... | collective-permute-start | bytes 417800 | tf_op jit(solution)/shard_map/ppermute | solution.py:302
  20.4 7.1 %collective-permute-start.6 = (bf16[544,128]{1,0:T(8,128)(2,1)}, bf16[544,128]{1,0:T(8,128)(2,1)S(1)}, u32[]{:S(2)}, u32[]{:S(2)}) collective-permute-start(bf16[544,128]{1,0:T(8,128)(2,1)} %get-tuple-element.28), channel_id=1, source_target_pairs={{0,88},{4,92},{8,80},{12,84},{1,89},{5,93},{9,81},{13,85},{2,90},{... | collective-permute-start | bytes 417800 | tf_op jit(solution)/shard_map/ppermute | solution.py:302
  22.6 4.9 %collective-permute-start.7 = (bf16[544,128]{1,0:T(8,128)(2,1)}, bf16[544,128]{1,0:T(8,128)(2,1)S(1)}, u32[]{:S(2)}, u32[]{:S(2)}) collective-permute-start(bf16[544,128]{1,0:T(8,128)(2,1)} %get-tuple-element.29), channel_id=1, source_target_pairs={{0,96},{4,100},{8,104},{12,108},{1,97},{5,101},{9,105},{13,109},{2... | collective-permute-start | bytes 417800 | tf_op jit(solution)/shard_map/ppermute | solution.py:302
  23.9 5.6 %copy-start.3 = (bf16[544,128]{1,0:T(8,128)(2,1)}, bf16[544,128]{1,0:T(8,128)(2,1)S(1)}, u32[]{:S(2)}) copy-start(bf16[544,128]{1,0:T(8,128)(2,1)S(1)} %collective-permute-done.3.refs_1_) | copy-start | bytes 417796
  23.9 5.6 %collective-permute-start.8 = (bf16[544,128]{1,0:T(8,128)(2,1)}, bf16[544,128]{1,0:T(8,128)(2,1)S(1)}, u32[]{:S(2)}, u32[]{:S(2)}) collective-permute-start(bf16[544,128]{1,0:T(8,128)(2,1)} %get-tuple-element.30), channel_id=1, source_target_pairs={{0,120},{4,124},{8,112},{12,116},{1,121},{5,125},{9,113},{13,117},... | collective-permute-start | bytes 417800 | tf_op jit(solution)/shard_map/ppermute | solution.py:302
  25.2 4.3 %copy-start.4 = (bf16[544,128]{1,0:T(8,128)(2,1)}, bf16[544,128]{1,0:T(8,128)(2,1)S(1)}, u32[]{:S(2)}) copy-start(bf16[544,128]{1,0:T(8,128)(2,1)S(1)} %collective-permute-done.4.refs_2_) | copy-start | bytes 417796
  25.2 4.3 %collective-permute-start.9 = (bf16[544,128]{1,0:T(8,128)(2,1)}, bf16[544,128]{1,0:T(8,128)(2,1)S(1)}, u32[]{:S(2)}, u32[]{:S(2)}) collective-permute-start(bf16[544,128]{1,0:T(8,128)(2,1)} %get-tuple-element.31), channel_id=1, source_target_pairs={{0,24},{4,28},{8,16},{12,20},{1,25},{5,29},{9,17},{13,21},{2,26},{... | collective-permute-start | bytes 417800 | tf_op jit(solution)/shard_map/ppermute | solution.py:302
  26.5 3.0 %copy-start.5 = (bf16[544,128]{1,0:T(8,128)(2,1)}, bf16[544,128]{1,0:T(8,128)(2,1)S(1)}, u32[]{:S(2)}) copy-start(bf16[544,128]{1,0:T(8,128)(2,1)S(1)} %collective-permute-done.5.refs_3_) | copy-start | bytes 417796
  27.5 2.0 %copy-start.6 = (bf16[544,128]{1,0:T(8,128)(2,1)}, bf16[544,128]{1,0:T(8,128)(2,1)S(1)}, u32[]{:S(2)}) copy-start(bf16[544,128]{1,0:T(8,128)(2,1)S(1)} %collective-permute-done.6.refs_4_) | copy-start | bytes 417796
  27.5 2.1 %copy-start.7 = (bf16[544,128]{1,0:T(8,128)(2,1)}, bf16[544,128]{1,0:T(8,128)(2,1)S(1)}, u32[]{:S(2)}) copy-start(bf16[544,128]{1,0:T(8,128)(2,1)S(1)} %collective-permute-done.7.refs_5_) | copy-start | bytes 417796
  29.5 0.7 copy-start.8
  29.5 0.7 copy-start.9
  53.1 14.9 %copy-start = (bf16[64,32,128]{2,1,0:T(8,128)(2,1)}, bf16[64,32,128]{2,1,0:T(8,128)(2,1)S(1)}, u32[]{:S(2)}) copy-start(bf16[64,32,128]{2,1,0:T(8,128)(2,1)S(1)} %all_to_all.15) | copy-start | bytes 1572868
  53.1 14.9 %collective-permute-start.10 = (bf16[16,4,32,128]{3,2,1,0:T(8,128)(2,1)S(1)}, bf16[16,4,32,128]{3,2,1,0:T(8,128)(2,1)S(1)}, u32[]{:S(2)}, u32[]{:S(2)}) collective-permute-start(bf16[16,4,32,128]{3,2,1,0:T(8,128)(2,1)S(1)} %bitcast.18), channel_id=1, source_target_pairs={{0,4},{4,0},{1,5},{5,1},{2,6},{6,2},{3,7},{7,3},{8,12},{12,8},{9,1... | collective-permute-start | bytes 1572872 | tf_op jit(solution)/shard_map/ppermute | solution.py:321
  57.3 5.3 %collective-permute-start.2 = (bf16[520,128]{1,0:T(8,128)(2,1)}, bf16[520,128]{1,0:T(8,128)(2,1)S(1)}, u32[]{:S(2)}, u32[]{:S(2)}) collective-permute-start(bf16[520,128]{1,0:T(8,128)(2,1)} %get-tuple-element.23.own), channel_id=1, source_target_pairs={{0,3},{1,0},{2,1},{3,2},{4,7},{5,4},{6,5},{7,6},{8,11},{9,8},{10,9... | collective-permute-start | bytes 399368 | tf_op jit(solution)/shard_map/ppermute | solution.py:304
  57.9 6.5 %collective-permute-start.1 = (bf16[520,128]{1,0:T(8,128)(2,1)}, bf16[520,128]{1,0:T(8,128)(2,1)S(1)}, u32[]{:S(2)}, u32[]{:S(2)}) collective-permute-start(bf16[520,128]{1,0:T(8,128)(2,1)} %get-tuple-element.23.own), channel_id=1, source_target_pairs={{0,2},{1,3},{2,0},{3,1},{4,6},{5,7},{6,4},{7,5},{8,10},{9,11},{10,... | collective-permute-start | bytes 399368 | tf_op jit(solution)/shard_map/ppermute | solution.py:304
  59.4 8.5 %collective-permute-start = (bf16[520,128]{1,0:T(8,128)(2,1)}, bf16[520,128]{1,0:T(8,128)(2,1)S(1)}, u32[]{:S(2)}, u32[]{:S(2)}) collective-permute-start(bf16[520,128]{1,0:T(8,128)(2,1)} %get-tuple-element.23.own), channel_id=1, source_target_pairs={{0,1},{1,2},{2,3},{3,0},{4,5},{5,6},{6,7},{7,4},{8,9},{9,10},{10,1... | collective-permute-start | bytes 399368 | tf_op jit(solution)/shard_map/ppermute | solution.py:304
  62.6 5.4 %copy-start.10 = (bf16[520,128]{1,0:T(8,128)(2,1)}, bf16[520,128]{1,0:T(8,128)(2,1)S(1)}, u32[]{:S(2)}) copy-start(bf16[520,128]{1,0:T(8,128)(2,1)S(1)} %collective-permute-done.2.d3) | copy-start | bytes 399364
  64.5 3.5 %copy-start.11 = (bf16[520,128]{1,0:T(8,128)(2,1)}, bf16[520,128]{1,0:T(8,128)(2,1)S(1)}, u32[]{:S(2)}) copy-start(bf16[520,128]{1,0:T(8,128)(2,1)S(1)} %collective-permute-done.1.d2) | copy-start | bytes 399364
  68.0 0.7 copy-start.12
  68.0 0.8 copy-start.1
  74.7 12.5 %all-to-all-start.1 = ((f32[32,8,128]{2,1,0:T(8,128)}), f32[32,8,128]{2,1,0:T(8,128)S(1)}, u32[]{:S(2)}, u32[]{:S(2)}) async-start(f32[32,8,128]{2,1,0:T(8,128)} %get-tuple-element.38), calls=%async_computation.1 | async-start | bytes 262144 | tf_op jit(solution)/shard_map/all_to_all | solution.py:366
  87.3 0.7 copy-start.2
  90.7 19.0 %all-to-all-start.2 = ((bf16[128,8,128]{2,1,0:T(8,128)(2,1)}), bf16[128,8,128]{2,1,0:T(8,128)(2,1)S(1)}, u32[]{:S(2)}, u32[]{:S(2)}) async-start(bf16[128,8,128]{2,1,0:T(8,128)(2,1)} %solve.1), calls=%async_computation.2 | async-start | bytes 524288 | tf_op jit(solution)/shard_map/all_to_all | solution.py:375
Sparse Core Ops, SparseCore 0:
  32.1 51.5 all-gather.2

commit v7 on v4

--- a/solution.py
+++ b/solution.py
@@ -18,7 +18,7 @@
 WIDE = ("chip", "core")
 PIECES = 8
 CPP = NC // PIECES
-SCATTER_ORDER = (2, 4, 3, 5, 6, 7, 1)
+SCATTER_ORDER = (2, 6, 4, 1, 3, 7, 5)
 SUB = 16
 EXTRA = SUB + 8 + 8
 
@@ -79,15 +79,18 @@
 
 
 def merge_kernel(*refs):
-    parts, (piece, copies) = refs[:PIECES], refs[PIECES:]
-    first = parts[0][...]
-    is_source = lax.axis_index("chip") < 2
-    total = jnp.where(is_source, first, jnp.zeros_like(first))
-    for part in parts[1:]:
-        total = total + part[...]
-    piece[...] = total[: CPP * BS]
+    parts, (piece, copies, buf) = refs[:PIECES], refs[PIECES:]
+    chip = lax.axis_index("chip")
+    place = (chip >> 2) * 2 + ((chip & 3) >> 1)
+    for p, part in zip((0, *SCATTER_ORDER), parts):
+
+        @pl.when(place == p)
+        def _():
+            pltpu.sync_copy(part, buf)
+
+    piece[...] = buf[: CPP * BS]
     for d in range(NW * 2):
-        copies[d] = total[CPP * BS :]
+        copies[d] = buf[CPP * BS :]
 
 
 def wide_index():
@@ -295,8 +298,9 @@
             jax.ShapeDtypeStruct((CPP * BS, BS), BF),
             jax.ShapeDtypeStruct((NW * 2, EXTRA, BS), BF),
         ),
-        in_specs=vmem(PIECES),
+        in_specs=[pl.BlockSpec(memory_space=pl.ANY)] * PIECES,
         out_specs=tuple(vmem(2)),
+        scratch_shapes=[pltpu.VMEM((CPP * BS + EXTRA, BS), BF)],
         name="merge",
     )(sent[0], *pieces)
 

time: 117 us -> 116 us (level)
  starting transfers between devices: 33.3 us -> 30.9 us
  blocking collectives: 21.1 us -> 23.2 us
    all_to_all x1, blocking collectives: 21.1 us -> 23.2 us  [body(): lax.all_to_all(copies, ('chip', 'narrow'), 0, 0)]
    ppermute x7, starting transfers between devices: 14.8 us -> 13.3 us  [body(): lax.ppermute(sent[p], WIDE, [(i, holder(p, i)) for i in range(NP)])]
where the time goes in v7:
time: 116 us; the launch traced here: 115 us
  Pallas kernels  31.4 us (27%)
  starting transfers between devices  30.9 us (27%)
  blocking collectives  23.2 us (20%)
  between operations  14.3 us (12%)
  waiting for transfers between devices  12.1 us (10%)
  local copies, waits for them, and re-layouts  3.38 us (3%)
    all_to_all x1, blocking collectives, body(): lax.all_to_all(copies, ('chip', 'narrow'), 0, 0)  23.2 us
    ppermute x7, starting transfers between devices, body(): lax.ppermute(sent[p], WIDE, [(i, holder(p, i)) for i in range(NP)])  13.3 us
    pallas_call x1, Pallas kernels, body(): pl.pallas_call(update_kernel, out_shape=jax.ShapeDtypeStruct((NR, BS, NC,...  9.93 us
    ppermute x3, waiting for transfers between devices, body(): lax.ppermute(mine, 'narrow', [(i, (i + d) % 4) for i in range(4)])  8.56 us
    all_to_all x1, starting transfers between devices, body(): xall = lax.all_to_all(xg, ('narrow', *WIDE), 0, 0)  8.1 us
    pallas_call x1, Pallas kernels, body(): pl.pallas_call(panel_kernel, out_shape=(jax.ShapeDtypeStruct((NR * BS, NP...  5.38 us
    pallas_call x1, Pallas kernels, body(): pl.pallas_call(combine_kernel, out_shape=jax.ShapeDtypeStruct((15, NR * B...  4.28 us
    pallas_call x1, Pallas kernels, body(): pl.pallas_call(forward_kernel, out_shape=(jax.ShapeDtypeStruct((8, BS), F...  4.25 us
  transfers between devices with their start and end apart: 14, of which 6 were waited for; matrix products, arithmetic and copies ran while one was open for 0% of the time, Pallas kernels for 23%

profile of v7, /device:TPU:1, one launch (start us, length us, event | category | flops | bytes accessed | tf_op | source)
XLA Modules:
  0.0 115.3 jit_solution(14132233649380672265)
XLA Ops:
  7.2 0.0 all-gather.3.cloned.1.call-start
  7.2 3.0 %prep.1 = (bf16[544,128]{1,0:T(8,128)(2,1)}, bf16[544,128]{1,0:T(8,128)(2,1)}, bf16[544,128]{1,0:T(8,128)(2,1)}, bf16[544,128]{1,0:T(8,128)(2,1)}, bf16[544,128]...) custom-call(bf16[4,128,32,128]{3,2,1,0:T(8,128)(2,1)} %bitcast.15, ...), custom_call_target="tpu_custom_call" | custom-call | tf_op jit(solution)/shard_map/prep/pallas_call | solution.py:280
  10.2 3.9 %collective-permute-start.3 = (bf16[544,128]{1,0:T(8,128)(2,1)}, bf16[544,128]{1,0:T(8,128)(2,1)S(1)}, u32[]{:S(2)}, u32[]{:S(2)}) collective-permute-start(bf16[544,128]{1,0:T(8,128)(2,1)} %get-tuple-element.25), channel_id=1, source_target_pairs={{0,32},{4,36},{8,40},{12,44},{1,33},{5,37},{9,41},{13,45},{2,34},{... | collective-permute-start | bytes 417800 | tf_op jit(solution)/shard_map/ppermute | solution.py:291
  14.2 1.9 %collective-permute-start.4 = (bf16[544,128]{1,0:T(8,128)(2,1)}, bf16[544,128]{1,0:T(8,128)(2,1)S(1)}, u32[]{:S(2)}, u32[]{:S(2)}) collective-permute-start(bf16[544,128]{1,0:T(8,128)(2,1)} %get-tuple-element.26), channel_id=1, source_target_pairs={{0,96},{4,100},{8,104},{12,108},{1,97},{5,101},{9,105},{13,109},{2... | collective-permute-start | bytes 417800 | tf_op jit(solution)/shard_map/ppermute | solution.py:291
  16.1 1.3 %collective-permute-start.5 = (bf16[544,128]{1,0:T(8,128)(2,1)}, bf16[544,128]{1,0:T(8,128)(2,1)S(1)}, u32[]{:S(2)}, u32[]{:S(2)}) collective-permute-start(bf16[544,128]{1,0:T(8,128)(2,1)} %get-tuple-element.27), channel_id=1, source_target_pairs={{0,64},{4,68},{8,72},{12,76},{1,65},{5,69},{9,73},{13,77},{2,66},{... | collective-permute-start | bytes 417800 | tf_op jit(solution)/shard_map/ppermute | solution.py:291
  17.4 1.3 %collective-permute-start.6 = (bf16[544,128]{1,0:T(8,128)(2,1)}, bf16[544,128]{1,0:T(8,128)(2,1)S(1)}, u32[]{:S(2)}, u32[]{:S(2)}) collective-permute-start(bf16[544,128]{1,0:T(8,128)(2,1)} %get-tuple-element.28), channel_id=1, source_target_pairs={{0,24},{4,28},{8,16},{12,20},{1,25},{5,29},{9,17},{13,21},{2,26},{... | collective-permute-start | bytes 417800 | tf_op jit(solution)/shard_map/ppermute | solution.py:291
  18.8 1.6 %collective-permute-start.7 = (bf16[544,128]{1,0:T(8,128)(2,1)}, bf16[544,128]{1,0:T(8,128)(2,1)S(1)}, u32[]{:S(2)}, u32[]{:S(2)}) collective-permute-start(bf16[544,128]{1,0:T(8,128)(2,1)} %get-tuple-element.29), channel_id=1, source_target_pairs={{0,56},{4,60},{8,48},{12,52},{1,57},{5,61},{9,49},{13,53},{2,58},{... | collective-permute-start | bytes 417800 | tf_op jit(solution)/shard_map/ppermute | solution.py:291
  20.4 0.0 collective-permute-done.3.refs_1_
  20.4 0.0 copy-start.3
  20.4 1.9 %collective-permute-start.8 = (bf16[544,128]{1,0:T(8,128)(2,1)}, bf16[544,128]{1,0:T(8,128)(2,1)S(1)}, u32[]{:S(2)}, u32[]{:S(2)}) collective-permute-start(bf16[544,128]{1,0:T(8,128)(2,1)} %get-tuple-element.30), channel_id=1, source_target_pairs={{0,120},{4,124},{8,112},{12,116},{1,121},{5,125},{9,113},{13,117},... | collective-permute-start | bytes 417800 | tf_op jit(solution)/shard_map/ppermute | solution.py:291
  22.3 0.0 collective-permute-done.4.refs_2_
  22.4 1.3 %collective-permute-start.9 = (bf16[544,128]{1,0:T(8,128)(2,1)}, bf16[544,128]{1,0:T(8,128)(2,1)S(1)}, u32[]{:S(2)}, u32[]{:S(2)}) collective-permute-start(bf16[544,128]{1,0:T(8,128)(2,1)} %get-tuple-element.31), channel_id=1, source_target_pairs={{0,88},{4,92},{8,80},{12,84},{1,89},{5,93},{9,81},{13,85},{2,90},{... | collective-permute-start | bytes 417800 | tf_op jit(solution)/shard_map/ppermute | solution.py:291
  23.7 0.0 collective-permute-done.5.refs_3_
  23.7 0.0 copy-start.5
  23.7 0.0 collective-permute-done.6.refs_4_
  23.7 0.0 copy-start.6
  23.7 0.0 collective-permute-done.7.refs_5_
  23.7 0.0 copy-start.7
  23.7 1.3 %collective-permute-done.8.refs_6_ = bf16[544,128]{1,0:T(8,128)(2,1)S(1)} collective-permute-done((bf16[544,128]{1,0:T(8,128)(2,1)}, bf16[544,128]{1,0:T(8,128)(2,1)S(1)}, u32[]{:S(2)}, u32[]{:S(2)}) %collective-permute-start.8) | collective-permute-done | bytes 139296 | tf_op jit(solution)/shard_map/ppermute | solution.py:291
  25.0 1.3 %collective-permute-done.9.refs_7_ = bf16[544,128]{1,0:T(8,128)(2,1)S(1)} collective-permute-done((bf16[544,128]{1,0:T(8,128)(2,1)}, bf16[544,128]{1,0:T(8,128)(2,1)S(1)}, u32[]{:S(2)}, u32[]{:S(2)}) %collective-permute-start.9) | collective-permute-done | bytes 139296 | tf_op jit(solution)/shard_map/ppermute | solution.py:291
  26.3 0.0 copy-done.3
  26.4 0.6 copy-done.9
  27.0 1.8 %merge.1 = (bf16[512,128]{1,0:T(8,128)(2,1)}, bf16[64,32,128]{2,1,0:T(8,128)(2,1)}) custom-call(bf16[544,128]{1,0:T(8,128)(2,1)} %get-tuple-element.24.refs_0_, bf16[544,128]{1,0:T(8,128)(2,1)} %copy-done.3, bf16[544,128]{1,0:T(8,128)(2,1)} %copy-done.4, bf16[544,128]{1,0:T(8,128)(2,1)} %copy-done.5, bf16[544,128]{1,0:T(8,128)(2,1)} %copy-done.6, ...), custom_call_target="tpu_custom_call" | custom-call | tf_op jit(solution)/shard_map/merge/pallas_call | solution.py:295
  28.7 0.0 all-gather.3.cloned.1.call-update
  28.8 23.2 %all_to_all.15 = bf16[64,32,128]{2,1,0:T(8,128)(2,1)S(1)} all-to-all(bf16[64,32,128]{2,1,0:T(8,128)(2,1)} %get-tuple-element.32), channel_id=1, replica_groups=mesh['chip'=16,'core'=2,'narrow'=4] {'chip','narrow'}, dimensions={0} | all-to-all | bytes 1048576 | tf_op jit(solution)/shard_map/all_to_all | solution.py:309
  52.0 3.2 %collective-permute-start.10 = (bf16[16,4,32,128]{3,2,1,0:T(8,128)(2,1)S(1)}, bf16[16,4,32,128]{3,2,1,0:T(8,128)(2,1)S(1)}, u32[]{:S(2)}, u32[]{:S(2)}) collective-permute-start(bf16[16,4,32,128]{3,2,1,0:T(8,128)(2,1)S(1)} %bitcast.18), channel_id=1, source_target_pairs={{0,4},{4,0},{1,5},{5,1},{2,6},{6,2},{3,7},{7,3},{8,12},{12,8},{9,1... | collective-permute-start | bytes 1572872 | tf_op jit(solution)/shard_map/ppermute | solution.py:310
  55.2 0.7 collective-permute-start.2
  55.9 1.5 %collective-permute-start.1 = (bf16[520,128]{1,0:T(8,128)(2,1)}, bf16[520,128]{1,0:T(8,128)(2,1)S(1)}, u32[]{:S(2)}, u32[]{:S(2)}) collective-permute-start(bf16[520,128]{1,0:T(8,128)(2,1)} %get-tuple-element.23.own), channel_id=1, source_target_pairs={{0,2},{1,3},{2,0},{3,1},{4,6},{5,7},{6,4},{7,5},{8,10},{9,11},{10,... | collective-permute-start | bytes 399368 | tf_op jit(solution)/shard_map/ppermute | solution.py:293
  57.4 0.0 collective-permute-start
  57.4 3.1 %collective-permute-done.2.d3 = bf16[520,128]{1,0:T(8,128)(2,1)S(1)} collective-permute-done((bf16[520,128]{1,0:T(8,128)(2,1)}, bf16[520,128]{1,0:T(8,128)(2,1)S(1)}, u32[]{:S(2)}, u32[]{:S(2)}) %collective-permute-start.2) | collective-permute-done | bytes 133152 | tf_op jit(solution)/shard_map/ppermute | solution.py:293
  60.6 1.9 %collective-permute-done.1.d2 = bf16[520,128]{1,0:T(8,128)(2,1)S(1)} collective-permute-done((bf16[520,128]{1,0:T(8,128)(2,1)}, bf16[520,128]{1,0:T(8,128)(2,1)S(1)}, u32[]{:S(2)}, u32[]{:S(2)}) %collective-permute-start.1) | collective-permute-done | bytes 133152 | tf_op jit(solution)/shard_map/ppermute | solution.py:293
  62.5 3.5 %collective-permute-done.d1 = bf16[520,128]{1,0:T(8,128)(2,1)S(1)} collective-permute-done((bf16[520,128]{1,0:T(8,128)(2,1)}, bf16[520,128]{1,0:T(8,128)(2,1)S(1)}, u32[]{:S(2)}, u32[]{:S(2)}) %collective-permute-start) | collective-permute-done | bytes 133152 | tf_op jit(solution)/shard_map/ppermute | solution.py:293
  66.0 0.0 collective-permute-done.10.far
  66.0 0.6 copy-done.12
  66.6 0.2 copy-done.1
  66.8 5.4 %panel.1 = (bf16[512,512]{1,0:T(8,128)(2,1)}, bf16[4,512,128]{2,1,0:T(8,128)(2,1)}, f32[32,8,128]{2,1,0:T(8,128)}, bf16[512,128]{1,0:T(8,128)(2,1)}, s32[4,128]{1,0:T(4,128)}) custom-call(s32[4]{0:T(128)} %order.9, bf16[520,128]{1,0:T(8,128)(2,1)} %get-tuple-element.23.own, bf16[520,128]{1,0:T(8,128)(2,1)} %copy-done.12, bf16[520,128]{1,0:T(8,128)(2,1)} %copy-done.11, ...), custom_call_target="tpu_custom_call" | custom-call | tf_op jit(solution)/shard_map/panel/pallas_call | solution.py:312
  72.2 4.0 %all-to-all-start.1 = ((f32[32,8,128]{2,1,0:T(8,128)}), f32[32,8,128]{2,1,0:T(8,128)S(1)}, u32[]{:S(2)}, u32[]{:S(2)}) async-start(f32[32,8,128]{2,1,0:T(8,128)} %get-tuple-element.38), calls=%async_computation.1 | async-start | bytes 262144 | tf_op jit(solution)/shard_map/all_to_all | solution.py:355
  76.2 4.3 %combine.1.h = bf16[15,512,128]{2,1,0:T(8,128)(2,1)} custom-call(s32[4]{0:T(128)} %order.9, bf16[512,512]{1,0:T(8,128)(2,1)} %get-tuple-element.35.lown, bf16[4,512,128]{2,1,0:T(8,128)(2,1)} %get-tuple-element.36.lpiv, bf16[4,128,128]{2,1,0:T(8,128)(2,1)} %w_ref.7), custom_call_target="tpu_custom_call" | custom-call | tf_op jit(solution)/shard_map/combine/pallas_call | solution.py:347
  80.5 4.3 %forward.1 = (f32[8,128]{1,0:T(8,128)}, bf16[4,128,256]{2,1,0:T(8,128)(2,1)}) custom-call(s32[4]{0:T(128)} %order.9, bf16[16,4,32,128]{3,2,1,0:T(8,128)(2,1)} %bitcast.20, bf16[16,4,32,128]{3,2,1,0:T(8,128)(2,1)} %copy-done.1, bf16[4,128,128]{2,1,0:T(8,128)(2,1)} %w_ref.7, bf16[4,128,256]{2,1,0:T(8,128)(2,1)} %bitcast.25, ...), custom_call_target="tpu_custom_call" | custom-call | tf_op jit(solution)/shard_map/forward/pallas_call | solution.py:332
  84.7 0.0 all-to-all-done.1.parts
  84.8 0.7 copy-done.2
  85.4 2.8 %solve.1 = bf16[128,8,128]{2,1,0:T(8,128)(2,1)} custom-call(s32[4]{0:T(128)} %order.9, f32[32,8,128]{2,1,0:T(8,128)} %copy-done.2, f32[8,128]{1,0:T(8,128)} %get-tuple-element.39.zt, bf16[4,512,128]{2,1,0:T(8,128)(2,1)} %get-tuple-element.36.lpiv, bf16[4,128,128]{2,1,0:T(8,128)(2,1)} %w_ref.7, bf16[15,512,128]{2,1,0:T(8,128)(2,1)} %combine.1.h), custom_call_target="tpu_custom_call" | custom-call | tf_op jit(solution)/shard_map/solve/pallas_call | solution.py:356
  88.2 8.1 %all-to-all-start.2 = ((bf16[128,8,128]{2,1,0:T(8,128)(2,1)}), bf16[128,8,128]{2,1,0:T(8,128)(2,1)S(1)}, u32[]{:S(2)}, u32[]{:S(2)}) async-start(bf16[128,8,128]{2,1,0:T(8,128)(2,1)} %solve.1), calls=%async_computation.2 | async-start | bytes 524288 | tf_op jit(solution)/shard_map/all_to_all | solution.py:364
  96.3 0.0 all-gather.3.cloned.1.call-done
  96.3 9.9 %update.1 = bf16[4,128,32,128]{3,2,1,0:T(8,128)(2,1)} custom-call(s32[4]{0:T(128)} %order.9, s32[4,32]{1,0:T(4,128)} %bitcast.28, s32[4,128]{1,0:T(4,128)} %get-tuple-element.33.mpiv, bf16[4,128,32,128]{3,2,1,0:T(8,128)(2,1)} %bitcast.17, bf16[32,512,128]{2,1,0:T(8,128)(2,1)} %bitcast.21, bf16[15,512,128]{2,1,0:T(8,128)(2,1)} %combine.1.h, ...), custom_call_target="tpu_custom_call" | custom-call | tf_op jit(solution)/shard_map/update/pallas_call | solution.py:366
  106.3 0.9 all-to-all-done.2
  107.2 0.4 copy.9
  107.6 0.9 reshape.41
  (17 shorter events, 0.0 us)
Async XLA Ops:
  7.2 89.2 %all-gather.3.cloned.1.call-start = ((), (), s32[]{:S(2)}) async-start(), calls=%async_computation.3 | async-start | bytes 4325376 | tf_op jit(solution)/shard_map/all_gather | solution.py:307
  10.2 10.1 %collective-permute-start.3 = (bf16[544,128]{1,0:T(8,128)(2,1)}, bf16[544,128]{1,0:T(8,128)(2,1)S(1)}, u32[]{:S(2)}, u32[]{:S(2)}) collective-permute-start(bf16[544,128]{1,0:T(8,128)(2,1)} %get-tuple-element.25), channel_id=1, source_target_pairs={{0,32},{4,36},{8,40},{12,44},{1,33},{5,37},{9,41},{13,45},{2,34},{... | collective-permute-start | bytes 417800 | tf_op jit(solution)/shard_map/ppermute | solution.py:291
  14.2 8.2 %collective-permute-start.4 = (bf16[544,128]{1,0:T(8,128)(2,1)}, bf16[544,128]{1,0:T(8,128)(2,1)S(1)}, u32[]{:S(2)}, u32[]{:S(2)}) collective-permute-start(bf16[544,128]{1,0:T(8,128)(2,1)} %get-tuple-element.26), channel_id=1, source_target_pairs={{0,96},{4,100},{8,104},{12,108},{1,97},{5,101},{9,105},{13,109},{2... | collective-permute-start | bytes 417800 | tf_op jit(solution)/shard_map/ppermute | solution.py:291
  16.1 7.5 %collective-permute-start.5 = (bf16[544,128]{1,0:T(8,128)(2,1)}, bf16[544,128]{1,0:T(8,128)(2,1)S(1)}, u32[]{:S(2)}, u32[]{:S(2)}) collective-permute-start(bf16[544,128]{1,0:T(8,128)(2,1)} %get-tuple-element.27), channel_id=1, source_target_pairs={{0,64},{4,68},{8,72},{12,76},{1,65},{5,69},{9,73},{13,77},{2,66},{... | collective-permute-start | bytes 417800 | tf_op jit(solution)/shard_map/ppermute | solution.py:291
  17.4 6.3 %collective-permute-start.6 = (bf16[544,128]{1,0:T(8,128)(2,1)}, bf16[544,128]{1,0:T(8,128)(2,1)S(1)}, u32[]{:S(2)}, u32[]{:S(2)}) collective-permute-start(bf16[544,128]{1,0:T(8,128)(2,1)} %get-tuple-element.28), channel_id=1, source_target_pairs={{0,24},{4,28},{8,16},{12,20},{1,25},{5,29},{9,17},{13,21},{2,26},{... | collective-permute-start | bytes 417800 | tf_op jit(solution)/shard_map/ppermute | solution.py:291
  18.8 4.9 %collective-permute-start.7 = (bf16[544,128]{1,0:T(8,128)(2,1)}, bf16[544,128]{1,0:T(8,128)(2,1)S(1)}, u32[]{:S(2)}, u32[]{:S(2)}) collective-permute-start(bf16[544,128]{1,0:T(8,128)(2,1)} %get-tuple-element.29), channel_id=1, source_target_pairs={{0,56},{4,60},{8,48},{12,52},{1,57},{5,61},{9,49},{13,53},{2,58},{... | collective-permute-start | bytes 417800 | tf_op jit(solution)/shard_map/ppermute | solution.py:291
  20.4 6.0 %copy-start.3 = (bf16[544,128]{1,0:T(8,128)(2,1)}, bf16[544,128]{1,0:T(8,128)(2,1)S(1)}, u32[]{:S(2)}) copy-start(bf16[544,128]{1,0:T(8,128)(2,1)S(1)} %collective-permute-done.3.refs_1_) | copy-start | bytes 417796
  20.4 4.6 %collective-permute-start.8 = (bf16[544,128]{1,0:T(8,128)(2,1)}, bf16[544,128]{1,0:T(8,128)(2,1)S(1)}, u32[]{:S(2)}, u32[]{:S(2)}) collective-permute-start(bf16[544,128]{1,0:T(8,128)(2,1)} %get-tuple-element.30), channel_id=1, source_target_pairs={{0,120},{4,124},{8,112},{12,116},{1,121},{5,125},{9,113},{13,117},... | collective-permute-start | bytes 417800 | tf_op jit(solution)/shard_map/ppermute | solution.py:291
  22.3 4.0 %copy-start.4 = (bf16[544,128]{1,0:T(8,128)(2,1)}, bf16[544,128]{1,0:T(8,128)(2,1)S(1)}, u32[]{:S(2)}) copy-start(bf16[544,128]{1,0:T(8,128)(2,1)S(1)} %collective-permute-done.4.refs_2_) | copy-start | bytes 417796
  22.4 4.0 %collective-permute-start.9 = (bf16[544,128]{1,0:T(8,128)(2,1)}, bf16[544,128]{1,0:T(8,128)(2,1)S(1)}, u32[]{:S(2)}, u32[]{:S(2)}) collective-permute-start(bf16[544,128]{1,0:T(8,128)(2,1)} %get-tuple-element.31), channel_id=1, source_target_pairs={{0,88},{4,92},{8,80},{12,84},{1,89},{5,93},{9,81},{13,85},{2,90},{... | collective-permute-start | bytes 417800 | tf_op jit(solution)/shard_map/ppermute | solution.py:291
  23.7 2.7 %copy-start.5 = (bf16[544,128]{1,0:T(8,128)(2,1)}, bf16[544,128]{1,0:T(8,128)(2,1)S(1)}, u32[]{:S(2)}) copy-start(bf16[544,128]{1,0:T(8,128)(2,1)S(1)} %collective-permute-done.5.refs_3_) | copy-start | bytes 417796
  23.7 2.6 %copy-start.6 = (bf16[544,128]{1,0:T(8,128)(2,1)}, bf16[544,128]{1,0:T(8,128)(2,1)S(1)}, u32[]{:S(2)}) copy-start(bf16[544,128]{1,0:T(8,128)(2,1)S(1)} %collective-permute-done.6.refs_4_) | copy-start | bytes 417796
  23.7 2.6 %copy-start.7 = (bf16[544,128]{1,0:T(8,128)(2,1)}, bf16[544,128]{1,0:T(8,128)(2,1)S(1)}, u32[]{:S(2)}) copy-start(bf16[544,128]{1,0:T(8,128)(2,1)S(1)} %collective-permute-done.7.refs_5_) | copy-start | bytes 417796
  25.0 1.4 %copy-start.8 = (bf16[544,128]{1,0:T(8,128)(2,1)}, bf16[544,128]{1,0:T(8,128)(2,1)S(1)}, u32[]{:S(2)}) copy-start(bf16[544,128]{1,0:T(8,128)(2,1)S(1)} %collective-permute-done.8.refs_6_) | copy-start | bytes 417796
  26.3 0.7 copy-start.9
  52.0 14.0 %copy-start = (bf16[64,32,128]{2,1,0:T(8,128)(2,1)}, bf16[64,32,128]{2,1,0:T(8,128)(2,1)S(1)}, u32[]{:S(2)}) copy-start(bf16[64,32,128]{2,1,0:T(8,128)(2,1)S(1)} %all_to_all.15) | copy-start | bytes 1572868
  52.0 14.0 %collective-permute-start.10 = (bf16[16,4,32,128]{3,2,1,0:T(8,128)(2,1)S(1)}, bf16[16,4,32,128]{3,2,1,0:T(8,128)(2,1)S(1)}, u32[]{:S(2)}, u32[]{:S(2)}) collective-permute-start(bf16[16,4,32,128]{3,2,1,0:T(8,128)(2,1)S(1)} %bitcast.18), channel_id=1, source_target_pairs={{0,4},{4,0},{1,5},{5,1},{2,6},{6,2},{3,7},{7,3},{8,12},{12,8},{9,1... | collective-permute-start | bytes 1572872 | tf_op jit(solution)/shard_map/ppermute | solution.py:310
  55.2 5.3 %collective-permute-start.2 = (bf16[520,128]{1,0:T(8,128)(2,1)}, bf16[520,128]{1,0:T(8,128)(2,1)S(1)}, u32[]{:S(2)}, u32[]{:S(2)}) collective-permute-start(bf16[520,128]{1,0:T(8,128)(2,1)} %get-tuple-element.23.own), channel_id=1, source_target_pairs={{0,3},{1,0},{2,1},{3,2},{4,7},{5,4},{6,5},{7,6},{8,11},{9,8},{10,9... | collective-permute-start | bytes 399368 | tf_op jit(solution)/shard_map/ppermute | solution.py:293
  55.9 6.5 %collective-permute-start.1 = (bf16[520,128]{1,0:T(8,128)(2,1)}, bf16[520,128]{1,0:T(8,128)(2,1)S(1)}, u32[]{:S(2)}, u32[]{:S(2)}) collective-permute-start(bf16[520,128]{1,0:T(8,128)(2,1)} %get-tuple-element.23.own), channel_id=1, source_target_pairs={{0,2},{1,3},{2,0},{3,1},{4,6},{5,7},{6,4},{7,5},{8,10},{9,11},{10,... | collective-permute-start | bytes 399368 | tf_op jit(solution)/shard_map/ppermute | solution.py:293
  57.4 8.6 %collective-permute-start = (bf16[520,128]{1,0:T(8,128)(2,1)}, bf16[520,128]{1,0:T(8,128)(2,1)S(1)}, u32[]{:S(2)}, u32[]{:S(2)}) collective-permute-start(bf16[520,128]{1,0:T(8,128)(2,1)} %get-tuple-element.23.own), channel_id=1, source_target_pairs={{0,1},{1,2},{2,3},{3,0},{4,5},{5,6},{6,7},{7,4},{8,9},{9,10},{10,1... | collective-permute-start | bytes 399368 | tf_op jit(solution)/shard_map/ppermute | solution.py:293
  60.6 5.4 %copy-start.10 = (bf16[520,128]{1,0:T(8,128)(2,1)}, bf16[520,128]{1,0:T(8,128)(2,1)S(1)}, u32[]{:S(2)}) copy-start(bf16[520,128]{1,0:T(8,128)(2,1)S(1)} %collective-permute-done.2.d3) | copy-start | bytes 399364
  62.5 3.5 %copy-start.11 = (bf16[520,128]{1,0:T(8,128)(2,1)}, bf16[520,128]{1,0:T(8,128)(2,1)S(1)}, u32[]{:S(2)}) copy-start(bf16[520,128]{1,0:T(8,128)(2,1)S(1)} %collective-permute-done.1.d2) | copy-start | bytes 399364
  66.0 0.7 copy-start.12
  66.0 0.8 copy-start.1
  72.2 12.5 %all-to-all-start.1 = ((f32[32,8,128]{2,1,0:T(8,128)}), f32[32,8,128]{2,1,0:T(8,128)S(1)}, u32[]{:S(2)}, u32[]{:S(2)}) async-start(f32[32,8,128]{2,1,0:T(8,128)} %get-tuple-element.38), calls=%async_computation.1 | async-start | bytes 262144 | tf_op jit(solution)/shard_map/all_to_all | solution.py:355
  84.7 0.7 copy-start.2
  88.2 19.0 %all-to-all-start.2 = ((bf16[128,8,128]{2,1,0:T(8,128)(2,1)}), bf16[128,8,128]{2,1,0:T(8,128)(2,1)S(1)}, u32[]{:S(2)}, u32[]{:S(2)}) async-start(bf16[128,8,128]{2,1,0:T(8,128)(2,1)} %solve.1), calls=%async_computation.2 | async-start | bytes 524288 | tf_op jit(solution)/shard_map/all_to_all | solution.py:364
Sparse Core Ops, SparseCore 0:
  28.9 52.6 all-gather.2

commit v8 on v7

--- a/solution.py
+++ b/solution.py
@@ -154,7 +154,10 @@
             tpart[:, s * 2 + j, :] = mine_cols[:, s * BS : (s + 1) * BS]
 
 
-def forward_kernel(order, near, far, w_ref, b_ref, lown, lpiv, zt, frhs, bs, ztall):
+PAIRS = [(t, s) for s in range(NP) for t in range(s + 1, NP)]
+
+
+def forward_kernel(order, near, far, w_ref, b_ref, lown, lpiv, zt, frhs, wl, bs, ztall):
     w, q = wide_index(), lax.axis_index("narrow")
     for r in range(NR):
         bs[r] = b_ref[r].astype(F32)
@@ -176,22 +179,25 @@
             bs[i] = (bs[i] - elim[i * BS : (i + 1) * BS]).astype(BF).astype(F32)
         for t in range(s + 1, NP):
             i = order[t]
-            elim = dot(lpiv[s, pl.ds(pl.multiple_of(i * BS, BS), BS), :], z)
+            low = lpiv[s, pl.ds(pl.multiple_of(i * BS, BS), BS), :]
+            wl[PAIRS.index((t, s))] = dot(w_ref[i], low, 0, 0).astype(BF)
+            elim = dot(low, z)
             bs[NR + i] = (bs[NR + i] - elim).astype(BF).astype(F32)
     for r in range(NR):
         frhs[r] = bs[r].astype(BF)
 
 
-def solve_kernel(order, parts, zt, lpiv, w_ref, h, out, xs):
+def solve_kernel(order, parts, zt, wl, w_ref, h, out, xs):
     total = jnp.sum(parts[...], axis=0)
+    c = {}
     for s in reversed(range(NP)):
-        k = order[s]
         acc = total[s * 2 : s * 2 + 2]
         for t in range(s + 1, NP):
-            i = order[t]
-            acc = acc + dot(xs[i].astype(BF), lpiv[s, pl.ds(pl.multiple_of(i * BS, BS), BS), :])
-        c = (zt[s * 2 : s * 2 + 2] - acc).astype(BF)
-        xs[k] = dot(c, w_ref[k], 1, 1).astype(BF).astype(F32)
+            acc = acc + dot(c[t], wl[PAIRS.index((t, s))])
+        c[s] = (zt[s * 2 : s * 2 + 2] - acc).astype(BF)
+    for s in range(NP):
+        k = order[s]
+        xs[k] = dot(c[s], w_ref[k], 1, 1).astype(BF).astype(F32)
     x = jnp.concatenate([xs[i] for i in range(NP)], axis=0).astype(BF)
     for d in range(NW * 4):
         out[d] = x
@@ -329,14 +335,15 @@
         name="panel",
     )(panel_order, mine, *others, near, far, pivot_inverse, y)
 
-    zt, frhs = pl.pallas_call(
+    zt, frhs, wl = pl.pallas_call(
         forward_kernel,
         out_shape=(
             jax.ShapeDtypeStruct((8, BS), F32),
             jax.ShapeDtypeStruct((NR, BS, NRHS), BF),
+            jax.ShapeDtypeStruct((len(PAIRS), BS, BS), BF),
         ),
         in_specs=smem(1) + vmem(6),
-        out_specs=tuple(vmem(2)),
+        out_specs=tuple(vmem(3)),
         scratch_shapes=[
             pltpu.VMEM((NR + NP, BS, NRHS), F32),
             pltpu.VMEM((NRHS, BS), F32),
@@ -360,7 +367,7 @@
         out_specs=vmem(1)[0],
         scratch_shapes=[pltpu.VMEM((NP, 2, BS), F32)],
         name="solve",
-    )(panel_order, tparts, zt, lpiv, pivot_inverse, h)
+    )(panel_order, tparts, zt, wl, pivot_inverse, h)
     xall = lax.all_to_all(xg, ("narrow", *WIDE), 0, 0)
 
     front_out = pl.pallas_call(
@@ -378,7 +385,8 @@
         name="update",
     )(panel_order, mask, mpiv, blocks, ugath.reshape(NW, CPP * BS, BS), h, delta)
     front_out, xall = lax.optimization_barrier((front_out, xall))
-    window = xall.reshape(NW * 4, NP, 2, BS).transpose(1, 3, 2, 0).reshape(NP, BS, NRHS)
+    halves = xall.reshape(NW * 4, NP, 2, BS)
+    window = jnp.concatenate([halves[:, :, j].transpose(1, 2, 0) for j in range(2)], axis=2)
     return front_out.reshape(front.shape), frhs.reshape(rhs.shape), window
 
 

time: 116 us -> 116 us (level)
  starting transfers between devices: 30.9 us -> 33.6 us
  waiting for transfers between devices: 12.1 us -> 9.92 us
    ppermute x3, waiting for transfers between devices: 8.56 us -> 6.34 us  [body(): lax.ppermute(mine, 'narrow', [(i, (i + d) % 4) for i in range(4)])]
    ppermute x3, starting transfers between devices: 2.16 us -> 3.34 us  [body(): lax.ppermute(mine, 'narrow', [(i, (i + d) % 4) for i in range(4)])]
    unnamed x26 -> x28, local copies, waits for them, and re-layouts: 2.12 us -> 2.45 us
  transfers between devices with their start and end apart: 14 -> 14, of which waited for: 6 -> 5; matrix products, arithmetic and copies ran while one was open for 0% -> 0% of each run, Pallas kernels for 23% -> 23%
where the time goes in v8:
time: 116 us
  starting transfers between devices  33.6 us (29%)
  Pallas kernels  31.2 us (27%)
  blocking collectives  23.2 us (20%)
  between operations  14.2 us (12%)
  waiting for transfers between devices  9.92 us (9%)
  local copies, waits for them, and re-layouts  2.81 us (2%)
    all_to_all x1, blocking collectives, body(): lax.all_to_all(copies, ('chip', 'narrow'), 0, 0)  23.2 us
    ppermute x7, starting transfers between devices, body(): lax.ppermute(sent[p], WIDE, [(i, holder(p, i)) for i in range(NP)])  13.3 us
    pallas_call x1, Pallas kernels, body(): pl.pallas_call(update_kernel, out_shape=jax.ShapeDtypeStruct((NR, BS, NC,...  9.93 us
    all_to_all x1, starting transfers between devices, body(): xall = lax.all_to_all(xg, ('narrow', *WIDE), 0, 0)  8.97 us
    ppermute x3, waiting for transfers between devices, body(): lax.ppermute(mine, 'narrow', [(i, (i + d) % 4) for i in range(4)])  6.34 us
    pallas_call x1, Pallas kernels, body(): pl.pallas_call(panel_kernel, out_shape=(jax.ShapeDtypeStruct((NR * BS, NP...  5.36 us
    all_to_all x1, starting transfers between devices, body(): tparts = lax.all_to_all(tpart, WIDE, 0, 0)  4.64 us
    pallas_call x1, Pallas kernels, body(): pl.pallas_call(forward_kernel, out_shape=(jax.ShapeDtypeStruct((8, BS), F...  4.39 us
  transfers between devices with their start and end apart: 14, of which 5 were waited for; matrix products, arithmetic and copies ran while one was open for 0% of the time, Pallas kernels for 23%

profile of v8, /device:TPU:1, one launch (start us, length us, event | category | flops | bytes accessed | tf_op | source)
XLA Modules:
  0.0 115.7 jit_solution(12387535189192097603)
XLA Ops:
  7.2 0.0 all-gather.3.cloned.1.call-start
  7.2 3.0 %prep.1 = (bf16[544,128]{1,0:T(8,128)(2,1)}, bf16[544,128]{1,0:T(8,128)(2,1)}, bf16[544,128]{1,0:T(8,128)(2,1)}, bf16[544,128]{1,0:T(8,128)(2,1)}, bf16[544,128]...) custom-call(bf16[4,128,32,128]{3,2,1,0:T(8,128)(2,1)} %bitcast.19, ...), custom_call_target="tpu_custom_call" | custom-call | tf_op jit(solution)/shard_map/prep/pallas_call | solution.py:286
  10.2 3.9 %collective-permute-start.3 = (bf16[544,128]{1,0:T(8,128)(2,1)}, bf16[544,128]{1,0:T(8,128)(2,1)S(1)}, u32[]{:S(2)}, u32[]{:S(2)}) collective-permute-start(bf16[544,128]{1,0:T(8,128)(2,1)} %get-tuple-element.26), channel_id=1, source_target_pairs={{0,32},{4,36},{8,40},{12,44},{1,33},{5,37},{9,41},{13,45},{2,34},{... | collective-permute-start | bytes 417800 | tf_op jit(solution)/shard_map/ppermute | solution.py:297
  14.2 1.9 %collective-permute-start.4 = (bf16[544,128]{1,0:T(8,128)(2,1)}, bf16[544,128]{1,0:T(8,128)(2,1)S(1)}, u32[]{:S(2)}, u32[]{:S(2)}) collective-permute-start(bf16[544,128]{1,0:T(8,128)(2,1)} %get-tuple-element.27), channel_id=1, source_target_pairs={{0,96},{4,100},{8,104},{12,108},{1,97},{5,101},{9,105},{13,109},{2... | collective-permute-start | bytes 417800 | tf_op jit(solution)/shard_map/ppermute | solution.py:297
  16.1 1.3 %collective-permute-start.5 = (bf16[544,128]{1,0:T(8,128)(2,1)}, bf16[544,128]{1,0:T(8,128)(2,1)S(1)}, u32[]{:S(2)}, u32[]{:S(2)}) collective-permute-start(bf16[544,128]{1,0:T(8,128)(2,1)} %get-tuple-element.28), channel_id=1, source_target_pairs={{0,64},{4,68},{8,72},{12,76},{1,65},{5,69},{9,73},{13,77},{2,66},{... | collective-permute-start | bytes 417800 | tf_op jit(solution)/shard_map/ppermute | solution.py:297
  17.4 1.3 %collective-permute-start.6 = (bf16[544,128]{1,0:T(8,128)(2,1)}, bf16[544,128]{1,0:T(8,128)(2,1)S(1)}, u32[]{:S(2)}, u32[]{:S(2)}) collective-permute-start(bf16[544,128]{1,0:T(8,128)(2,1)} %get-tuple-element.29), channel_id=1, source_target_pairs={{0,24},{4,28},{8,16},{12,20},{1,25},{5,29},{9,17},{13,21},{2,26},{... | collective-permute-start | bytes 417800 | tf_op jit(solution)/shard_map/ppermute | solution.py:297
  18.7 1.6 %collective-permute-start.7 = (bf16[544,128]{1,0:T(8,128)(2,1)}, bf16[544,128]{1,0:T(8,128)(2,1)S(1)}, u32[]{:S(2)}, u32[]{:S(2)}) collective-permute-start(bf16[544,128]{1,0:T(8,128)(2,1)} %get-tuple-element.30), channel_id=1, source_target_pairs={{0,56},{4,60},{8,48},{12,52},{1,57},{5,61},{9,49},{13,53},{2,58},{... | collective-permute-start | bytes 417800 | tf_op jit(solution)/shard_map/ppermute | solution.py:297
  20.3 0.0 collective-permute-done.3.refs_1_
  20.4 1.9 %collective-permute-start.8 = (bf16[544,128]{1,0:T(8,128)(2,1)}, bf16[544,128]{1,0:T(8,128)(2,1)S(1)}, u32[]{:S(2)}, u32[]{:S(2)}) collective-permute-start(bf16[544,128]{1,0:T(8,128)(2,1)} %get-tuple-element.31), channel_id=1, source_target_pairs={{0,120},{4,124},{8,112},{12,116},{1,121},{5,125},{9,113},{13,117},... | collective-permute-start | bytes 417800 | tf_op jit(solution)/shard_map/ppermute | solution.py:297
  22.3 0.0 collective-permute-done.4.refs_2_
  22.3 1.3 %collective-permute-start.9 = (bf16[544,128]{1,0:T(8,128)(2,1)}, bf16[544,128]{1,0:T(8,128)(2,1)S(1)}, u32[]{:S(2)}, u32[]{:S(2)}) collective-permute-start(bf16[544,128]{1,0:T(8,128)(2,1)} %get-tuple-element.32), channel_id=1, source_target_pairs={{0,88},{4,92},{8,80},{12,84},{1,89},{5,93},{9,81},{13,85},{2,90},{... | collective-permute-start | bytes 417800 | tf_op jit(solution)/shard_map/ppermute | solution.py:297
  23.6 0.0 collective-permute-done.5.refs_3_
  23.7 0.0 collective-permute-done.6.refs_4_
  23.7 0.0 copy-start.6
  23.7 0.0 collective-permute-done.7.refs_5_
  23.7 1.3 %collective-permute-done.8.refs_6_ = bf16[544,128]{1,0:T(8,128)(2,1)S(1)} collective-permute-done((bf16[544,128]{1,0:T(8,128)(2,1)}, bf16[544,128]{1,0:T(8,128)(2,1)S(1)}, u32[]{:S(2)}, u32[]{:S(2)}) %collective-permute-start.8) | collective-permute-done | bytes 139296 | tf_op jit(solution)/shard_map/ppermute | solution.py:297
  25.0 1.3 %collective-permute-done.9.refs_7_ = bf16[544,128]{1,0:T(8,128)(2,1)S(1)} collective-permute-done((bf16[544,128]{1,0:T(8,128)(2,1)}, bf16[544,128]{1,0:T(8,128)(2,1)S(1)}, u32[]{:S(2)}, u32[]{:S(2)}) %collective-permute-start.9) | collective-permute-done | bytes 139296 | tf_op jit(solution)/shard_map/ppermute | solution.py:297
  26.3 0.6 copy-done.9
  27.0 1.8 %merge.1 = (bf16[512,128]{1,0:T(8,128)(2,1)}, bf16[64,32,128]{2,1,0:T(8,128)(2,1)}) custom-call(bf16[544,128]{1,0:T(8,128)(2,1)} %get-tuple-element.25.refs_0_, bf16[544,128]{1,0:T(8,128)(2,1)} %copy-done.3, bf16[544,128]{1,0:T(8,128)(2,1)} %copy-done.4, bf16[544,128]{1,0:T(8,128)(2,1)} %copy-done.5, bf16[544,128]{1,0:T(8,128)(2,1)} %copy-done.6, ...), custom_call_target="tpu_custom_call" | custom-call | tf_op jit(solution)/shard_map/merge/pallas_call | solution.py:301
  28.7 0.0 all-gather.3.cloned.1.call-update
  28.8 23.2 %all_to_all.15 = bf16[64,32,128]{2,1,0:T(8,128)(2,1)S(1)} all-to-all(bf16[64,32,128]{2,1,0:T(8,128)(2,1)} %get-tuple-element.33), channel_id=1, replica_groups=mesh['chip'=16,'core'=2,'narrow'=4] {'chip','narrow'}, dimensions={0} | all-to-all | bytes 1048576 | tf_op jit(solution)/shard_map/all_to_all | solution.py:315
  52.0 3.2 %collective-permute-start.10 = (bf16[16,4,32,128]{3,2,1,0:T(8,128)(2,1)S(1)}, bf16[16,4,32,128]{3,2,1,0:T(8,128)(2,1)S(1)}, u32[]{:S(2)}, u32[]{:S(2)}) collective-permute-start(bf16[16,4,32,128]{3,2,1,0:T(8,128)(2,1)S(1)} %bitcast.22), channel_id=1, source_target_pairs={{0,4},{4,0},{1,5},{5,1},{2,6},{6,2},{3,7},{7,3},{8,12},{12,8},{9,1... | collective-permute-start | bytes 1572872 | tf_op jit(solution)/shard_map/ppermute | solution.py:316
  55.2 0.4 collective-permute-start
  55.6 1.5 %collective-permute-start.1 = (bf16[520,128]{1,0:T(8,128)(2,1)}, bf16[520,128]{1,0:T(8,128)(2,1)S(1)}, u32[]{:S(2)}, u32[]{:S(2)}) collective-permute-start(bf16[520,128]{1,0:T(8,128)(2,1)} %get-tuple-element.24.own), channel_id=1, source_target_pairs={{0,2},{1,3},{2,0},{3,1},{4,6},{5,7},{6,4},{7,5},{8,10},{9,11},{10,... | collective-permute-start | bytes 399368 | tf_op jit(solution)/shard_map/ppermute | solution.py:299
  57.1 1.5 %collective-permute-start.2 = (bf16[520,128]{1,0:T(8,128)(2,1)}, bf16[520,128]{1,0:T(8,128)(2,1)S(1)}, u32[]{:S(2)}, u32[]{:S(2)}) collective-permute-start(bf16[520,128]{1,0:T(8,128)(2,1)} %get-tuple-element.24.own), channel_id=1, source_target_pairs={{0,3},{1,0},{2,1},{3,2},{4,7},{5,4},{6,5},{7,6},{8,11},{9,8},{10,9... | collective-permute-start | bytes 399368 | tf_op jit(solution)/shard_map/ppermute | solution.py:299
  58.6 6.0 %collective-permute-done.d1 = bf16[520,128]{1,0:T(8,128)(2,1)S(1)} collective-permute-done((bf16[520,128]{1,0:T(8,128)(2,1)}, bf16[520,128]{1,0:T(8,128)(2,1)S(1)}, u32[]{:S(2)}, u32[]{:S(2)}) %collective-permute-start) | collective-permute-done | bytes 133152 | tf_op jit(solution)/shard_map/ppermute | solution.py:299
  64.6 0.0 collective-permute-done.1.d2
  64.6 0.3 collective-permute-done.2.d3
  64.9 0.0 collective-permute-done.10.far
  64.9 0.3 copy-done.10
  65.3 0.0 copy-done.11
  65.3 0.3 copy-done.12
  65.6 0.2 copy-done.1
  65.8 5.4 %panel.1 = (bf16[512,512]{1,0:T(8,128)(2,1)}, bf16[4,512,128]{2,1,0:T(8,128)(2,1)}, f32[32,8,128]{2,1,0:T(8,128)}, bf16[512,128]{1,0:T(8,128)(2,1)}, s32[4,128]{1,0:T(4,128)}) custom-call(s32[4]{0:T(128)} %order.9, bf16[520,128]{1,0:T(8,128)(2,1)} %get-tuple-element.24.own, bf16[520,128]{1,0:T(8,128)(2,1)} %copy-done.10, bf16[520,128]{1,0:T(8,128)(2,1)} %copy-done.11, ...), custom_call_target="tpu_custom_call" | custom-call | tf_op jit(solution)/shard_map/panel/pallas_call | solution.py:318
  71.1 4.6 %all-to-all-start.1 = ((f32[32,8,128]{2,1,0:T(8,128)}), f32[32,8,128]{2,1,0:T(8,128)S(1)}, u32[]{:S(2)}, u32[]{:S(2)}) async-start(f32[32,8,128]{2,1,0:T(8,128)} %get-tuple-element.39), calls=%async_computation.1 | async-start | bytes 262144 | tf_op jit(solution)/shard_map/all_to_all | solution.py:362
  75.8 4.3 %combine.1.h = bf16[15,512,128]{2,1,0:T(8,128)(2,1)} custom-call(s32[4]{0:T(128)} %order.9, bf16[512,512]{1,0:T(8,128)(2,1)} %get-tuple-element.36.lown, bf16[4,512,128]{2,1,0:T(8,128)(2,1)} %get-tuple-element.37.lpiv, bf16[4,128,128]{2,1,0:T(8,128)(2,1)} %w_ref.7), custom_call_target="tpu_custom_call" | custom-call | tf_op jit(solution)/shard_map/combine/pallas_call | solution.py:354
  80.1 4.4 %forward.1 = (f32[8,128]{1,0:T(8,128)}, bf16[4,128,256]{2,1,0:T(8,128)(2,1)}, bf16[6,128,128]{2,1,0:T(8,128)(2,1)}) custom-call(s32[4]{0:T(128)} %order.9, bf16[16,4,32,128]{3,2,1,0:T(8,128)(2,1)} %bitcast.24, bf16[16,4,32,128]{3,2,1,0:T(8,128)(2,1)} %copy-done.1, bf16[4,128,128]{2,1,0:T(8,128)(2,1)} %w_ref.7, bf16[4,128,256]{2,1,0:T(8,128)(2,1)} %bitcast.29, ...), custom_call_target="tpu_custom_call" | custom-call | tf_op jit(solution)/shard_map/forward/pallas_call | solution.py:338
  84.5 0.0 all-to-all-done.1.parts
  84.5 0.7 copy-done.2
  85.2 2.4 %solve.1 = bf16[128,8,128]{2,1,0:T(8,128)(2,1)} custom-call(s32[4]{0:T(128)} %order.9, f32[32,8,128]{2,1,0:T(8,128)} %copy-done.2, f32[8,128]{1,0:T(8,128)} %get-tuple-element.40.zt, bf16[6,128,128]{2,1,0:T(8,128)(2,1)} %get-tuple-element.41.wl, bf16[4,128,128]{2,1,0:T(8,128)(2,1)} %w_ref.7, bf16[15,512,128]{2,1,0:T(8,128)(2,1)} %combine.1.h), custom_call_target="tpu_custom_call" | custom-call | tf_op jit(solution)/shard_map/solve/pallas_call | solution.py:363
  87.6 9.0 %all-to-all-start.2 = ((bf16[128,8,128]{2,1,0:T(8,128)(2,1)}), bf16[128,8,128]{2,1,0:T(8,128)(2,1)S(1)}, u32[]{:S(2)}, u32[]{:S(2)}) async-start(bf16[128,8,128]{2,1,0:T(8,128)(2,1)} %solve.1), calls=%async_computation.2 | async-start | bytes 524288 | tf_op jit(solution)/shard_map/all_to_all | solution.py:371
  96.5 0.0 all-gather.3.cloned.1.call-done
  96.6 9.9 %update.1 = bf16[4,128,32,128]{3,2,1,0:T(8,128)(2,1)} custom-call(s32[4]{0:T(128)} %order.9, s32[4,32]{1,0:T(4,128)} %bitcast.34, s32[4,128]{1,0:T(4,128)} %get-tuple-element.34.mpiv, bf16[4,128,32,128]{3,2,1,0:T(8,128)(2,1)} %bitcast.21, bf16[32,512,128]{2,1,0:T(8,128)(2,1)} %bitcast.25, bf16[15,512,128]{2,1,0:T(8,128)(2,1)} %combine.1.h, ...), custom_call_target="tpu_custom_call" | custom-call | tf_op jit(solution)/shard_map/update/pallas_call | solution.py:373
  106.5 0.9 all-to-all-done.2
  107.4 0.4 fusion
  107.8 0.2 copy.13
  108.0 0.2 copy.14
  108.1 0.7 pad_maximum_fusion
  (19 shorter events, 0.0 us)
Async XLA Ops:
  7.2 89.4 %all-gather.3.cloned.1.call-start = ((), (), s32[]{:S(2)}) async-start(), calls=%async_computation.3 | async-start | bytes 4325376 | tf_op jit(solution)/shard_map/all_gather | solution.py:313
  10.2 10.1 %collective-permute-start.3 = (bf16[544,128]{1,0:T(8,128)(2,1)}, bf16[544,128]{1,0:T(8,128)(2,1)S(1)}, u32[]{:S(2)}, u32[]{:S(2)}) collective-permute-start(bf16[544,128]{1,0:T(8,128)(2,1)} %get-tuple-element.26), channel_id=1, source_target_pairs={{0,32},{4,36},{8,40},{12,44},{1,33},{5,37},{9,41},{13,45},{2,34},{... | collective-permute-start | bytes 417800 | tf_op jit(solution)/shard_map/ppermute | solution.py:297
  14.2 8.2 %collective-permute-start.4 = (bf16[544,128]{1,0:T(8,128)(2,1)}, bf16[544,128]{1,0:T(8,128)(2,1)S(1)}, u32[]{:S(2)}, u32[]{:S(2)}) collective-permute-start(bf16[544,128]{1,0:T(8,128)(2,1)} %get-tuple-element.27), channel_id=1, source_target_pairs={{0,96},{4,100},{8,104},{12,108},{1,97},{5,101},{9,105},{13,109},{2... | collective-permute-start | bytes 417800 | tf_op jit(solution)/shard_map/ppermute | solution.py:297
  16.1 7.5 %collective-permute-start.5 = (bf16[544,128]{1,0:T(8,128)(2,1)}, bf16[544,128]{1,0:T(8,128)(2,1)S(1)}, u32[]{:S(2)}, u32[]{:S(2)}) collective-permute-start(bf16[544,128]{1,0:T(8,128)(2,1)} %get-tuple-element.28), channel_id=1, source_target_pairs={{0,64},{4,68},{8,72},{12,76},{1,65},{5,69},{9,73},{13,77},{2,66},{... | collective-permute-start | bytes 417800 | tf_op jit(solution)/shard_map/ppermute | solution.py:297
  17.4 6.3 %collective-permute-start.6 = (bf16[544,128]{1,0:T(8,128)(2,1)}, bf16[544,128]{1,0:T(8,128)(2,1)S(1)}, u32[]{:S(2)}, u32[]{:S(2)}) collective-permute-start(bf16[544,128]{1,0:T(8,128)(2,1)} %get-tuple-element.29), channel_id=1, source_target_pairs={{0,24},{4,28},{8,16},{12,20},{1,25},{5,29},{9,17},{13,21},{2,26},{... | collective-permute-start | bytes 417800 | tf_op jit(solution)/shard_map/ppermute | solution.py:297
  18.7 4.9 %collective-permute-start.7 = (bf16[544,128]{1,0:T(8,128)(2,1)}, bf16[544,128]{1,0:T(8,128)(2,1)S(1)}, u32[]{:S(2)}, u32[]{:S(2)}) collective-permute-start(bf16[544,128]{1,0:T(8,128)(2,1)} %get-tuple-element.30), channel_id=1, source_target_pairs={{0,56},{4,60},{8,48},{12,52},{1,57},{5,61},{9,49},{13,53},{2,58},{... | collective-permute-start | bytes 417800 | tf_op jit(solution)/shard_map/ppermute | solution.py:297
  20.4 6.0 %copy-start.3 = (bf16[544,128]{1,0:T(8,128)(2,1)}, bf16[544,128]{1,0:T(8,128)(2,1)S(1)}, u32[]{:S(2)}) copy-start(bf16[544,128]{1,0:T(8,128)(2,1)S(1)} %collective-permute-done.3.refs_1_) | copy-start | bytes 417796
  20.4 4.6 %collective-permute-start.8 = (bf16[544,128]{1,0:T(8,128)(2,1)}, bf16[544,128]{1,0:T(8,128)(2,1)S(1)}, u32[]{:S(2)}, u32[]{:S(2)}) collective-permute-start(bf16[544,128]{1,0:T(8,128)(2,1)} %get-tuple-element.31), channel_id=1, source_target_pairs={{0,120},{4,124},{8,112},{12,116},{1,121},{5,125},{9,113},{13,117},... | collective-permute-start | bytes 417800 | tf_op jit(solution)/shard_map/ppermute | solution.py:297
  22.3 4.0 %copy-start.4 = (bf16[544,128]{1,0:T(8,128)(2,1)}, bf16[544,128]{1,0:T(8,128)(2,1)S(1)}, u32[]{:S(2)}) copy-start(bf16[544,128]{1,0:T(8,128)(2,1)S(1)} %collective-permute-done.4.refs_2_) | copy-start | bytes 417796
  22.3 4.0 %collective-permute-start.9 = (bf16[544,128]{1,0:T(8,128)(2,1)}, bf16[544,128]{1,0:T(8,128)(2,1)S(1)}, u32[]{:S(2)}, u32[]{:S(2)}) collective-permute-start(bf16[544,128]{1,0:T(8,128)(2,1)} %get-tuple-element.32), channel_id=1, source_target_pairs={{0,88},{4,92},{8,80},{12,84},{1,89},{5,93},{9,81},{13,85},{2,90},{... | collective-permute-start | bytes 417800 | tf_op jit(solution)/shard_map/ppermute | solution.py:297
  23.7 2.7 %copy-start.5 = (bf16[544,128]{1,0:T(8,128)(2,1)}, bf16[544,128]{1,0:T(8,128)(2,1)S(1)}, u32[]{:S(2)}) copy-start(bf16[544,128]{1,0:T(8,128)(2,1)S(1)} %collective-permute-done.5.refs_3_) | copy-start | bytes 417796
  23.7 2.6 %copy-start.6 = (bf16[544,128]{1,0:T(8,128)(2,1)}, bf16[544,128]{1,0:T(8,128)(2,1)S(1)}, u32[]{:S(2)}) copy-start(bf16[544,128]{1,0:T(8,128)(2,1)S(1)} %collective-permute-done.6.refs_4_) | copy-start | bytes 417796
  23.7 2.6 %copy-start.7 = (bf16[544,128]{1,0:T(8,128)(2,1)}, bf16[544,128]{1,0:T(8,128)(2,1)S(1)}, u32[]{:S(2)}) copy-start(bf16[544,128]{1,0:T(8,128)(2,1)S(1)} %collective-permute-done.7.refs_5_) | copy-start | bytes 417796
  25.0 1.4 %copy-start.8 = (bf16[544,128]{1,0:T(8,128)(2,1)}, bf16[544,128]{1,0:T(8,128)(2,1)S(1)}, u32[]{:S(2)}) copy-start(bf16[544,128]{1,0:T(8,128)(2,1)S(1)} %collective-permute-done.8.refs_6_) | copy-start | bytes 417796
  26.3 0.7 copy-start.9
  52.0 12.9 %copy-start = (bf16[64,32,128]{2,1,0:T(8,128)(2,1)}, bf16[64,32,128]{2,1,0:T(8,128)(2,1)S(1)}, u32[]{:S(2)}) copy-start(bf16[64,32,128]{2,1,0:T(8,128)(2,1)S(1)} %all_to_all.15) | copy-start | bytes 1572868
  52.0 12.9 %collective-permute-start.10 = (bf16[16,4,32,128]{3,2,1,0:T(8,128)(2,1)S(1)}, bf16[16,4,32,128]{3,2,1,0:T(8,128)(2,1)S(1)}, u32[]{:S(2)}, u32[]{:S(2)}) collective-permute-start(bf16[16,4,32,128]{3,2,1,0:T(8,128)(2,1)S(1)} %bitcast.22), channel_id=1, source_target_pairs={{0,4},{4,0},{1,5},{5,1},{2,6},{6,2},{3,7},{7,3},{8,12},{12,8},{9,1... | collective-permute-start | bytes 1572872 | tf_op jit(solution)/shard_map/ppermute | solution.py:316
  55.2 9.4 %collective-permute-start = (bf16[520,128]{1,0:T(8,128)(2,1)}, bf16[520,128]{1,0:T(8,128)(2,1)S(1)}, u32[]{:S(2)}, u32[]{:S(2)}) collective-permute-start(bf16[520,128]{1,0:T(8,128)(2,1)} %get-tuple-element.24.own), channel_id=1, source_target_pairs={{0,1},{1,2},{2,3},{3,0},{4,5},{5,6},{6,7},{7,4},{8,9},{9,10},{10,1... | collective-permute-start | bytes 399368 | tf_op jit(solution)/shard_map/ppermute | solution.py:299
  55.6 9.0 %collective-permute-start.1 = (bf16[520,128]{1,0:T(8,128)(2,1)}, bf16[520,128]{1,0:T(8,128)(2,1)S(1)}, u32[]{:S(2)}, u32[]{:S(2)}) collective-permute-start(bf16[520,128]{1,0:T(8,128)(2,1)} %get-tuple-element.24.own), channel_id=1, source_target_pairs={{0,2},{1,3},{2,0},{3,1},{4,6},{5,7},{6,4},{7,5},{8,10},{9,11},{10,... | collective-permute-start | bytes 399368 | tf_op jit(solution)/shard_map/ppermute | solution.py:299
  57.1 7.8 %collective-permute-start.2 = (bf16[520,128]{1,0:T(8,128)(2,1)}, bf16[520,128]{1,0:T(8,128)(2,1)S(1)}, u32[]{:S(2)}, u32[]{:S(2)}) collective-permute-start(bf16[520,128]{1,0:T(8,128)(2,1)} %get-tuple-element.24.own), channel_id=1, source_target_pairs={{0,3},{1,0},{2,1},{3,2},{4,7},{5,4},{6,5},{7,6},{8,11},{9,8},{10,9... | collective-permute-start | bytes 399368 | tf_op jit(solution)/shard_map/ppermute | solution.py:299
  64.6 0.7 copy-start.10
  64.6 0.7 copy-start.11
  64.9 0.7 copy-start.12
  64.9 0.8 copy-start.1
  71.1 13.4 %all-to-all-start.1 = ((f32[32,8,128]{2,1,0:T(8,128)}), f32[32,8,128]{2,1,0:T(8,128)S(1)}, u32[]{:S(2)}, u32[]{:S(2)}) async-start(f32[32,8,128]{2,1,0:T(8,128)} %get-tuple-element.39), calls=%async_computation.1 | async-start | bytes 262144 | tf_op jit(solution)/shard_map/all_to_all | solution.py:362
  84.5 0.7 copy-start.2
  87.6 19.9 %all-to-all-start.2 = ((bf16[128,8,128]{2,1,0:T(8,128)(2,1)}), bf16[128,8,128]{2,1,0:T(8,128)(2,1)S(1)}, u32[]{:S(2)}, u32[]{:S(2)}) async-start(bf16[128,8,128]{2,1,0:T(8,128)(2,1)} %solve.1), calls=%async_computation.2 | async-start | bytes 524288 | tf_op jit(solution)/shard_map/all_to_all | solution.py:371
Sparse Core Ops, SparseCore 0:
  28.9 52.8 all-gather.2
